TPU v7x, 512 devices: a whole 4x8x8 slice. The times are simulated.
512 devices in a mesh: snap: 4 (over y_lo), gx: 16 (over z, core), gy: 8 (over y_hi, x).
Axes of the slice: x: 4, y: 8 (y_hi: 2, y_lo: 4; y = y_hi * 4 + y_lo), z: 8, core: 2. Of those that a mesh axis runs over, the one named last changes fastest.
Arguments:
- displacements: float32 [64, 3, 64, 1024], P('snap', None, 'gx', 'gy')
- forces: float32 [64, 3, 64, 1024], P('snap', None, 'gx', 'gy')
- neighbours: int32 [8, 64, 1024], P(None, 'gx', 'gy'), may hold values 0 or 1
- species: int32 [64, 1024], P('gx', 'gy'), may hold values from 0 to 2
- block_of: int32 [64, 1024], P('gx', 'gy'), may hold values from 0 to 3, as said below
- precond: float32 [512, 3, 24, 24], P(('gx', 'gy')), may hold values from -0.1 to 0.8, as said below
- vectors: float32 [256, 3, 64, 1024], P('snap', None, 'gx', 'gy'), may hold values from -6 to 6
Outputs:
- constants: float32 [512, 3, 24, 3], P(('gx', 'gy'))
- chebyshev: float32 [256, 3, 64, 1024], P('snap', None, 'gx', 'gy')
Inputs may be any that keep to these rules, and one draw needn't show every extreme that they name: `block_of`: on each device's 4 x 128 atoms, every block index holds exactly 128 atoms. `precond`: each matrix has its diagonal between 0.4 and 0.8 and small off-diagonal entries.
All inputs are finite; a program needn't handle non-finite values. No bound on the sum of `neighbours` on one device may be relied on, other than what follows from the above.
Results may differ from a plain program's by a relative error of at most 0.00011.
Values sent between devices are 32-bit elements; how exact they have to be, the bound alone decides.
No kernel may reach another device: no remote copies, remote signals or barrier semaphores. Data moves between devices by JAX's collectives and lax.ppermute only.
A program may use at most 64 MiB of HBM per device.

v0:
```python
import jax
import jax.numpy as jnp
from jax import lax
from jax.sharding import PartitionSpec as P

AB = 128
NSPEC = 3


offsets = ((-1, -1), (-1, 0), (-1, 1), (0, -1), (0, 1), (1, -1), (1, 0), (1, 1))


def padded_2(cells, sides, width):
    for axis, dim in sides:
        count = lax.axis_size(axis)
        head = lax.slice_in_dim(cells, 0, width, axis=dim)
        tail = lax.slice_in_dim(cells, cells.shape[dim] - width, cells.shape[dim], axis=dim)
        cells = jnp.concatenate(
            [
                lax.ppermute(tail, axis, [(i, (i + 1) % count) for i in range(count)]),
                cells,
                lax.ppermute(head, axis, [((i + 1) % count, i) for i in range(count)]),
            ],
            axis=dim,
        )
    return cells


def apply_operator(extended, weights, rows, cols):
    center = extended[:, :, 1 : 1 + rows, 1 : 1 + cols]
    result = jnp.zeros_like(center)
    for index, (step_x, step_y) in enumerate(offsets):
        moved = extended[:, :, 1 + step_x : 1 + step_x + rows, 1 + step_y : 1 + step_y + cols]
        differ = moved - center
        result = result - jnp.sum(differ[:, :, None] * weights[index][None], axis=1)
    return result


def refine(precond, gram, rhs):
    high = lax.Precision.HIGHEST
    first = jnp.einsum("gpq,gqa->gpa", precond, rhs, precision=high)
    remain = rhs - jnp.einsum("gpq,gqa->gpa", gram, first, precision=high)
    return first + jnp.einsum("gpq,gqa->gpa", precond, remain, precision=high)


def shards(displacements, forces, neighbours, species, block_of, precond, vectors):
    high = lax.Precision.HIGHEST
    snap_dev, _, rows, cols = displacements.shape
    count = rows * cols
    width = 3 * len(offsets)
    padded = padded_2(displacements, (("gx", 2), ("gy", 3)), 1)
    mask = neighbours.astype(jnp.float32)
    parts = []
    for index, (step_x, step_y) in enumerate(offsets):
        moved = padded[:, :, 1 + step_x : 1 + step_x + rows, 1 + step_y : 1 + step_y + cols]
        parts.append((moved - displacements) * mask[index][None, None])
    feats = jnp.stack(parts, 1).reshape(snap_dev, width, count)
    loads = forces.reshape(snap_dev, 3, count)
    n_groups = precond.shape[0] * precond.shape[1]
    group = (block_of * NSPEC + species).reshape(count)
    onehot = (jnp.arange(n_groups, dtype=jnp.int32)[:, None] == group[None, :]).astype(jnp.float32)
    pair = jnp.einsum("spi,sqi->pqi", feats, feats, precision=high).reshape(width * width, count)
    cross = jnp.einsum("spi,sai->pai", feats, loads, precision=high).reshape(width * 3, count)
    gram_part = jnp.dot(pair, onehot.T, precision=high).T.reshape(n_groups, width, width)
    rhs_part = jnp.dot(cross, onehot.T, precision=high).T.reshape(n_groups, width, 3)
    scale = 1.0 / (snap_dev * lax.axis_size("snap") * AB)
    inverses = precond.reshape(n_groups, width, width)
    gram_total, rhs_total = lax.psum((gram_part, rhs_part), "snap")
    theta = refine(inverses, gram_total * scale, rhs_total * scale)
    flat_weights = jnp.dot(theta.reshape(n_groups, width * 3).T, onehot, precision=high)
    flat_weights = flat_weights.reshape(len(offsets), 9, rows, cols) * mask[:, None]
    weights = flat_weights.reshape(len(offsets), 3, 3, rows, cols)

    def with_rim(field):
        return padded_2(field, (("gx", 2), ("gy", 3)), 1)

    first_term = apply_operator(with_rim(vectors), weights, rows, cols)
    chebyshev = 2.0 * apply_operator(with_rim(first_term), weights, rows, cols) - vectors
    return (theta.reshape(precond.shape[0], precond.shape[1], width, 3), chebyshev)


def solution(mesh):
    in_specs = (
        P("snap", None, "gx", "gy"),
        P("snap", None, "gx", "gy"),
        P(None, "gx", "gy"),
        P("gx", "gy"),
        P("gx", "gy"),
        P(("gx", "gy"), None, None, None),
        P("snap", None, "gx", "gy"),
    )
    out_specs = (P(("gx", "gy"), None, None, None), P("snap", None, "gx", "gy"))
    return jax.shard_map(shards, mesh=mesh, in_specs=in_specs, out_specs=out_specs, check_vma=False)
```

profile of v0, /device:TPU:6, one launch (start us, length us, event | category | flops | bytes accessed | tf_op | source)
XLA Modules:
  0.0 137.5 jit_solution(17028435509304071992)
XLA Ops:
  0.7 1.0 fusion.66
  1.7 8.5 %collective-permute-start.1 = (f32[16,3,1,128]{3,2,1,0:T(1,128)S(1)}, f32[16,3,1,128]{3,2,1,0:T(1,128)S(1)}, u32[]{:S(2)}, u32[]{:S(2)}) collective-permute-start(f32[16,3,1,128]{3,2,1,0:T(1,128)S(1)} %get-tuple-element.59), channel_id=1, source_target_pairs={{8,0},{16,8},{24,16},{32,24},{40,32},{48,40},{56,48},{64,56},{72,6... | collective-permute-start | bytes 73736 | tf_op jit(solution)/shard_map/ppermute | solution.py:22
  10.2 1.3 fusion.63
  11.5 3.0 %collective-permute-start.5 = (f32[64,3,1,128]{3,0,2,1:T(8,128)S(1)}, f32[64,3,1,128]{3,0,2,1:T(8,128)S(1)}, u32[]{:S(2)}, u32[]{:S(2)}) collective-permute-start(f32[64,3,1,128]{3,0,2,1:T(8,128)S(1)} %copy.276), channel_id=1, source_target_pairs={{8,0},{16,8},{24,16},{32,24},{40,32},{48,40},{56,48},{64,56},{72,6... | collective-permute-start | bytes 294920 | tf_op jit(solution)/shard_map/ppermute | solution.py:22
  14.5 0.7 convert_element_type.4
  15.2 0.7 add_bitcast_fusion
  16.0 1.0 pad_maximum_fusion.8
  17.1 7.6 %collective-permute-start.2 = (f32[16,3,6,1]{3,2,1,0:T(8,128)S(1)}, f32[16,3,6,1]{3,2,1,0:T(8,128)S(1)}, u32[]{:S(2)}, u32[]{:S(2)}) collective-permute-start(f32[16,3,6,1]{3,2,1,0:T(8,128)S(1)} %get-tuple-element.57), channel_id=1, source_target_pairs={{0,1},{1,2},{2,3},{3,4},{4,5},{5,6},{6,7},{7,0},{8,9},{9,10},{10,1... | collective-permute-start | bytes 3464 | tf_op jit(solution)/shard_map/ppermute | solution.py:20
  24.7 0.4 copy.253
  25.2 1.9 %collective-permute-start.3 = (f32[16,3,6,1]{3,2,1,0:T(8,128)S(1)}, f32[16,3,6,1]{3,2,1,0:T(8,128)S(1)}, u32[]{:S(2)}, u32[]{:S(2)}) collective-permute-start(f32[16,3,6,1]{3,2,1,0:T(8,128)S(1)} %get-tuple-element.56), channel_id=1, source_target_pairs={{1,0},{2,1},{3,2},{4,3},{5,4},{6,5},{7,6},{0,7},{9,8},{10,9},{11,1... | collective-permute-start | bytes 3464 | tf_op jit(solution)/shard_map/ppermute | solution.py:22
  27.1 3.8 %collective-permute-done.2 = f32[16,3,6,1]{3,2,1,0:T(8,128)S(1)} collective-permute-done((f32[16,3,6,1]{3,2,1,0:T(8,128)S(1)}, f32[16,3,6,1]{3,2,1,0:T(8,128)S(1)}, u32[]{:S(2)}, u32[]{:S(2)}) %collective-permute-start.2) | collective-permute-done | bytes 1184 | tf_op jit(solution)/shard_map/ppermute | solution.py:20
  31.3 9.0 %collective-permute-done.3 = f32[16,3,6,1]{3,2,1,0:T(8,128)S(1)} collective-permute-done((f32[16,3,6,1]{3,2,1,0:T(8,128)S(1)}, f32[16,3,6,1]{3,2,1,0:T(8,128)S(1)}, u32[]{:S(2)}, u32[]{:S(2)}) %collective-permute-start.3) | collective-permute-done | bytes 1184 | tf_op jit(solution)/shard_map/ppermute | solution.py:22
  40.3 0.3 fusion.38
  40.6 0.3 fusion.35
  40.9 0.3 fusion.32
  41.6 0.3 fusion.21
  42.0 0.3 reshape.100
  42.4 3.9 %copy.203 = f32[16,24,512]{1,0,2:T(8,128)} copy(f32[16,24,512]{2,1,0:T(8,128)S(1)} %reshape.100) | data formatting | bytes 1572864 | tf_op jit(solution)/shard_map/reshape | solution.py:57
  46.3 16.9 %convolution_bitcast_fusion = f32[24,24,512]{0,1,2:T(8,128)} fusion(f32[16,24,512]{1,0,2:T(8,128)} %copy.203), kind=kOutput, calls=%fused_computation | convolution fusion | flops 56623104 | bytes 1966080 | tf_op jit(solution)/shard_map/spi,sqi->pqi/dot_general | solution.py:62
  63.2 4.0 %convolution_bitcast_fusion.1 = f32[24,3,512]{0,1,2:T(4,128)S(1)} fusion(f32[16,24,512]{1,0,2:T(8,128)S(1)} %copy-done.1, f32[16,3,512]{0,1,2:T(4,128)S(1)} %bitcast.92), kind=kOutput, calls=%fused_computation.9 | convolution fusion | flops 7077888 | bytes 1032192 | tf_op jit(solution)/shard_map/spi,sai->pai/dot_general | solution.py:63
  67.2 0.4 fusion
  67.6 4.7 %copy.209 = f32[24,24,512]{2,1,0:T(8,128)S(1)} copy(f32[24,24,512]{0,1,2:T(8,128)} %convolution_bitcast_fusion) | data formatting | bytes 2359296 | tf_op jit(solution)/shard_map/spi,sqi->pqi/transpose | solution.py:62
  72.2 1.5 %fusion.49 = f32[12,24,24]{2,0,1:T(8,128)S(1)} fusion(f32[24,24,512]{2,1,0:T(8,128)S(1)} %copy.209, s32[512]{0:T(512)S(1)} %add_bitcast_fusion), kind=kOutput, calls=%fused_computation.109 | convolution fusion | flops 42473472 | bytes 1209344 | tf_op jit(solution)/shard_map/dot_general | solution.py:64
  73.9 20.5 %all-reduce = (f32[12,24,3]{1,0,2:T(8,128)S(1)}, f32[12,24,24]{2,1,0:T(8,128)S(1)}) all-reduce(f32[12,24,3]{1,0,2:T(8,128)S(1)} %fusion, f32[12,24,24]{2,1,0:T(8,128)S(1)} %copy.210), channel_id=1, replica_groups=mesh['snap'=4,'gx'=16,'gy'=8] {'snap'}, use_global_device_ids=true, to_apply=%region_0.0 | all-reduce | flops 7776 | bytes 62208 | tf_op jit(solution)/shard_map/psum | solution.py:68
  94.4 0.3 fusion.55
  94.7 0.3 fusion.16
  95.1 0.3 convolution_add_fusion
  96.4 0.3 copy.216
  96.7 1.9 %collective-permute-start.6 = (f32[64,3,6,1]{0,2,3,1:T(8,128)S(1)}, f32[64,3,6,1]{0,2,3,1:T(8,128)S(1)}, u32[]{:S(2)}, u32[]{:S(2)}) collective-permute-start(f32[64,3,6,1]{0,2,3,1:T(8,128)S(1)} %copy.216), channel_id=1, source_target_pairs={{0,1},{1,2},{2,3},{3,4},{4,5},{5,6},{6,7},{7,0},{8,9},{9,10},{10,1... | collective-permute-start | bytes 13832 | tf_op jit(solution)/shard_map/ppermute | solution.py:20
  98.6 0.3 copy.227
  98.9 3.9 %collective-permute-start.7 = (f32[64,3,6,1]{0,2,3,1:T(8,128)S(1)}, f32[64,3,6,1]{0,2,3,1:T(8,128)S(1)}, u32[]{:S(2)}, u32[]{:S(2)}) collective-permute-start(f32[64,3,6,1]{0,2,3,1:T(8,128)S(1)} %copy.227), channel_id=1, source_target_pairs={{1,0},{2,1},{3,2},{4,3},{5,4},{6,5},{7,6},{0,7},{9,8},{10,9},{11,1... | collective-permute-start | bytes 13832 | tf_op jit(solution)/shard_map/ppermute | solution.py:22
  103.1 0.4 fusion.15
  104.0 6.5 %collective-permute-done.7 = f32[64,3,6,1]{0,2,3,1:T(8,128)S(1)} collective-permute-done((f32[64,3,6,1]{0,2,3,1:T(8,128)S(1)}, f32[64,3,6,1]{0,2,3,1:T(8,128)S(1)}, u32[]{:S(2)}, u32[]{:S(2)}) %collective-permute-start.7) | collective-permute-done | bytes 4640 | tf_op jit(solution)/shard_map/ppermute | solution.py:22
  110.8 1.0 fusion.9
  112.5 0.3 subtract_subtract_fusion
  112.9 0.5 collective-permute-start.8
  113.4 1.7 %collective-permute-done.9 = f32[64,3,1,128]{3,0,2,1:T(8,128)S(1)} collective-permute-done((f32[64,3,1,128]{3,0,2,1:T(8,128)S(1)}, f32[64,3,1,128]{3,0,2,1:T(8,128)S(1)}, u32[]{:S(2)}, u32[]{:S(2)}) %collective-permute-start.9) | collective-permute-done | bytes 98336 | tf_op jit(solution)/shard_map/ppermute | solution.py:22
  115.1 3.8 %collective-permute-done.8 = f32[64,3,1,128]{3,0,2,1:T(8,128)S(1)} collective-permute-done((f32[64,3,1,128]{3,0,2,1:T(8,128)S(1)}, f32[64,3,1,128]{3,0,2,1:T(8,128)S(1)}, u32[]{:S(2)}, u32[]{:S(2)}) %collective-permute-start.8) | collective-permute-done | bytes 98336 | tf_op jit(solution)/shard_map/ppermute | solution.py:20
  119.1 0.3 copy.254
  119.4 1.9 %collective-permute-start.10 = (f32[64,3,6,1]{0,2,3,1:T(8,128)S(1)}, f32[64,3,6,1]{0,2,3,1:T(8,128)S(1)}, u32[]{:S(2)}, u32[]{:S(2)}) collective-permute-start(f32[64,3,6,1]{0,2,3,1:T(8,128)S(1)} %copy.254), channel_id=1, source_target_pairs={{0,1},{1,2},{2,3},{3,4},{4,5},{5,6},{6,7},{7,0},{8,9},{9,10},{10,1... | collective-permute-start | bytes 13832 | tf_op jit(solution)/shard_map/ppermute | solution.py:20
  121.3 0.3 copy.255
  121.6 3.9 %collective-permute-start.11 = (f32[64,3,6,1]{0,2,3,1:T(8,128)S(1)}, f32[64,3,6,1]{0,2,3,1:T(8,128)S(1)}, u32[]{:S(2)}, u32[]{:S(2)}) collective-permute-start(f32[64,3,6,1]{0,2,3,1:T(8,128)S(1)} %copy.255), channel_id=1, source_target_pairs={{1,0},{2,1},{3,2},{4,3},{5,4},{6,5},{7,6},{0,7},{9,8},{10,9},{11,1... | collective-permute-start | bytes 13832 | tf_op jit(solution)/shard_map/ppermute | solution.py:22
  125.6 0.6 copy.247
  126.4 6.8 %collective-permute-done.11 = f32[64,3,6,1]{0,2,3,1:T(8,128)S(1)} collective-permute-done((f32[64,3,6,1]{0,2,3,1:T(8,128)S(1)}, f32[64,3,6,1]{0,2,3,1:T(8,128)S(1)}, u32[]{:S(2)}, u32[]{:S(2)}) %collective-permute-start.11) | collective-permute-done | bytes 4640 | tf_op jit(solution)/shard_map/ppermute | solution.py:22
  133.5 0.4 maximum_maximum_fusion
  133.9 0.4 slice_subtract_fusion.5
  136.1 0.3 multiply_subtract_fusion
  136.5 1.0 copy.248
  (97 shorter events, 6.0 us)
Async XLA Ops:
  0.6 93.7 %copy-start = (f32[4,3,24,24]{3,2,1,0:T(8,128)S(1)}, f32[4,3,24,24]{3,2,1,0:T(8,128)}, u32[]{:S(2)}) copy-start(f32[4,3,24,24]{3,2,1,0:T(8,128)} %param.12) | copy-start | bytes 82948
  0.6 24.1 %copy-start.16 = (f32[16,3,4,128]{3,2,1,0:T(4,128)S(1)}, f32[16,3,4,128]{3,2,1,0:T(4,128)}, u32[]{:S(2)}) copy-start(f32[16,3,4,128]{3,2,1,0:T(4,128)} %param.8) | copy-start | bytes 294916
  1.7 14.3 %collective-permute-start.1 = (f32[16,3,1,128]{3,2,1,0:T(1,128)S(1)}, f32[16,3,1,128]{3,2,1,0:T(1,128)S(1)}, u32[]{:S(2)}, u32[]{:S(2)}) collective-permute-start(f32[16,3,1,128]{3,2,1,0:T(1,128)S(1)} %get-tuple-element.59), channel_id=1, source_target_pairs={{8,0},{16,8},{24,16},{32,24},{40,32},{48,40},{56,48},{64,56},{72,6... | collective-permute-start | bytes 73736 | tf_op jit(solution)/shard_map/ppermute | solution.py:22
  10.2 5.8 %collective-permute-start = (f32[16,3,1,128]{3,2,1,0:T(1,128)S(1)}, f32[16,3,1,128]{3,2,1,0:T(1,128)S(1)}, u32[]{:S(2)}, u32[]{:S(2)}) collective-permute-start(f32[16,3,1,128]{3,2,1,0:T(1,128)S(1)} %get-tuple-element.58), channel_id=1, source_target_pairs={{0,8},{8,16},{16,24},{24,32},{32,40},{40,48},{48,56},{56,64},{64,7... | collective-permute-start | bytes 73736 | tf_op jit(solution)/shard_map/ppermute | solution.py:20
  11.5 84.6 %collective-permute-start.4 = (f32[64,3,1,128]{3,0,2,1:T(8,128)S(1)}, f32[64,3,1,128]{3,0,2,1:T(8,128)S(1)}, u32[]{:S(2)}, u32[]{:S(2)}) collective-permute-start(f32[64,3,1,128]{3,0,2,1:T(8,128)S(1)} %copy.275), channel_id=1, source_target_pairs={{0,8},{8,16},{16,24},{24,32},{32,40},{40,48},{48,56},{56,64},{64,7... | collective-permute-start | bytes 294920 | tf_op jit(solution)/shard_map/ppermute | solution.py:20
  11.5 84.6 %collective-permute-start.5 = (f32[64,3,1,128]{3,0,2,1:T(8,128)S(1)}, f32[64,3,1,128]{3,0,2,1:T(8,128)S(1)}, u32[]{:S(2)}, u32[]{:S(2)}) collective-permute-start(f32[64,3,1,128]{3,0,2,1:T(8,128)S(1)} %copy.276), channel_id=1, source_target_pairs={{8,0},{16,8},{24,16},{32,24},{40,32},{48,40},{56,48},{64,56},{72,6... | collective-permute-start | bytes 294920 | tf_op jit(solution)/shard_map/ppermute | solution.py:22
  15.2 15.7 %copy-start.2 = (f32[16,3,4,128]{3,2,1,0:T(4,128)S(1)}, f32[16,3,4,128]{3,2,1,0:T(4,128)}, u32[]{:S(2)}) copy-start(f32[16,3,4,128]{3,2,1,0:T(4,128)} %param.7) | copy-start | bytes 294916
  17.1 13.9 %collective-permute-start.2 = (f32[16,3,6,1]{3,2,1,0:T(8,128)S(1)}, f32[16,3,6,1]{3,2,1,0:T(8,128)S(1)}, u32[]{:S(2)}, u32[]{:S(2)}) collective-permute-start(f32[16,3,6,1]{3,2,1,0:T(8,128)S(1)} %get-tuple-element.57), channel_id=1, source_target_pairs={{0,1},{1,2},{2,3},{3,4},{4,5},{5,6},{6,7},{7,0},{8,9},{9,10},{10,1... | collective-permute-start | bytes 3464 | tf_op jit(solution)/shard_map/ppermute | solution.py:20
  25.2 15.1 %collective-permute-start.3 = (f32[16,3,6,1]{3,2,1,0:T(8,128)S(1)}, f32[16,3,6,1]{3,2,1,0:T(8,128)S(1)}, u32[]{:S(2)}, u32[]{:S(2)}) collective-permute-start(f32[16,3,6,1]{3,2,1,0:T(8,128)S(1)} %get-tuple-element.56), channel_id=1, source_target_pairs={{1,0},{2,1},{3,2},{4,3},{5,4},{6,5},{7,6},{0,7},{9,8},{10,9},{11,1... | collective-permute-start | bytes 3464 | tf_op jit(solution)/shard_map/ppermute | solution.py:22
  46.3 16.9 %copy-start.1 = (f32[16,24,512]{1,0,2:T(8,128)S(1)}, f32[16,24,512]{1,0,2:T(8,128)}, u32[]{:S(2)}) copy-start(f32[16,24,512]{1,0,2:T(8,128)} %copy.203) | copy-start | bytes 2359300
  94.4 1.7 %copy-start.3 = (f32[64,3,4,128]{3,2,1,0:T(4,128)S(1)}, f32[64,3,4,128]{3,2,1,0:T(4,128)}, u32[]{:S(2)}) copy-start(f32[64,3,4,128]{3,2,1,0:T(4,128)} %param.13) | copy-start | bytes 1179652
  95.9 15.9 %copy-start.12 = (f32[1,9,4,128]{3,2,1,0:T(4,128)}, f32[1,9,4,128]{3,2,1,0:T(4,128)S(1)}, u32[]{:S(2)}) copy-start(f32[1,9,4,128]{3,2,1,0:T(4,128)S(1)} %copy.241) | copy-start | bytes 55300
  95.9 15.9 %copy-start.4 = (f32[1,9,4,128]{3,2,1,0:T(4,128)}, f32[1,9,4,128]{3,2,1,0:T(4,128)S(1)}, u32[]{:S(2)}) copy-start(f32[1,9,4,128]{3,2,1,0:T(4,128)S(1)} %copy.236) | copy-start | bytes 55300
  95.9 7.6 %copy-start.14 = (f32[1,9,4,128]{3,2,1,0:T(4,128)}, f32[1,9,4,128]{3,2,1,0:T(4,128)S(1)}, u32[]{:S(2)}) copy-start(f32[1,9,4,128]{3,2,1,0:T(4,128)S(1)} %copy.239) | copy-start | bytes 55300
  96.0 16.0 %copy-start.10 = (f32[1,9,4,128]{3,2,1,0:T(4,128)}, f32[1,9,4,128]{3,2,1,0:T(4,128)S(1)}, u32[]{:S(2)}) copy-start(f32[1,9,4,128]{3,2,1,0:T(4,128)S(1)} %copy.234) | copy-start | bytes 55300
  96.0 16.0 %copy-start.8 = (f32[1,9,4,128]{3,2,1,0:T(4,128)}, f32[1,9,4,128]{3,2,1,0:T(4,128)S(1)}, u32[]{:S(2)}) copy-start(f32[1,9,4,128]{3,2,1,0:T(4,128)S(1)} %copy.232) | copy-start | bytes 55300
  96.0 16.2 %copy-start.6 = (f32[1,9,4,128]{3,2,1,0:T(4,128)}, f32[1,9,4,128]{3,2,1,0:T(4,128)S(1)}, u32[]{:S(2)}) copy-start(f32[1,9,4,128]{3,2,1,0:T(4,128)S(1)} %copy.230) | copy-start | bytes 55300
  96.7 7.0 %collective-permute-start.6 = (f32[64,3,6,1]{0,2,3,1:T(8,128)S(1)}, f32[64,3,6,1]{0,2,3,1:T(8,128)S(1)}, u32[]{:S(2)}, u32[]{:S(2)}) collective-permute-start(f32[64,3,6,1]{0,2,3,1:T(8,128)S(1)} %copy.216), channel_id=1, source_target_pairs={{0,1},{1,2},{2,3},{3,4},{4,5},{5,6},{6,7},{7,0},{8,9},{9,10},{10,1... | collective-permute-start | bytes 13832 | tf_op jit(solution)/shard_map/ppermute | solution.py:20
  98.9 11.6 %collective-permute-start.7 = (f32[64,3,6,1]{0,2,3,1:T(8,128)S(1)}, f32[64,3,6,1]{0,2,3,1:T(8,128)S(1)}, u32[]{:S(2)}, u32[]{:S(2)}) collective-permute-start(f32[64,3,6,1]{0,2,3,1:T(8,128)S(1)} %copy.227), channel_id=1, source_target_pairs={{1,0},{2,1},{3,2},{4,3},{5,4},{6,5},{7,6},{0,7},{9,8},{10,9},{11,1... | collective-permute-start | bytes 13832 | tf_op jit(solution)/shard_map/ppermute | solution.py:22
  112.8 2.2 %collective-permute-start.9 = (f32[64,3,1,128]{3,0,2,1:T(8,128)S(1)}, f32[64,3,1,128]{3,0,2,1:T(8,128)S(1)}, u32[]{:S(2)}, u32[]{:S(2)}) collective-permute-start(f32[64,3,1,128]{3,0,2,1:T(8,128)S(1)} %get-tuple-element.43), channel_id=1, source_target_pairs={{8,0},{16,8},{24,16},{32,24},{40,32},{48,40},{56,48},{64,56},{72,6... | collective-permute-start | bytes 294920 | tf_op jit(solution)/shard_map/ppermute | solution.py:22
  112.9 6.0 %collective-permute-start.8 = (f32[64,3,1,128]{3,0,2,1:T(8,128)S(1)}, f32[64,3,1,128]{3,0,2,1:T(8,128)S(1)}, u32[]{:S(2)}, u32[]{:S(2)}) collective-permute-start(f32[64,3,1,128]{3,0,2,1:T(8,128)S(1)} %get-tuple-element.42), channel_id=1, source_target_pairs={{0,8},{8,16},{16,24},{24,32},{32,40},{40,48},{48,56},{56,64},{64,7... | collective-permute-start | bytes 294920 | tf_op jit(solution)/shard_map/ppermute | solution.py:20
  119.4 6.8 %collective-permute-start.10 = (f32[64,3,6,1]{0,2,3,1:T(8,128)S(1)}, f32[64,3,6,1]{0,2,3,1:T(8,128)S(1)}, u32[]{:S(2)}, u32[]{:S(2)}) collective-permute-start(f32[64,3,6,1]{0,2,3,1:T(8,128)S(1)} %copy.254), channel_id=1, source_target_pairs={{0,1},{1,2},{2,3},{3,4},{4,5},{5,6},{6,7},{7,0},{8,9},{9,10},{10,1... | collective-permute-start | bytes 13832 | tf_op jit(solution)/shard_map/ppermute | solution.py:20
  121.6 11.6 %collective-permute-start.11 = (f32[64,3,6,1]{0,2,3,1:T(8,128)S(1)}, f32[64,3,6,1]{0,2,3,1:T(8,128)S(1)}, u32[]{:S(2)}, u32[]{:S(2)}) collective-permute-start(f32[64,3,6,1]{0,2,3,1:T(8,128)S(1)} %copy.255), channel_id=1, source_target_pairs={{1,0},{2,1},{3,2},{4,3},{5,4},{6,5},{7,6},{0,7},{9,8},{10,9},{11,1... | collective-permute-start | bytes 13832 | tf_op jit(solution)/shard_map/ppermute | solution.py:22
  133.9 0.7 copy-start.13
  133.9 0.8 copy-start.15
  134.4 0.7 copy-start.5
  134.6 0.7 copy-start.11
  134.8 0.7 copy-start.9
  135.1 0.7 copy-start.7
where the time goes:
time: 138 us; the launch traced here: 137 us
  starting transfers between devices  33.3 us (24%)
  waiting for transfers between devices  31.7 us (23%)
  matrix products  24.1 us (17%)
  blocking collectives  20.5 us (15%)
  local copies, waits for them, and re-layouts  17.8 us (13%)
  other arithmetic  8.86 us (6%)
    ppermute x6, waiting for transfers between devices, padded_2(): lax.ppermute(head, axis, [((i + 1) % count, i) for i in range(count)])  24 us
    ppermute x6, starting transfers between devices, padded_2(): lax.ppermute(head, axis, [((i + 1) % count, i) for i in range(count)])  21.3 us
    psum x1, blocking collectives, shards(): gram_total, rhs_total = lax.psum((gram_part, rhs_part), 'snap')  20.5 us
    dot_general x1, matrix products, shards(): jnp.einsum('spi,sqi->pqi', feats, feats, precision=high)  16.9 us
    ppermute x6, starting transfers between devices, padded_2(): lax.ppermute(tail, axis, [(i, (i + 1) % count) for i in range(count)])  12 us
    ppermute x6, waiting for transfers between devices, padded_2(): lax.ppermute(tail, axis, [(i, (i + 1) % count) for i in range(count)])  7.65 us
    transpose x1, local copies, waits for them, and re-layouts, shards(): jnp.einsum('spi,sqi->pqi', feats, feats, precision=high)  4.65 us
    reshape x2, local copies, waits for them, and re-layouts, shards(): feats = jnp.stack(parts, 1).reshape(snap_dev, width, count)  4.23 us
  transfers between devices with their start and end apart: 12, of which 6 were waited for; matrix products, arithmetic and copies ran while one was open for 31% of the time, Pallas kernels for 0%

commit v1 on v0

v1 whole, which is shorter than its diff:
```python
import functools

import jax
import jax.numpy as jnp
from jax import lax
from jax.experimental import pallas as pl
from jax.experimental.pallas import tpu as pltpu
from jax.sharding import PartitionSpec as P

AB = 128
NSPEC = 3
OFFSETS = ((-1, -1), (-1, 0), (-1, 1), (0, -1), (0, 1), (1, -1), (1, 0), (1, 1))
NG = 12
NP = 24
HIGH = lax.Precision.HIGHEST
F32 = jnp.float32


def lanes_of(shape):
    return lax.broadcasted_iota(jnp.int32, shape, 1)


def subs_of(shape):
    return lax.broadcasted_iota(jnp.int32, shape, 0)


def lane_slot(slot, k):
    return slot // 5, (slot % 5) * 18 + k


def pack_columns(even, tile_at, slots, near_ref, far_ref):
    lane = lanes_of((8, 128))
    for t in range(2):
        first = jnp.zeros((8, 128), F32)
        last = jnp.zeros((8, 128), F32)
        for slot in slots:
            for k in range(18):
                tile, at = lane_slot(slot, k)
                if tile != t:
                    continue
                here = lane == at
                values = tile_at(slot, k)
                first = jnp.where(here, pltpu.roll(values, at, 1) if at else values, first)
                last = jnp.where(here, pltpu.roll(values, (at + 1) % 128, 1), last)
        rows = pl.ds(8 * t, 8)
        near_ref[rows, :] = jnp.where(even, last, first)
        far_ref[rows, :] = jnp.where(even, first, last)


def spread_columns(even, tile_at, slots, near_ref, far_ref, shift_ref, height):
    lane = lanes_of((8, 128))
    from_left, from_right = [], []
    for t in range(2):
        near, far = near_ref[pl.ds(8 * t, 8), :], far_ref[pl.ds(8 * t, 8), :]
        from_left.append(jnp.where(even, far, near))
        from_right.append(jnp.where(even, near, far))
    for k in range(18):
        for place, slot in enumerate(slots):
            tile, at = lane_slot(slot, k)
            values = tile_at(slot, k)
            edge_left = pltpu.roll(from_left[tile], (128 - at) % 128, 1) if at else from_left[tile]
            edge_right = pltpu.roll(from_right[tile], (127 - at) % 128, 1)
            base = k * height + 8 * place
            shift_ref[pl.ds(base, 8), :] = jnp.where(lane == 0, edge_left, pltpu.roll(values, 1, 1))
            shift_ref[pl.ds(18 * height + base, 8), :] = values
            shift_ref[pl.ds(36 * height + base, 8), :] = jnp.where(lane == 127, edge_right, pltpu.roll(values, 127, 1))


def rows_kernel(par, disp, vec, core, other):
    even = par[0] == 0
    for b in range(3):
        for source, count, base in ((disp, 16, 0), (vec, 64, 48)):
            low = source[pl.ds(4 * b, count, stride=12), :]
            high = source[pl.ds(4 * b + 3, count, stride=12), :]
            at = pl.ds(base + b * count, count)
            core[at, :] = jnp.where(even, high, low)
            other[at, :] = jnp.where(even, low, high)


def natural_tile(source, count, core, other, base, even):
    def tile(place, k):
        b, x = k // 6, k % 6 - 1
        if 0 <= x < 4:
            return source[pl.ds(12 * 8 * place + 4 * b + x, 8, stride=12), :]
        at = pl.ds(base + b * count + 8 * place, 8)
        return jnp.where(even, other[at, :], core[at, :]) if x < 0 else jnp.where(even, core[at, :], other[at, :])

    return tile


def blocked_tile(source, core, other, even):
    def tile(place, k):
        b, x = k // 6, k % 6 - 1
        if 0 <= x < 4:
            return source[pl.ds((4 * b + x) * 64 + 8 * place, 8), :]
        at = pl.ds(b * 64 + 8 * place, 8)
        return jnp.where(even, other[at, :], core[at, :]) if x < 0 else jnp.where(even, core[at, :], other[at, :])

    return tile


def columns_kernel(par, disp, vec, core, other, near, far):
    even = par[0] == 0
    disp_tile = natural_tile(disp, 16, core, other, 0, even)
    vec_tile = natural_tile(vec, 64, core, other, 48, even)
    pack_columns(
        par[1] == 0,
        lambda slot, k: disp_tile(slot, k) if slot < 2 else vec_tile(slot - 2, k),
        range(10),
        near,
        far,
    )


def term_columns_kernel(par, term, core, other, near, far):
    tile = blocked_tile(term, core, other, par[0] == 0)
    pack_columns(par[1] == 0, tile, range(8), near, far)


def fold_rows(tiles, sub):
    for bit in (1, 2, 4):
        low = (sub & bit) == 0
        tiles = [
            jnp.where(low, tiles[2 * i], tiles[2 * i + 1])
            + pltpu.roll(jnp.where(low, tiles[2 * i + 1], tiles[2 * i]), bit, 0)
            for i in range(len(tiles) // 2)
        ]
    return tiles[0]


def fold_lanes(tiles, quarter):
    for bit in (1, 2):
        low = (quarter & bit) == 0
        tiles = [
            jnp.where(low, tiles[2 * i], tiles[2 * i + 1])
            + pltpu.roll(jnp.where(low, tiles[2 * i + 1], tiles[2 * i]), 32 * bit, 1)
            for i in range(len(tiles) // 2)
        ]
    return tiles[0]


PAIRS = [(q, p) for q in range(NP) for p in range(q, NP + 3)]
PAIR_AT = {pair: i for i, pair in enumerate(PAIRS)}
PAYLOAD = 168
CHUNK = 62


def gram_kernel(copies, par, disp, forces, nbr, species, block_of, core, other, near, far, out, shift, feats, sums):
    tile = natural_tile(disp, 16, core, other, 0, par[0] == 0)
    spread_columns(par[1] == 0, tile, range(2), near, far, shift, 16)
    for x in range(4):
        for o, (dx, dy) in enumerate(OFFSETS):
            mask = nbr[pl.ds(4 * o + x, 1), :].astype(F32)
            for b in range(3):
                moved = shift[pl.ds(((dy + 1) * 18 + 6 * b + x + dx + 1) * 16, 16), :]
                center = shift[pl.ds((18 + 6 * b + x + 1) * 16, 16), :]
                feats[pl.ds((3 * o + b) * 64 + x, 16, stride=4), :] = (moved - center) * mask
        for a in range(3):
            feats[pl.ds((NP + a) * 64 + x, 16, stride=4), :] = forces[pl.ds(4 * a + x, 16, stride=12), :]
    for q in range(NP):
        left = feats[pl.ds(q * 64, 64), :].reshape(8, 8, 128)
        for p in range(q, NP + 3):
            right = feats[pl.ds(p * 64, 64), :].reshape(8, 8, 128)
            sums[pl.ds(PAIR_AT[q, p] * 8, 8), :] = jnp.sum(left * right, axis=0)
    group = block_of[...] * NSPEC + species[...]
    which = subs_of((32, 128))
    members = jnp.concatenate([(which == group[x : x + 1, :]).astype(F32) for x in range(4)], axis=0)
    members = members.astype(jnp.bfloat16)
    members = jnp.concatenate([members, members], axis=1)
    sub, quarter = subs_of((8, 128)), lanes_of((8, 128)) // 32
    own = ((sub & 3) == quarter).astype(F32)
    for c in range(len(PAIRS) // CHUNK):
        at = pl.ds(c * CHUNK * 8, CHUNK * 8)
        value = sums[at, :]
        high = value.astype(jnp.bfloat16)
        low = (value - high.astype(F32)).astype(jnp.bfloat16)
        by_group = lax.dot_general(
            jnp.concatenate([high, low], axis=1), members, (((1,), (1,)), ((), ())), preferred_element_type=F32
        )
        sums[at, :] = (by_group.reshape(CHUNK, 8, 128) * own[None]).reshape(CHUNK * 8, 128)

    def entry(q, p):
        return sums[pl.ds(PAIR_AT[min(q, p), max(q, p)] * 8, 8), :]

    packed = []
    for first in range(0, 72, 4):
        packed.append(
            fold_lanes(
                [fold_rows([entry(i // 3, 8 * (i % 3) + r) for r in range(8)], sub) for i in range(first, first + 4)],
                quarter,
            )
        )
    for block in range(3):
        tiles = [fold_rows([entry(8 * block + r, NP + a) for r in range(8)], sub) for a in range(3)]
        packed.append(fold_lanes(tiles + [jnp.zeros((8, 128), F32)], quarter))
    for i, value in enumerate(packed):
        for copy in range(copies):
            out[pl.ds(copy * PAYLOAD + 8 * i, 8), :] = value


def apply_operator(shift, weights, height, emit):
    for x in range(4):
        total = [None] * 3
        for b in range(3):
            center = shift[pl.ds((18 + 6 * b + x + 1) * height, height), :]
            for o, (dx, dy) in enumerate(OFFSETS):
                moved = shift[pl.ds(((dy + 1) * 18 + 6 * b + x + dx + 1) * height, height), :]
                differ = center - moved
                for a in range(3):
                    term = differ * weights[pl.ds(72 * x + 24 * a + 3 * o + b, 1), :]
                    total[a] = term if total[a] is None else total[a] + term
        for a in range(3):
            emit(a, x, total[a])


def fit_kernel(
    copies, scale, par, sums, precond, vec, nbr, species, block_of, core, other, near, far,
    theta, weights, term, core_out, other_out, shift, gram,
):
    lane = lanes_of((8, 128))
    quarter = lane // 32

    def total(i):
        value = sums[pl.ds(8 * i, 8), :]
        for copy in range(1, copies):
            value = value + sums[pl.ds(copy * PAYLOAD + 8 * i, 8), :]
        return value * scale

    for m in range(18):
        value = total(m)
        for k in range(4):
            part = jnp.where(quarter == k, value, 0.0)
            part = part + pltpu.roll(part, 32, 1)
            gram[pl.ds(8 * (4 * m + k), 8), :] = part + pltpu.roll(part, 64, 1)
    rhs = jnp.concatenate([total(18 + i) for i in range(3)], axis=0)
    of_group = lanes_of((NP, 128)) & 31

    def solve(right):
        every = jnp.dot(precond[...], right, precision=HIGH, preferred_element_type=F32)
        result = every[0:NP]
        for g in range(1, NG):
            result = jnp.where(of_group == g, every[g * NP : (g + 1) * NP], result)
        return result

    first = solve(rhs)
    remain = rhs
    for q in range(NP):
        remain = remain - gram[pl.ds(NP * q, NP), :] * first[q : q + 1, :]
    fitted = first + solve(remain)
    theta[...] = fitted

    of_part = lanes_of((NP, 128)) // 32
    stacked = jnp.concatenate(
        [jnp.where((of_part == a) & (of_group < NG), fitted, 0.0) for a in range(3)], axis=0
    )
    group = block_of[...] * NSPEC + species[...]
    which = subs_of((128, 128)) & 31
    p_row, o_col = subs_of((NP, 8)), lanes_of((NP, 8))
    repeat = ((p_row >= 3 * o_col) & (p_row < 3 * o_col + 3)).astype(F32)
    for x in range(4):
        member = (which == group[x : x + 1, :]).astype(F32)
        by_atom = jnp.dot(stacked, member, precision=HIGH, preferred_element_type=F32)
        mask = nbr[pl.ds(x, 8, stride=4), :].astype(F32)
        mask = jnp.dot(repeat, mask, precision=HIGH, preferred_element_type=F32)
        weights[pl.ds(72 * x, 72), :] = by_atom * jnp.concatenate([mask, mask, mask], axis=0)

    even = par[0] == 0
    tile = natural_tile(vec, 64, core, other, 48, even)
    spread_columns(par[1] == 0, lambda slot, k: tile(slot - 2, k), range(2, 10), near, far, shift, 64)

    edge = {}

    def emit(a, x, value):
        term[pl.ds((4 * a + x) * 64, 64), :] = value
        if x == 0:
            core_out[pl.ds(64 * a, 64), :] = value
            other_out[pl.ds(64 * a, 64), :] = value
        if x == 3:
            at = pl.ds(64 * a, 64)
            low = core_out[at, :]
            core_out[at, :] = jnp.where(even, value, low)
            other_out[at, :] = jnp.where(even, low, value)

    apply_operator(shift, weights, 64, emit)


def last_kernel(par, term, core, other, near, far, weights, vec, out, shift):
    tile = blocked_tile(term, core, other, par[0] == 0)
    spread_columns(par[1] == 0, tile, range(8), near, far, shift, 64)

    def emit(a, x, value):
        at = pl.ds(4 * a + x, 64, stride=12)
        out[at, :] = 2.0 * value - vec[at, :]

    apply_operator(shift, weights, 64, emit)


def call(kernel, name, n_in, outs, scratch=()):
    in_vmem = pl.BlockSpec(memory_space=pltpu.VMEM)
    return pl.pallas_call(
        kernel,
        name=name,
        in_specs=[pl.BlockSpec(memory_space=pltpu.SMEM)] + [in_vmem] * n_in,
        out_specs=[in_vmem] * len(outs),
        out_shape=[jax.ShapeDtypeStruct((rows, 128), F32) for rows in outs],
        scratch_shapes=[pltpu.VMEM((rows, 128), F32) for rows in scratch],
        compiler_params=pltpu.CompilerParams(vmem_limit_bytes=40 << 20),
    )


def swap(value, axis, odd):
    n = lax.axis_size(axis)
    if odd:
        pairs = [(i, (i + 1) % n) for i in range(1, n, 2)]
        pairs += [((i + 1) % n, i) for i in range(1, n, 2)]
    else:
        pairs = [(i, i ^ 1) for i in range(n)]
    return lax.ppermute(value, axis, pairs)


def shards(displacements, forces, neighbours, species, block_of, precond, vectors):
    snap = lax.axis_size("snap")
    scale = 1.0 / (displacements.shape[0] * snap * AB)
    disp = displacements.reshape(-1, 128)
    load = forces.reshape(-1, 128)
    vec = vectors.reshape(-1, 128)
    nbr = neighbours.reshape(-1, 128)
    par = jnp.stack([lax.axis_index("gx") % 2, lax.axis_index("gy") % 2]).astype(jnp.int32)

    core, other = call(rows_kernel, "rows", 2, (240, 240))(par, disp, vec)
    core, other = swap(core, "gx", False), swap(other, "gx", True)
    near, far = call(columns_kernel, "columns", 4, (16, 16))(par, disp, vec, core, other)
    far, near = swap(far, "gy", True), swap(near, "gy", False)
    (part,) = call(
        functools.partial(gram_kernel, snap), "gram", 9, (snap * PAYLOAD,), (54 * 16, 27 * 64, len(PAIRS) * 8)
    )(par, disp, load, nbr, species, block_of, core, other, near, far)
    part = lax.all_to_all(part, "snap", 0, 0, tiled=True)
    theta, weights, term, core2, other2 = call(
        functools.partial(fit_kernel, snap, scale), "fit", 10, (NP, 288, 768, 192, 192), (54 * 64, 576)
    )(par, part, precond.reshape(NG * NP, NP), vec, nbr, species, block_of, core, other, near, far)
    core2, other2 = swap(core2, "gx", False), swap(other2, "gx", True)
    near2, far2 = call(term_columns_kernel, "term_columns", 3, (16, 16))(par, term, core2, other2)
    far2, near2 = swap(far2, "gy", True), swap(near2, "gy", False)
    (result,) = call(last_kernel, "last", 7, (768,), (54 * 64,))(par, term, core2, other2, near2, far2, weights, vec)

    constants = theta.reshape(NP, 4, 32)[:, :3, :NG].transpose(2, 0, 1)
    return (
        constants.reshape(precond.shape[0], precond.shape[1], NP, 3),
        result.reshape(vectors.shape),
    )


def solution(mesh):
    in_specs = (
        P("snap", None, "gx", "gy"),
        P("snap", None, "gx", "gy"),
        P(None, "gx", "gy"),
        P("gx", "gy"),
        P("gx", "gy"),
        P(("gx", "gy"), None, None, None),
        P("snap", None, "gx", "gy"),
    )
    out_specs = (P(("gx", "gy"), None, None, None), P("snap", None, "gx", "gy"))
    return jax.shard_map(shards, mesh=mesh, in_specs=in_specs, out_specs=out_specs, check_vma=False)
```

time: 138 us -> 79.8 us (0.58)
  matrix products: 24.1 us -> 0 us
  waiting for transfers between devices: 31.7 us -> 12.5 us
  local copies, waits for them, and re-layouts: 17.8 us -> 2.73 us
  Pallas kernels: 0 us -> 9.37 us
  other arithmetic: 8.86 us -> 0.08 us
  starting transfers between devices: 33.3 us -> 40.6 us
  blocking collectives: 20.5 us -> 13.2 us
    dot_general x8 -> x0, matrix products: 24.1 us -> none  [the longest x1 16.9 us: shards(): jnp.einsum('spi,sqi->pqi', feats, feats, precision=high)]
    psum x1 -> x0, blocking collectives: 20.5 us -> none  [shards(): gram_total, rhs_total = lax.psum((gram_part, rhs_part), 'snap')]
    ppermute x12 -> x8, waiting for transfers between devices: 31.7 us -> 12.5 us  [swap(): return lax.ppermute(value, axis, pairs)]
    all_to_all x0 -> x1, blocking collectives: none -> 13.2 us  [shards(): part = lax.all_to_all(part, 'snap', 0, 0, tiled=True)]
    pallas_call x0 -> x6, Pallas kernels: none -> 9.37 us  [the longest x1 2.43 us: shards(): call(functools.partial(fit_kernel, snap, scale), 'fit', 10, (NP, 288, 768...]
    ppermute x12 -> x8, starting transfers between devices: 33.3 us -> 40.6 us  [swap(): return lax.ppermute(value, axis, pairs)]
    transpose x1 -> x0, local copies, waits for them, and re-layouts: 4.65 us -> none  [shards(): jnp.einsum('spi,sqi->pqi', feats, feats, precision=high)]
    reshape x4 -> x1, local copies, waits for them, and re-layouts: 4.67 us -> 0.08 us  [shards(): constants = theta.reshape(NP, 4, 32)[:, :3, :NG].transpose(2, 0, 1)]
  transfers between devices with their start and end apart: 12 -> 8, of which waited for: 6 -> 4; matrix products, arithmetic and copies ran while one was open for 31% -> 1% of each run, Pallas kernels for 0% -> 0%
where the time goes in v1:
time: 79.8 us; the launch traced here: 79.3 us
  starting transfers between devices  40.6 us (51%)
  blocking collectives  13.2 us (17%)
  waiting for transfers between devices  12.5 us (16%)
  Pallas kernels  9.37 us (12%)
  local copies, waits for them, and re-layouts  2.73 us (3%)
  between operations  0.83 us (1%)
    ppermute x8, starting transfers between devices, swap(): return lax.ppermute(value, axis, pairs)  40.6 us
    all_to_all x1, blocking collectives, shards(): part = lax.all_to_all(part, 'snap', 0, 0, tiled=True)  13.2 us
    ppermute x8, waiting for transfers between devices, swap(): return lax.ppermute(value, axis, pairs)  12.5 us
    unnamed x18, local copies, waits for them, and re-layouts  2.64 us
    pallas_call x1, Pallas kernels, shards(): call(functools.partial(fit_kernel, snap, scale), 'fit', 10, (NP, 288, 768...  2.43 us
    pallas_call x1, Pallas kernels, shards(): call(last_kernel, 'last', 7, (768,), (54 * 64,))  2.31 us
    pallas_call x1, Pallas kernels, shards(): call(functools.partial(gram_kernel, snap), 'gram', 9, (snap * PAYLOAD,),...  2.17 us
  transfers between devices with their start and end apart: 8, of which 4 were waited for; matrix products, arithmetic and copies ran while one was open for 1% of the time, Pallas kernels for 0%

profile of v1, /device:TPU:6, one launch (start us, length us, event | category | flops | bytes accessed | tf_op | source)
XLA Modules:
  0.0 79.3 jit_solution(14320256572510364803)
XLA Ops:
  0.6 0.1 pad_add_fusion.par
  0.7 0.0 copy-start
  0.7 1.0 %copy-done = f32[64,3,4,128]{3,2,1,0:T(4,128)S(1)} copy-done((f32[64,3,4,128]{3,2,1,0:T(4,128)S(1)}, f32[64,3,4,128]{3,2,1,0:T(4,128)}, u32[]{:S(2)}) %copy-start) | copy-done | bytes 393240
  1.7 0.0 copy-start.2
  1.7 0.9 %copy-done.2 = f32[16,3,4,128]{3,2,1,0:T(4,128)S(1)} copy-done((f32[16,3,4,128]{3,2,1,0:T(4,128)S(1)}, f32[16,3,4,128]{3,2,1,0:T(4,128)}, u32[]{:S(2)}) %copy-start.2) | copy-done | bytes 98328
  2.6 0.6 rows.1
  3.2 1.9 %collective-permute-start = (f32[240,128]{1,0:T(8,128)S(1)}, f32[240,128]{1,0:T(8,128)S(1)}, u32[]{:S(2)}, u32[]{:S(2)}) collective-permute-start(f32[240,128]{1,0:T(8,128)S(1)} %get-tuple-element.13), channel_id=1, source_target_pairs={{0,8},{8,0},{16,24},{24,16},{32,40},{40,32},{48,56},{56,48},{64,72... | collective-permute-start | bytes 368648 | tf_op jit(solution)/shard_map/ppermute | solution.py:318
  5.1 0.0 copy-start.4
  5.1 11.2 %collective-permute-start.1 = (f32[240,128]{1,0:T(8,128)S(1)}, f32[240,128]{1,0:T(8,128)S(1)}, u32[]{:S(2)}, u32[]{:S(2)}) collective-permute-start(f32[240,128]{1,0:T(8,128)S(1)} %get-tuple-element.14), channel_id=1, source_target_pairs={{8,16},{24,32},{40,48},{56,64},{72,80},{88,96},{104,112},{120,0},{... | collective-permute-start | bytes 368648 | tf_op jit(solution)/shard_map/ppermute | solution.py:318
  16.3 0.0 collective-permute-done.core
  16.3 2.5 %collective-permute-done.1.other = f32[240,128]{1,0:T(8,128)S(1)} collective-permute-done((f32[240,128]{1,0:T(8,128)S(1)}, f32[240,128]{1,0:T(8,128)S(1)}, u32[]{:S(2)}, u32[]{:S(2)}) %collective-permute-start.1) | collective-permute-done | bytes 122912 | tf_op jit(solution)/shard_map/ppermute | solution.py:318
  18.9 0.0 copy-start.5
  18.9 1.0 %columns.1 = (f32[16,128]{1,0:T(8,128)S(1)}, f32[16,128]{1,0:T(8,128)S(1)}) custom-call(s32[2]{0:T(128)S(1)} %pad_add_fusion.par, f32[192,128]{1,0:T(8,128)S(1)} %bitcast.21, f32[768,128]{1,0:T(8,128)S(1)} %bitcast.15, f32[240,128]{1,0:T(8,128)S(1)} %collective-permute-done.core, f32[240,128]{1,0:T(8,128)S(1)} %collective-permute-done.1.other), custom_call_target="tpu_custom_call" | custom-call | tf_op jit(solution)/shard_map/columns/pallas_call | solution.py:332
  19.9 2.7 %collective-permute-start.2 = (f32[16,128]{1,0:T(8,128)S(1)}, f32[16,128]{1,0:T(8,128)S(1)}, u32[]{:S(2)}, u32[]{:S(2)}) collective-permute-start(f32[16,128]{1,0:T(8,128)S(1)} %get-tuple-element.15), channel_id=1, source_target_pairs={{0,1},{1,0},{2,3},{3,2},{4,5},{5,4},{6,7},{7,6},{8,9},{9,8},{10,11... | collective-permute-start | bytes 24584 | tf_op jit(solution)/shard_map/ppermute | solution.py:318
  22.6 0.0 copy-start.7
  22.6 0.0 copy-start.6
  22.6 8.3 %collective-permute-start.3 = (f32[16,128]{1,0:T(8,128)S(1)}, f32[16,128]{1,0:T(8,128)S(1)}, u32[]{:S(2)}, u32[]{:S(2)}) collective-permute-start(f32[16,128]{1,0:T(8,128)S(1)} %get-tuple-element.16), channel_id=1, source_target_pairs={{1,2},{3,4},{5,6},{7,0},{2,1},{4,3},{6,5},{0,7},{9,10},{11,12},{13... | collective-permute-start | bytes 24584 | tf_op jit(solution)/shard_map/ppermute | solution.py:318
  30.9 0.0 collective-permute-done.2.near
  30.9 3.2 %collective-permute-done.3.far = f32[16,128]{1,0:T(8,128)S(1)} collective-permute-done((f32[16,128]{1,0:T(8,128)S(1)}, f32[16,128]{1,0:T(8,128)S(1)}, u32[]{:S(2)}, u32[]{:S(2)}) %collective-permute-start.3) | collective-permute-done | bytes 8224 | tf_op jit(solution)/shard_map/ppermute | solution.py:318
  34.2 0.0 copy-done.4
  34.2 0.0 copy-done.5
  34.2 0.0 copy-done.7
  34.2 0.0 copy-done.6
  34.2 2.2 %gram.1 = f32[672,128]{1,0:T(8,128)S(1)} custom-call(s32[2]{0:T(128)S(1)} %pad_add_fusion.par, f32[192,128]{1,0:T(8,128)S(1)} %bitcast.22, f32[192,128]{1,0:T(8,128)S(1)} %bitcast.24, s32[32,128]{1,0:T(8,128)S(1)} %bitcast.25, s32[4,128]{1,0:T(4,128)S(1)} %copy-done.6, s32[4,128]{1,0:T(4,128)S(1)} %copy-done.7, f32[240,128]{1,0:T(8,128)S(1)} %collective-permute-done.core, ...), custom_call_target="tpu_custom_call" | custom-call | tf_op jit(solution)/shard_map/gram/pallas_call | solution.py:334
  36.4 0.0 copy-start.1
  36.4 0.0 copy-start.3
  36.4 13.2 %all_to_all.11 = f32[4,168,128]{2,1,0:T(8,128)S(1)} all-to-all(f32[4,168,128]{2,1,0:T(8,128)S(1)} %bitcast.19), channel_id=1, replica_groups=mesh['snap'=4,'gx'=16,'gy'=8] {'snap'}, dimensions={0} | all-to-all | bytes 688128 | tf_op jit(solution)/shard_map/all_to_all | solution.py:337
  49.6 0.0 copy-done.1
  49.6 0.0 copy-done.3
  49.6 2.4 %fit.1 = (f32[24,128]{1,0:T(8,128)S(1)}, f32[288,128]{1,0:T(8,128)S(1)}, f32[768,128]{1,0:T(8,128)S(1)}, f32[192,128]{1,0:T(8,128)S(1)}, f32[192,128]{1,0:T(8,128)S(1)}) custom-call(s32[2]{0:T(128)S(1)} %pad_add_fusion.par, f32[672,128]{1,0:T(8,128)S(1)} %bitcast.18, f32[288,24]{1,0:T(8,128)S(1)} %bitcast.23, f32[768,128]{1,0:T(8,128)S(1)} %bitcast.16, ...), custom_call_target="tpu_custom_call" | custom-call | tf_op jit(solution)/shard_map/fit/pallas_call | solution.py:338
  52.0 1.9 %collective-permute-start.4 = (f32[192,128]{1,0:T(8,128)S(1)}, f32[192,128]{1,0:T(8,128)S(1)}, u32[]{:S(2)}, u32[]{:S(2)}) collective-permute-start(f32[192,128]{1,0:T(8,128)S(1)} %get-tuple-element.19), channel_id=1, source_target_pairs={{0,8},{8,0},{16,24},{24,16},{32,40},{40,32},{48,56},{56,48},{64,72... | collective-permute-start | bytes 294920 | tf_op jit(solution)/shard_map/ppermute | solution.py:318
  53.9 6.4 %collective-permute-start.5 = (f32[192,128]{1,0:T(8,128)S(1)}, f32[192,128]{1,0:T(8,128)S(1)}, u32[]{:S(2)}, u32[]{:S(2)}) collective-permute-start(f32[192,128]{1,0:T(8,128)S(1)} %get-tuple-element.20), channel_id=1, source_target_pairs={{8,16},{24,32},{40,48},{56,64},{72,80},{88,96},{104,112},{120,0},{... | collective-permute-start | bytes 294920 | tf_op jit(solution)/shard_map/ppermute | solution.py:318
  60.3 0.0 collective-permute-done.4.core
  60.3 2.3 %collective-permute-done.5.other = f32[192,128]{1,0:T(8,128)S(1)} collective-permute-done((f32[192,128]{1,0:T(8,128)S(1)}, f32[192,128]{1,0:T(8,128)S(1)}, u32[]{:S(2)}, u32[]{:S(2)}) %collective-permute-start.5) | collective-permute-done | bytes 98336 | tf_op jit(solution)/shard_map/ppermute | solution.py:318
  62.6 0.9 %term_columns.1 = (f32[16,128]{1,0:T(8,128)S(1)}, f32[16,128]{1,0:T(8,128)S(1)}) custom-call(s32[2]{0:T(128)S(1)} %pad_add_fusion.par, f32[768,128]{1,0:T(8,128)S(1)} %get-tuple-element.18.term, f32[192,128]{1,0:T(8,128)S(1)} %collective-permute-done.4.core, f32[192,128]{1,0:T(8,128)S(1)} %collective-permute-done.5.other), custom_call_target="tpu_custom_call" | custom-call | tf_op jit(solution)/shard_map/term_columns/pallas_call | solution.py:342
  63.5 1.9 %collective-permute-start.6 = (f32[16,128]{1,0:T(8,128)S(1)}, f32[16,128]{1,0:T(8,128)S(1)}, u32[]{:S(2)}, u32[]{:S(2)}) collective-permute-start(f32[16,128]{1,0:T(8,128)S(1)} %get-tuple-element.21), channel_id=1, source_target_pairs={{0,1},{1,0},{2,3},{3,2},{4,5},{5,4},{6,7},{7,6},{8,9},{9,8},{10,11... | collective-permute-start | bytes 24584 | tf_op jit(solution)/shard_map/ppermute | solution.py:318
  65.4 6.3 %collective-permute-start.7 = (f32[16,128]{1,0:T(8,128)S(1)}, f32[16,128]{1,0:T(8,128)S(1)}, u32[]{:S(2)}, u32[]{:S(2)}) collective-permute-start(f32[16,128]{1,0:T(8,128)S(1)} %get-tuple-element.22), channel_id=1, source_target_pairs={{1,2},{3,4},{5,6},{7,0},{2,1},{4,3},{6,5},{0,7},{9,10},{11,12},{13... | collective-permute-start | bytes 24584 | tf_op jit(solution)/shard_map/ppermute | solution.py:318
  71.7 0.1 reshape.35
  71.8 0.1 copy.11
  71.9 0.6 copy.10
  72.5 0.0 collective-permute-done.6.near
  72.5 4.4 %collective-permute-done.7.far = f32[16,128]{1,0:T(8,128)S(1)} collective-permute-done((f32[16,128]{1,0:T(8,128)S(1)}, f32[16,128]{1,0:T(8,128)S(1)}, u32[]{:S(2)}, u32[]{:S(2)}) %collective-permute-start.7) | collective-permute-done | bytes 8224 | tf_op jit(solution)/shard_map/ppermute | solution.py:318
  77.0 2.3 %last.1 = f32[768,128]{1,0:T(8,128)} custom-call(s32[2]{0:T(128)S(1)} %pad_add_fusion.par, f32[768,128]{1,0:T(8,128)S(1)} %get-tuple-element.18.term, f32[192,128]{1,0:T(8,128)S(1)} %collective-permute-done.4.core, f32[192,128]{1,0:T(8,128)S(1)} %collective-permute-done.5.other, f32[16,128]{1,0:T(8,128)S(1)} %collective-permute-done.6.near, ...), custom_call_target="tpu_custom_call" | custom-call | tf_op jit(solution)/shard_map/last/pallas_call | solution.py:344
Async XLA Ops:
  0.7 1.0 %copy-start = (f32[64,3,4,128]{3,2,1,0:T(4,128)S(1)}, f32[64,3,4,128]{3,2,1,0:T(4,128)}, u32[]{:S(2)}) copy-start(f32[64,3,4,128]{3,2,1,0:T(4,128)} %param.13) | copy-start | bytes 1179652
  1.7 0.9 %copy-start.2 = (f32[16,3,4,128]{3,2,1,0:T(4,128)S(1)}, f32[16,3,4,128]{3,2,1,0:T(4,128)}, u32[]{:S(2)}) copy-start(f32[16,3,4,128]{3,2,1,0:T(4,128)} %param.7) | copy-start | bytes 294916
  3.2 13.1 %collective-permute-start = (f32[240,128]{1,0:T(8,128)S(1)}, f32[240,128]{1,0:T(8,128)S(1)}, u32[]{:S(2)}, u32[]{:S(2)}) collective-permute-start(f32[240,128]{1,0:T(8,128)S(1)} %get-tuple-element.13), channel_id=1, source_target_pairs={{0,8},{8,0},{16,24},{24,16},{32,40},{40,32},{48,56},{56,48},{64,72... | collective-permute-start | bytes 368648 | tf_op jit(solution)/shard_map/ppermute | solution.py:318
  5.1 29.1 %copy-start.4 = (f32[16,3,4,128]{3,2,1,0:T(4,128)S(1)}, f32[16,3,4,128]{3,2,1,0:T(4,128)}, u32[]{:S(2)}) copy-start(f32[16,3,4,128]{3,2,1,0:T(4,128)} %param.8) | copy-start | bytes 294916
  5.1 13.7 %collective-permute-start.1 = (f32[240,128]{1,0:T(8,128)S(1)}, f32[240,128]{1,0:T(8,128)S(1)}, u32[]{:S(2)}, u32[]{:S(2)}) collective-permute-start(f32[240,128]{1,0:T(8,128)S(1)} %get-tuple-element.14), channel_id=1, source_target_pairs={{8,16},{24,32},{40,48},{56,64},{72,80},{88,96},{104,112},{120,0},{... | collective-permute-start | bytes 368648 | tf_op jit(solution)/shard_map/ppermute | solution.py:318
  18.9 15.3 %copy-start.5 = (s32[8,4,128]{2,1,0:T(4,128)S(1)}, s32[8,4,128]{2,1,0:T(4,128)}, u32[]{:S(2)}) copy-start(s32[8,4,128]{2,1,0:T(4,128)} %param.9) | copy-start | bytes 49156
  19.9 11.1 %collective-permute-start.2 = (f32[16,128]{1,0:T(8,128)S(1)}, f32[16,128]{1,0:T(8,128)S(1)}, u32[]{:S(2)}, u32[]{:S(2)}) collective-permute-start(f32[16,128]{1,0:T(8,128)S(1)} %get-tuple-element.15), channel_id=1, source_target_pairs={{0,1},{1,0},{2,3},{3,2},{4,5},{5,4},{6,7},{7,6},{8,9},{9,8},{10,11... | collective-permute-start | bytes 24584 | tf_op jit(solution)/shard_map/ppermute | solution.py:318
  22.6 11.6 %copy-start.7 = (s32[4,128]{1,0:T(4,128)S(1)}, s32[4,128]{1,0:T(4,128)}, u32[]{:S(2)}) copy-start(s32[4,128]{1,0:T(4,128)} %block_of.3) | copy-start | bytes 6148
  22.6 11.6 %copy-start.6 = (s32[4,128]{1,0:T(4,128)S(1)}, s32[4,128]{1,0:T(4,128)}, u32[]{:S(2)}) copy-start(s32[4,128]{1,0:T(4,128)} %species.3) | copy-start | bytes 6148
  22.6 11.6 %collective-permute-start.3 = (f32[16,128]{1,0:T(8,128)S(1)}, f32[16,128]{1,0:T(8,128)S(1)}, u32[]{:S(2)}, u32[]{:S(2)}) collective-permute-start(f32[16,128]{1,0:T(8,128)S(1)} %get-tuple-element.16), channel_id=1, source_target_pairs={{1,2},{3,4},{5,6},{7,0},{2,1},{4,3},{6,5},{0,7},{9,10},{11,12},{13... | collective-permute-start | bytes 24584 | tf_op jit(solution)/shard_map/ppermute | solution.py:318
  36.4 13.2 %copy-start.1 = (f32[64,3,4,128]{3,2,1,0:T(4,128)S(1)}, f32[64,3,4,128]{3,2,1,0:T(4,128)}, u32[]{:S(2)}) copy-start(f32[64,3,4,128]{3,2,1,0:T(4,128)} %param.13) | copy-start | bytes 1179652
  36.4 13.2 %copy-start.3 = (f32[4,3,24,24]{3,2,1,0:T(8,128)S(1)}, f32[4,3,24,24]{3,2,1,0:T(8,128)}, u32[]{:S(2)}) copy-start(f32[4,3,24,24]{3,2,1,0:T(8,128)} %param.12) | copy-start | bytes 82948
  52.0 8.3 %collective-permute-start.4 = (f32[192,128]{1,0:T(8,128)S(1)}, f32[192,128]{1,0:T(8,128)S(1)}, u32[]{:S(2)}, u32[]{:S(2)}) collective-permute-start(f32[192,128]{1,0:T(8,128)S(1)} %get-tuple-element.19), channel_id=1, source_target_pairs={{0,8},{8,0},{16,24},{24,16},{32,40},{40,32},{48,56},{56,48},{64,72... | collective-permute-start | bytes 294920 | tf_op jit(solution)/shard_map/ppermute | solution.py:318
  53.9 8.7 %collective-permute-start.5 = (f32[192,128]{1,0:T(8,128)S(1)}, f32[192,128]{1,0:T(8,128)S(1)}, u32[]{:S(2)}, u32[]{:S(2)}) collective-permute-start(f32[192,128]{1,0:T(8,128)S(1)} %get-tuple-element.20), channel_id=1, source_target_pairs={{8,16},{24,32},{40,48},{56,64},{72,80},{88,96},{104,112},{120,0},{... | collective-permute-start | bytes 294920 | tf_op jit(solution)/shard_map/ppermute | solution.py:318
  63.5 9.0 %collective-permute-start.6 = (f32[16,128]{1,0:T(8,128)S(1)}, f32[16,128]{1,0:T(8,128)S(1)}, u32[]{:S(2)}, u32[]{:S(2)}) collective-permute-start(f32[16,128]{1,0:T(8,128)S(1)} %get-tuple-element.21), channel_id=1, source_target_pairs={{0,1},{1,0},{2,3},{3,2},{4,5},{5,4},{6,7},{7,6},{8,9},{9,8},{10,11... | collective-permute-start | bytes 24584 | tf_op jit(solution)/shard_map/ppermute | solution.py:318
  65.4 11.6 %collective-permute-start.7 = (f32[16,128]{1,0:T(8,128)S(1)}, f32[16,128]{1,0:T(8,128)S(1)}, u32[]{:S(2)}, u32[]{:S(2)}) collective-permute-start(f32[16,128]{1,0:T(8,128)S(1)} %get-tuple-element.22), channel_id=1, source_target_pairs={{1,2},{3,4},{5,6},{7,0},{2,1},{4,3},{6,5},{0,7},{9,10},{11,12},{13... | collective-permute-start | bytes 24584 | tf_op jit(solution)/shard_map/ppermute | solution.py:318

commit v2 on v1

v2 whole, which is shorter than its diff:
```python
import functools

import jax
import jax.numpy as jnp
from jax import lax
from jax.experimental import pallas as pl
from jax.experimental.pallas import tpu as pltpu
from jax.sharding import PartitionSpec as P

AB = 128
NSPEC = 3
OFFSETS = ((-1, -1), (-1, 0), (-1, 1), (0, -1), (0, 1), (1, -1), (1, 0), (1, 1))
NG = 12
NP = 24
HIGH = lax.Precision.HIGHEST
F32 = jnp.float32


def lanes_of(shape):
    return lax.broadcasted_iota(jnp.int32, shape, 1)


def subs_of(shape):
    return lax.broadcasted_iota(jnp.int32, shape, 0)


def lane_slot(slot, k):
    return slot // 3, (slot % 3) * 36 + 2 * k


def pack_columns(tile_at, slots, columns):
    pair = lanes_of((8, 128)) // 2
    packed = [jnp.zeros((8, 128), F32) for _ in range(columns.shape[0] // 8)]
    for slot in slots:
        for k in range(18):
            t, at = lane_slot(slot, k)
            packed[t] = jnp.where(pair == at // 2, pltpu.roll(tile_at(slot, k), (at + 1) % 128, 1), packed[t])
    for t, value in enumerate(packed):
        columns[pl.ds(8 * t, 8), :] = value


def spread_columns(even, tile_at, slots, near_ref, far_ref, shift_ref, height):
    lane = lanes_of((8, 128))
    edges = {}
    for t in sorted({lane_slot(slot, 0)[0] for slot in slots}):
        near, far = near_ref[pl.ds(8 * t, 8), :], far_ref[pl.ds(8 * t, 8), :]
        left, right = jnp.where(even, far, near), jnp.where(even, near, far)
        edges[t] = jnp.where((lane & 1) == 0, pltpu.roll(right, 127, 1), pltpu.roll(left, 1, 1))
    for k in range(18):
        for place, slot in enumerate(slots):
            t, at = lane_slot(slot, k)
            values = tile_at(slot, k)
            edge = pltpu.roll(edges[t], 127 - at, 1)
            base = k * height + 8 * place
            shift_ref[pl.ds(base, 8), :] = jnp.where(lane == 0, edge, pltpu.roll(values, 1, 1))
            shift_ref[pl.ds(18 * height + base, 8), :] = values
            shift_ref[pl.ds(36 * height + base, 8), :] = jnp.where(lane == 127, edge, pltpu.roll(values, 127, 1))


def rows_kernel(disp, vec, low, high, sems):
    copies = []
    for out, x in ((low, 0), (high, 3)):
        for source, at in ((disp, pl.ds(0, 48)), (vec, pl.ds(48, 192))):
            copies.append(pltpu.make_async_copy(source.at[:, x, :], out.at[at, :], sems.at[len(copies)]))
    for copy in copies:
        copy.start()
    for copy in copies:
        copy.wait()


def natural_tile(source, above, below, base):
    def tile(place, k):
        b, x = k // 6, k % 6 - 1
        if 0 <= x < 4:
            return source[pl.ds(12 * 8 * place + 4 * b + x, 8, stride=12), :]
        return (above if x < 0 else below)[pl.ds(base + 24 * place + b, 8, stride=3), :]

    return tile


def blocked_tile(source, above, below):
    def tile(place, k):
        b, x = k // 6, k % 6 - 1
        if 0 <= x < 4:
            return source[pl.ds((4 * b + x) * 64 + 8 * place, 8), :]
        return (above if x < 0 else below)[pl.ds(b * 64 + 8 * place, 8), :]

    return tile


def columns_kernel(disp, vec, above, below, columns):
    disp_tile = natural_tile(disp, above, below, 0)
    vec_tile = natural_tile(vec, above, below, 48)
    pack_columns(lambda slot, k: disp_tile(slot, k) if slot < 2 else vec_tile(slot - 2, k), range(10), columns)


def term_columns_kernel(term, above, below, columns):
    pack_columns(blocked_tile(term, above, below), range(8), columns)


def fold_rows(tiles, sub):
    for bit in (1, 2, 4):
        low = (sub & bit) == 0
        tiles = [
            jnp.where(low, tiles[2 * i], tiles[2 * i + 1])
            + pltpu.roll(jnp.where(low, tiles[2 * i + 1], tiles[2 * i]), bit, 0)
            for i in range(len(tiles) // 2)
        ]
    return tiles[0]


def fold_lanes(tiles, eighth):
    for bit in (1, 2, 4):
        low = (eighth & bit) == 0
        tiles = [
            jnp.where(low, tiles[2 * i], tiles[2 * i + 1])
            + pltpu.roll(jnp.where(low, tiles[2 * i + 1], tiles[2 * i]), 16 * bit, 1)
            for i in range(len(tiles) // 2)
        ]
    return tiles[0]


PAIRS = [(q, p) for q in range(NP) for p in range(q, NP + 3)]
PAIR_AT = {pair: i for i, pair in enumerate(PAIRS)}
BLOCKS = [(i, j) for i in range(3) for j in range(i, 3)]
PAYLOAD = 64
CHUNK = 62


def gram_kernel(copies, par, disp, forces, nbr, species, block_of, above, below, far, near, out, shift, feats, sums):
    tile = natural_tile(disp, above, below, 0)
    spread_columns(par[0] == 0, tile, range(2), near, far, shift, 16)
    for x in range(4):
        for o, (dx, dy) in enumerate(OFFSETS):
            mask = nbr[pl.ds(4 * o + x, 1), :].astype(F32)
            for b in range(3):
                moved = shift[pl.ds(((dy + 1) * 18 + 6 * b + x + dx + 1) * 16, 16), :]
                center = shift[pl.ds((18 + 6 * b + x + 1) * 16, 16), :]
                feats[pl.ds((3 * o + b) * 64 + x, 16, stride=4), :] = (moved - center) * mask
        for a in range(3):
            feats[pl.ds((NP + a) * 64 + x, 16, stride=4), :] = forces[pl.ds(4 * a + x, 16, stride=12), :]
    for q in range(NP):
        left = feats[pl.ds(q * 64, 64), :].reshape(8, 8, 128)
        for p in range(q, NP + 3):
            right = feats[pl.ds(p * 64, 64), :].reshape(8, 8, 128)
            sums[pl.ds(PAIR_AT[q, p] * 8, 8), :] = jnp.sum(left * right, axis=0)
    group = block_of[...] * NSPEC + species[...]
    which = subs_of((16, 128))
    members = jnp.concatenate([(which == group[x % 4 : x % 4 + 1, :]).astype(F32) for x in range(8)], axis=0)
    members = members.astype(jnp.bfloat16)
    members = jnp.concatenate([members, members], axis=1)
    sub, eighth = subs_of((8, 128)), lanes_of((8, 128)) // 16
    own = (sub == eighth).astype(F32)
    for c in range(len(PAIRS) // CHUNK):
        at = pl.ds(c * CHUNK * 8, CHUNK * 8)
        value = sums[at, :]
        high = value.astype(jnp.bfloat16)
        low = (value - high.astype(F32)).astype(jnp.bfloat16)
        by_group = lax.dot_general(
            jnp.concatenate([high, low], axis=1), members, (((1,), (1,)), ((), ())), preferred_element_type=F32
        )
        sums[at, :] = (by_group.reshape(CHUNK, 8, 128) * own[None]).reshape(CHUNK * 8, 128)

    def column(fixed, block):
        pairs = [(min(fixed, 8 * block + r), max(fixed, 8 * block + r)) for r in range(8)]
        return fold_rows([sums[pl.ds(PAIR_AT[pair] * 8, 8), :] for pair in pairs], sub)

    packed = [fold_lanes([column(8 * i + r, j) for r in range(8)], eighth) for i, j in BLOCKS]
    sides = [column(NP + a, block) for a in range(3) for block in range(3)] + [jnp.zeros((8, 128), F32)] * 7
    packed += [fold_lanes(sides[:8], eighth), fold_lanes(sides[8:], eighth)]
    for i, value in enumerate(packed):
        for copy in range(copies):
            out[pl.ds(copy * PAYLOAD + 8 * i, 8), :] = value


def apply_operator(shift, weights, height, emit):
    for x in range(4):
        total = [None] * 3
        for b in range(3):
            center = shift[pl.ds((18 + 6 * b + x + 1) * height, height), :]
            for o, (dx, dy) in enumerate(OFFSETS):
                moved = shift[pl.ds(((dy + 1) * 18 + 6 * b + x + dx + 1) * height, height), :]
                differ = center - moved
                for a in range(3):
                    term = differ * weights[pl.ds(72 * x + 24 * a + 3 * o + b, 1), :]
                    total[a] = term if total[a] is None else total[a] + term
        for a in range(3):
            emit(a, x, total[a])


def fit_kernel(
    copies, scale, par, sums, precond, vec, nbr, species, block_of, above, below, far, near,
    theta, weights, term, low_out, high_out, shift,
):
    sub, eighth = subs_of((8, 128)), lanes_of((8, 128)) // 16

    def total(i):
        value = sums[pl.ds(8 * i, 8), :]
        for copy in range(1, copies):
            value = value + sums[pl.ds(copy * PAYLOAD + 8 * i, 8), :]
        return value * scale

    def spread(value, k):
        value = jnp.where(eighth == k, value, 0.0)
        for step in (16, 32, 64):
            value = value + pltpu.roll(value, step, 1)
        return value

    sides = [spread(total(6 + i // 8), i % 8) for i in range(9)]
    rhs = []
    for block in range(3):
        value = jnp.where(eighth == 0, sides[block], 0.0)
        for a in (1, 2):
            value = jnp.where(eighth == a, sides[3 * a + block], value)
        rhs.append(value)
    of_group = lanes_of((NP, 128)) & 15

    def solve(right):
        every = jnp.dot(precond[...], right, precision=HIGH, preferred_element_type=F32)
        result = every[0:NP]
        for g in range(1, NG):
            result = jnp.where(of_group == g, every[g * NP : (g + 1) * NP], result)
        return result

    first = solve(jnp.concatenate(rhs, axis=0))
    part = [first[8 * i : 8 * i + 8] for i in range(3)]
    remain = list(rhs)
    for m, (i, j) in enumerate(BLOCKS):
        value = total(m)
        tiles = [spread(value, r) for r in range(8)]
        for r in range(8):
            remain[j] = remain[j] - tiles[r] * part[i][r : r + 1, :]
        if i != j:
            remain[i] = remain[i] - fold_rows([tiles[r] * part[j] for r in range(8)], sub)
    fitted = first + solve(jnp.concatenate(remain, axis=0))
    theta[...] = fitted

    of_part = lanes_of((NP, 128)) // 16
    stacked = jnp.concatenate(
        [jnp.where((of_part == a) & (of_group < NG), fitted, 0.0) for a in range(3)], axis=0
    )
    group = block_of[...] * NSPEC + species[...]
    which = subs_of((128, 128)) & 15
    p_row, o_col = subs_of((NP, 8)), lanes_of((NP, 8))
    repeat = ((p_row >= 3 * o_col) & (p_row < 3 * o_col + 3)).astype(F32)
    for x in range(4):
        member = (which == group[x : x + 1, :]).astype(F32)
        by_atom = jnp.dot(stacked, member, precision=HIGH, preferred_element_type=F32)
        mask = nbr[pl.ds(x, 8, stride=4), :].astype(F32)
        mask = jnp.dot(repeat, mask, precision=HIGH, preferred_element_type=F32)
        weights[pl.ds(72 * x, 72), :] = by_atom * jnp.concatenate([mask, mask, mask], axis=0)

    tile = natural_tile(vec, above, below, 48)
    spread_columns(par[0] == 0, lambda slot, k: tile(slot - 2, k), range(2, 10), near, far, shift, 64)

    def emit(a, x, value):
        term[pl.ds((4 * a + x) * 64, 64), :] = value
        if x == 0:
            low_out[pl.ds(64 * a, 64), :] = value
        if x == 3:
            high_out[pl.ds(64 * a, 64), :] = value

    apply_operator(shift, weights, 64, emit)


def last_kernel(par, term, above, below, far, near, weights, vec, out, shift):
    spread_columns(par[0] == 0, blocked_tile(term, above, below), range(8), near, far, shift, 64)

    def emit(a, x, value):
        at = pl.ds(4 * a + x, 64, stride=12)
        out[at, :] = 2.0 * value - vec[at, :]

    apply_operator(shift, weights, 64, emit)


IN_SMEM = pl.BlockSpec(memory_space=pltpu.SMEM)
IN_VMEM = pl.BlockSpec(memory_space=pltpu.VMEM)
ANYWHERE = pl.BlockSpec(memory_space=pl.ANY)


def call(kernel, name, ins, outs, scratch=()):
    return pl.pallas_call(
        kernel,
        name=name,
        in_specs=ins,
        out_specs=[IN_VMEM] * len(outs),
        out_shape=[jax.ShapeDtypeStruct((rows, 128), F32) for rows in outs],
        scratch_shapes=[pltpu.VMEM((rows, 128), F32) if isinstance(rows, int) else rows for rows in scratch],
        compiler_params=pltpu.CompilerParams(vmem_limit_bytes=40 << 20),
    )


def along(value, axis, step):
    n = lax.axis_size(axis)
    return lax.ppermute(value, axis, [(i, (i + step) % n) for i in range(n)])


def from_both(columns):
    n = lax.axis_size("gy")
    near = lax.ppermute(columns, "gy", [(i, i ^ 1) for i in range(n)])
    pairs = [(i, (i + 1) % n) for i in range(1, n, 2)]
    far = lax.ppermute(columns, "gy", pairs + [(j, i) for i, j in pairs])
    return near, far


def shards(displacements, forces, neighbours, species, block_of, precond, vectors):
    snap = lax.axis_size("snap")
    scale = 1.0 / (displacements.shape[0] * snap * AB)
    disp = displacements.reshape(-1, 128)
    load = forces.reshape(-1, 128)
    vec = vectors.reshape(-1, 128)
    nbr = neighbours.reshape(-1, 128)
    par = (lax.axis_index("gy") % 2).astype(jnp.int32).reshape(1)

    low, high = call(rows_kernel, "rows", [ANYWHERE] * 2, (240, 240), (pltpu.SemaphoreType.DMA((4,)),))(
        displacements.reshape(-1, 4, 128), vectors.reshape(-1, 4, 128)
    )
    above, below = along(high, "gx", 1), along(low, "gx", -1)
    (columns,) = call(columns_kernel, "columns", [IN_VMEM] * 4, (32,))(disp, vec, above, below)
    near, far = from_both(columns)
    (part,) = call(
        functools.partial(gram_kernel, snap),
        "gram",
        [IN_SMEM] + [IN_VMEM] * 9,
        (snap * PAYLOAD,),
        (54 * 16, 27 * 64, len(PAIRS) * 8),
    )(par, disp, load, nbr, species, block_of, above, below, far, near)
    part = lax.all_to_all(part, "snap", 0, 0, tiled=True)
    theta, weights, term, low, high = call(
        functools.partial(fit_kernel, snap, scale),
        "fit",
        [IN_SMEM] + [IN_VMEM] * 10,
        (NP, 288, 768, 192, 192),
        (54 * 64,),
    )(par, part, precond.reshape(NG * NP, NP), vec, nbr, species, block_of, above, below, far, near)
    above, below = along(high, "gx", 1), along(low, "gx", -1)
    (columns,) = call(term_columns_kernel, "term_columns", [IN_VMEM] * 3, (24,))(term, above, below)
    near, far = from_both(columns)
    (result,) = call(last_kernel, "last", [IN_SMEM] + [IN_VMEM] * 7, (768,), (54 * 64,))(
        par, term, above, below, far, near, weights, vec
    )

    constants = theta.reshape(NP, 8, 16)[:, :3, :NG].transpose(2, 0, 1)
    return (
        constants.reshape(precond.shape[0], precond.shape[1], NP, 3),
        result.reshape(vectors.shape),
    )


def solution(mesh):
    in_specs = (
        P("snap", None, "gx", "gy"),
        P("snap", None, "gx", "gy"),
        P(None, "gx", "gy"),
        P("gx", "gy"),
        P("gx", "gy"),
        P(("gx", "gy"), None, None, None),
        P("snap", None, "gx", "gy"),
    )
    out_specs = (P(("gx", "gy"), None, None, None), P("snap", None, "gx", "gy"))
    return jax.shard_map(shards, mesh=mesh, in_specs=in_specs, out_specs=out_specs, check_vma=False)
```

time: 79.8 us -> 61.5 us (0.77)
  the two profiles are of different devices: /device:TPU:6 before, /device:TPU:8 now
where the time goes in v2:
time: 61.5 us; the launch traced here: 61.1 us
  starting transfers between devices  30.4 us (49%)
  waiting for transfers between devices  11.4 us (19%)
  blocking collectives  9.02 us (15%)
  Pallas kernels  6.19 us (10%)
  local copies, waits for them, and re-layouts  3.39 us (6%)
  between operations  0.78 us (1%)
    ppermute x2, starting transfers between devices, from_both(): far = lax.ppermute(columns, 'gy', pairs + [(j, i) for i, j in pairs])  15 us
    ppermute x4, starting transfers between devices, along(): return lax.ppermute(value, axis, [(i, (i + step) % n) for i in range(n)])  11.5 us
    all_to_all x1, blocking collectives, shards(): part = lax.all_to_all(part, 'snap', 0, 0, tiled=True)  9.02 us
    ppermute x4, waiting for transfers between devices, along(): return lax.ppermute(value, axis, [(i, (i + step) % n) for i in range(n)])  4.75 us
    ppermute x2, starting transfers between devices, from_both(): near = lax.ppermute(columns, 'gy', [(i, i ^ 1) for i in range(n)])  3.84 us
    ppermute x2, waiting for transfers between devices, from_both(): far = lax.ppermute(columns, 'gy', pairs + [(j, i) for i, j in pairs])  3.59 us
    unnamed x19, local copies, waits for them, and re-layouts  3.2 us
    ppermute x2, waiting for transfers between devices, from_both(): near = lax.ppermute(columns, 'gy', [(i, i ^ 1) for i in range(n)])  3.02 us
  transfers between devices with their start and end apart: 8, of which 5 were waited for; matrix products, arithmetic and copies ran while one was open for 1% of the time, Pallas kernels for 0%

profile of v2, /device:TPU:8, one launch (start us, length us, event | category | flops | bytes accessed | tf_op | source)
XLA Modules:
  0.0 61.1 jit_solution(14738796790365866016)
XLA Ops:
  0.6 0.0 copy-start
  0.6 1.0 %copy-done = f32[64,3,4,128]{3,2,1,0:T(4,128)S(1)} copy-done((f32[64,3,4,128]{3,2,1,0:T(4,128)S(1)}, f32[64,3,4,128]{3,2,1,0:T(4,128)}, u32[]{:S(2)}) %copy-start) | copy-done | bytes 393240
  1.6 0.0 copy-start.2
  1.6 0.9 %copy-done.2 = f32[16,3,4,128]{3,2,1,0:T(4,128)S(1)} copy-done((f32[16,3,4,128]{3,2,1,0:T(4,128)S(1)}, f32[16,3,4,128]{3,2,1,0:T(4,128)}, u32[]{:S(2)}) %copy-start.2) | copy-done | bytes 98328
  2.5 0.2 rows.1
  2.7 0.0 collective-permute-start
  2.8 8.5 %collective-permute-start.1 = (f32[240,128]{1,0:T(8,128)S(1)}, f32[240,128]{1,0:T(8,128)S(1)}, u32[]{:S(2)}, u32[]{:S(2)}) collective-permute-start(f32[240,128]{1,0:T(8,128)S(1)} %get-tuple-element.10), channel_id=1, source_target_pairs={{0,120},{8,0},{16,8},{24,16},{32,24},{40,32},{48,40},{56,48},{64,5... | collective-permute-start | bytes 368648 | tf_op jit(solution)/shard_map/ppermute | solution.py:295
  11.3 2.5 %collective-permute-done.above = f32[240,128]{1,0:T(8,128)S(1)} collective-permute-done((f32[240,128]{1,0:T(8,128)S(1)}, f32[240,128]{1,0:T(8,128)S(1)}, u32[]{:S(2)}, u32[]{:S(2)}) %collective-permute-start) | collective-permute-done | bytes 122912 | tf_op jit(solution)/shard_map/ppermute | solution.py:295
  13.8 0.0 collective-permute-done.1.below
  13.8 0.0 copy-start.3
  13.8 0.0 copy-start.5
  13.8 0.3 columns.1
  14.1 0.0 copy-start.6
  14.1 9.0 %collective-permute-start.2 = (f32[32,128]{1,0:T(8,128)S(1)}, f32[32,128]{1,0:T(8,128)S(1)}, u32[]{:S(2)}, u32[]{:S(2)}) collective-permute-start(f32[32,128]{1,0:T(8,128)S(1)} %columns.1), channel_id=1, source_target_pairs={{1,2},{3,4},{5,6},{7,0},{2,1},{4,3},{6,5},{0,7},{9,10},{11,12},{13... | collective-permute-start | bytes 49160 | tf_op jit(solution)/shard_map/ppermute | solution.py:302
  23.1 1.9 %collective-permute-start.3 = (f32[32,128]{1,0:T(8,128)S(1)}, f32[32,128]{1,0:T(8,128)S(1)}, u32[]{:S(2)}, u32[]{:S(2)}) collective-permute-start(f32[32,128]{1,0:T(8,128)S(1)} %columns.1), channel_id=1, source_target_pairs={{0,1},{1,0},{2,3},{3,2},{4,5},{5,4},{6,7},{7,6},{8,9},{9,8},{10,11... | collective-permute-start | bytes 49160 | tf_op jit(solution)/shard_map/ppermute | solution.py:300
  25.1 0.7 %collective-permute-done.2.far = f32[32,128]{1,0:T(8,128)S(1)} collective-permute-done((f32[32,128]{1,0:T(8,128)S(1)}, f32[32,128]{1,0:T(8,128)S(1)}, u32[]{:S(2)}, u32[]{:S(2)}) %collective-permute-start.2) | collective-permute-done | bytes 16416 | tf_op jit(solution)/shard_map/ppermute | solution.py:302
  25.7 3.0 %collective-permute-done.3.near = f32[32,128]{1,0:T(8,128)S(1)} collective-permute-done((f32[32,128]{1,0:T(8,128)S(1)}, f32[32,128]{1,0:T(8,128)S(1)}, u32[]{:S(2)}, u32[]{:S(2)}) %collective-permute-start.3) | collective-permute-done | bytes 16416 | tf_op jit(solution)/shard_map/ppermute | solution.py:300
  28.7 0.0 copy-start.8
  28.8 0.0 copy-start.7
  28.8 0.0 copy-done.3
  28.8 0.0 copy-done.5
  28.8 0.0 copy-done.6
  28.8 0.7 %copy-done.8 = s32[4,128]{1,0:T(4,128)S(1)} copy-done((s32[4,128]{1,0:T(4,128)S(1)}, s32[4,128]{1,0:T(4,128)}, u32[]{:S(2)}) %copy-start.8) | copy-done | bytes 2072
  29.4 0.0 copy-done.7
  29.4 0.0 copy-start.1
  29.4 1.6 %gram.1 = f32[256,128]{1,0:T(8,128)S(1)} custom-call(s32[1]{0:T(128)} %bitcast.par, f32[192,128]{1,0:T(8,128)S(1)} %bitcast.20, f32[192,128]{1,0:T(8,128)S(1)} %bitcast.24, s32[32,128]{1,0:T(8,128)S(1)} %bitcast.25, s32[4,128]{1,0:T(4,128)S(1)} %copy-done.7, s32[4,128]{1,0:T(4,128)S(1)} %copy-done.8, f32[240,128]{1,0:T(8,128)S(1)} %collective-permute-done.above, ...), custom_call_target="tpu_custom_call" | custom-call | tf_op jit(solution)/shard_map/gram/pallas_call | solution.py:321
  31.1 0.0 copy-start.4
  31.1 9.0 %all_to_all.11 = f32[4,64,128]{2,1,0:T(8,128)S(1)} all-to-all(f32[4,64,128]{2,1,0:T(8,128)S(1)} %bitcast.22), channel_id=1, replica_groups=mesh['snap'=4,'gx'=16,'gy'=8] {'snap'}, dimensions={0} | all-to-all | bytes 262144 | tf_op jit(solution)/shard_map/all_to_all | solution.py:328
  40.1 0.0 copy-done.1
  40.1 0.0 copy-done.4
  40.1 2.1 %fit.1 = (f32[24,128]{1,0:T(8,128)S(1)}, f32[288,128]{1,0:T(8,128)S(1)}, f32[768,128]{1,0:T(8,128)S(1)}, f32[192,128]{1,0:T(8,128)S(1)}, f32[192,128]{1,0:T(8,128)S(1)}) custom-call(s32[1]{0:T(128)} %bitcast.par, f32[256,128]{1,0:T(8,128)S(1)} %bitcast.21, f32[288,24]{1,0:T(8,128)S(1)} %bitcast.23, f32[768,128]{1,0:T(8,128)S(1)} %bitcast.16, ...), custom_call_target="tpu_custom_call" | custom-call | tf_op jit(solution)/shard_map/fit/pallas_call | solution.py:329
  42.3 0.0 collective-permute-start.4
  42.3 2.9 %collective-permute-start.5 = (f32[192,128]{1,0:T(8,128)S(1)}, f32[192,128]{1,0:T(8,128)S(1)}, u32[]{:S(2)}, u32[]{:S(2)}) collective-permute-start(f32[192,128]{1,0:T(8,128)S(1)} %get-tuple-element.14), channel_id=1, source_target_pairs={{0,120},{8,0},{16,8},{24,16},{32,24},{40,32},{48,40},{56,48},{64,5... | collective-permute-start | bytes 294920 | tf_op jit(solution)/shard_map/ppermute | solution.py:295
  45.2 0.1 reshape.47
  45.3 2.2 %collective-permute-done.4.above = f32[192,128]{1,0:T(8,128)S(1)} collective-permute-done((f32[192,128]{1,0:T(8,128)S(1)}, f32[192,128]{1,0:T(8,128)S(1)}, u32[]{:S(2)}, u32[]{:S(2)}) %collective-permute-start.4) | collective-permute-done | bytes 98336 | tf_op jit(solution)/shard_map/ppermute | solution.py:295
  47.5 0.0 collective-permute-done.5.below
  47.5 0.2 term_columns.1
  47.8 6.0 %collective-permute-start.6 = (f32[24,128]{1,0:T(8,128)S(1)}, f32[24,128]{1,0:T(8,128)S(1)}, u32[]{:S(2)}, u32[]{:S(2)}) collective-permute-start(f32[24,128]{1,0:T(8,128)S(1)} %term_columns.1), channel_id=1, source_target_pairs={{1,2},{3,4},{5,6},{7,0},{2,1},{4,3},{6,5},{0,7},{9,10},{11,12},{13... | collective-permute-start | bytes 36872 | tf_op jit(solution)/shard_map/ppermute | solution.py:302
  53.8 1.9 %collective-permute-start.7 = (f32[24,128]{1,0:T(8,128)S(1)}, f32[24,128]{1,0:T(8,128)S(1)}, u32[]{:S(2)}, u32[]{:S(2)}) collective-permute-start(f32[24,128]{1,0:T(8,128)S(1)} %term_columns.1), channel_id=1, source_target_pairs={{0,1},{1,0},{2,3},{3,2},{4,5},{5,4},{6,7},{7,6},{8,9},{9,8},{10,11... | collective-permute-start | bytes 36872 | tf_op jit(solution)/shard_map/ppermute | solution.py:300
  55.7 0.1 copy.9
  55.8 0.6 %copy.10 = f32[4,3,24,3]{2,0,3,1:T(4,128)} copy(f32[4,3,24,3]{2,3,1,0:T(4,128)S(1)} %bitcast.28) | data formatting | bytes 6912
  56.5 2.9 %collective-permute-done.6.far = f32[24,128]{1,0:T(8,128)S(1)} collective-permute-done((f32[24,128]{1,0:T(8,128)S(1)}, f32[24,128]{1,0:T(8,128)S(1)}, u32[]{:S(2)}, u32[]{:S(2)}) %collective-permute-start.6) | collective-permute-done | bytes 12320 | tf_op jit(solution)/shard_map/ppermute | solution.py:302
  59.4 0.0 collective-permute-done.7.near
  59.4 1.7 %last.1 = f32[768,128]{1,0:T(8,128)} custom-call(s32[1]{0:T(128)} %bitcast.par, f32[768,128]{1,0:T(8,128)S(1)} %get-tuple-element.12.term, f32[192,128]{1,0:T(8,128)S(1)} %collective-permute-done.4.above, f32[192,128]{1,0:T(8,128)S(1)} %collective-permute-done.5.below, f32[24,128]{1,0:T(8,128)S(1)} %collective-permute-done.6.far, ...), custom_call_target="tpu_custom_call" | custom-call | tf_op jit(solution)/shard_map/last/pallas_call | solution.py:339
  (1 shorter events, 0.0 us)
Async XLA Ops:
  0.6 1.0 %copy-start = (f32[64,3,4,128]{3,2,1,0:T(4,128)S(1)}, f32[64,3,4,128]{3,2,1,0:T(4,128)}, u32[]{:S(2)}) copy-start(f32[64,3,4,128]{3,2,1,0:T(4,128)} %param.13) | copy-start | bytes 1179652
  1.6 0.9 %copy-start.2 = (f32[16,3,4,128]{3,2,1,0:T(4,128)S(1)}, f32[16,3,4,128]{3,2,1,0:T(4,128)}, u32[]{:S(2)}) copy-start(f32[16,3,4,128]{3,2,1,0:T(4,128)} %param.7) | copy-start | bytes 294916
  2.7 11.1 %collective-permute-start = (f32[240,128]{1,0:T(8,128)S(1)}, f32[240,128]{1,0:T(8,128)S(1)}, u32[]{:S(2)}, u32[]{:S(2)}) collective-permute-start(f32[240,128]{1,0:T(8,128)S(1)} %get-tuple-element.9), channel_id=1, source_target_pairs={{0,8},{8,16},{16,24},{24,32},{32,40},{40,48},{48,56},{56,64},{64,7... | collective-permute-start | bytes 368648 | tf_op jit(solution)/shard_map/ppermute | solution.py:295
  2.8 11.0 %collective-permute-start.1 = (f32[240,128]{1,0:T(8,128)S(1)}, f32[240,128]{1,0:T(8,128)S(1)}, u32[]{:S(2)}, u32[]{:S(2)}) collective-permute-start(f32[240,128]{1,0:T(8,128)S(1)} %get-tuple-element.10), channel_id=1, source_target_pairs={{0,120},{8,0},{16,8},{24,16},{32,24},{40,32},{48,40},{56,48},{64,5... | collective-permute-start | bytes 368648 | tf_op jit(solution)/shard_map/ppermute | solution.py:295
  13.8 15.0 %copy-start.3 = (f32[16,3,4,128]{3,2,1,0:T(4,128)S(1)}, f32[16,3,4,128]{3,2,1,0:T(4,128)}, u32[]{:S(2)}) copy-start(f32[16,3,4,128]{3,2,1,0:T(4,128)} %param.7) | copy-start | bytes 294916
  13.8 15.0 %copy-start.5 = (f32[16,3,4,128]{3,2,1,0:T(4,128)S(1)}, f32[16,3,4,128]{3,2,1,0:T(4,128)}, u32[]{:S(2)}) copy-start(f32[16,3,4,128]{3,2,1,0:T(4,128)} %param.8) | copy-start | bytes 294916
  14.1 14.7 %copy-start.6 = (s32[8,4,128]{2,1,0:T(4,128)S(1)}, s32[8,4,128]{2,1,0:T(4,128)}, u32[]{:S(2)}) copy-start(s32[8,4,128]{2,1,0:T(4,128)} %param.9) | copy-start | bytes 49156
  14.1 11.6 %collective-permute-start.2 = (f32[32,128]{1,0:T(8,128)S(1)}, f32[32,128]{1,0:T(8,128)S(1)}, u32[]{:S(2)}, u32[]{:S(2)}) collective-permute-start(f32[32,128]{1,0:T(8,128)S(1)} %columns.1), channel_id=1, source_target_pairs={{1,2},{3,4},{5,6},{7,0},{2,1},{4,3},{6,5},{0,7},{9,10},{11,12},{13... | collective-permute-start | bytes 49160 | tf_op jit(solution)/shard_map/ppermute | solution.py:302
  23.1 5.6 %collective-permute-start.3 = (f32[32,128]{1,0:T(8,128)S(1)}, f32[32,128]{1,0:T(8,128)S(1)}, u32[]{:S(2)}, u32[]{:S(2)}) collective-permute-start(f32[32,128]{1,0:T(8,128)S(1)} %columns.1), channel_id=1, source_target_pairs={{0,1},{1,0},{2,3},{3,2},{4,5},{5,4},{6,7},{7,6},{8,9},{9,8},{10,11... | collective-permute-start | bytes 49160 | tf_op jit(solution)/shard_map/ppermute | solution.py:300
  28.7 0.7 %copy-start.8 = (s32[4,128]{1,0:T(4,128)S(1)}, s32[4,128]{1,0:T(4,128)}, u32[]{:S(2)}) copy-start(s32[4,128]{1,0:T(4,128)} %block_of.3) | copy-start | bytes 6148
  28.8 0.7 %copy-start.7 = (s32[4,128]{1,0:T(4,128)S(1)}, s32[4,128]{1,0:T(4,128)}, u32[]{:S(2)}) copy-start(s32[4,128]{1,0:T(4,128)} %species.3) | copy-start | bytes 6148
  29.4 10.7 %copy-start.1 = (f32[64,3,4,128]{3,2,1,0:T(4,128)S(1)}, f32[64,3,4,128]{3,2,1,0:T(4,128)}, u32[]{:S(2)}) copy-start(f32[64,3,4,128]{3,2,1,0:T(4,128)} %param.13) | copy-start | bytes 1179652
  31.1 9.0 %copy-start.4 = (f32[4,3,24,24]{3,2,1,0:T(8,128)S(1)}, f32[4,3,24,24]{3,2,1,0:T(8,128)}, u32[]{:S(2)}) copy-start(f32[4,3,24,24]{3,2,1,0:T(8,128)} %param.12) | copy-start | bytes 82948
  42.3 5.3 %collective-permute-start.4 = (f32[192,128]{1,0:T(8,128)S(1)}, f32[192,128]{1,0:T(8,128)S(1)}, u32[]{:S(2)}, u32[]{:S(2)}) collective-permute-start(f32[192,128]{1,0:T(8,128)S(1)} %get-tuple-element.13), channel_id=1, source_target_pairs={{0,8},{8,16},{16,24},{24,32},{32,40},{40,48},{48,56},{56,64},{64,7... | collective-permute-start | bytes 294920 | tf_op jit(solution)/shard_map/ppermute | solution.py:295
  42.3 5.2 %collective-permute-start.5 = (f32[192,128]{1,0:T(8,128)S(1)}, f32[192,128]{1,0:T(8,128)S(1)}, u32[]{:S(2)}, u32[]{:S(2)}) collective-permute-start(f32[192,128]{1,0:T(8,128)S(1)} %get-tuple-element.14), channel_id=1, source_target_pairs={{0,120},{8,0},{16,8},{24,16},{32,24},{40,32},{48,40},{56,48},{64,5... | collective-permute-start | bytes 294920 | tf_op jit(solution)/shard_map/ppermute | solution.py:295
  47.8 11.6 %collective-permute-start.6 = (f32[24,128]{1,0:T(8,128)S(1)}, f32[24,128]{1,0:T(8,128)S(1)}, u32[]{:S(2)}, u32[]{:S(2)}) collective-permute-start(f32[24,128]{1,0:T(8,128)S(1)} %term_columns.1), channel_id=1, source_target_pairs={{1,2},{3,4},{5,6},{7,0},{2,1},{4,3},{6,5},{0,7},{9,10},{11,12},{13... | collective-permute-start | bytes 36872 | tf_op jit(solution)/shard_map/ppermute | solution.py:302
  53.8 5.6 %collective-permute-start.7 = (f32[24,128]{1,0:T(8,128)S(1)}, f32[24,128]{1,0:T(8,128)S(1)}, u32[]{:S(2)}, u32[]{:S(2)}) collective-permute-start(f32[24,128]{1,0:T(8,128)S(1)} %term_columns.1), channel_id=1, source_target_pairs={{0,1},{1,0},{2,3},{3,2},{4,5},{5,4},{6,7},{7,6},{8,9},{9,8},{10,11... | collective-permute-start | bytes 36872 | tf_op jit(solution)/shard_map/ppermute | solution.py:300

commit v3 on v2

--- a/solution.py
+++ b/solution.py
@@ -39,33 +39,50 @@
         columns[pl.ds(8 * t, 8), :] = value
 
 
-def spread_columns(even, tile_at, slots, near_ref, far_ref, shift_ref, height):
+def edge_tiles(even, slots, far_ref, near_ref):
     lane = lanes_of((8, 128))
     edges = {}
     for t in sorted({lane_slot(slot, 0)[0] for slot in slots}):
         near, far = near_ref[pl.ds(8 * t, 8), :], far_ref[pl.ds(8 * t, 8), :]
         left, right = jnp.where(even, far, near), jnp.where(even, near, far)
         edges[t] = jnp.where((lane & 1) == 0, pltpu.roll(right, 127, 1), pltpu.roll(left, 1, 1))
+
+    def edge(slot, k):
+        t, at = lane_slot(slot, k)
+        return pltpu.roll(edges[t], 127 - at, 1)
+
+    return edge
+
+
+def spread_columns(edge, tile_at, slots, shift_ref, height):
+    lane = lanes_of((8, 128))
     for k in range(18):
         for place, slot in enumerate(slots):
-            t, at = lane_slot(slot, k)
             values = tile_at(slot, k)
-            edge = pltpu.roll(edges[t], 127 - at, 1)
+            outside = edge(slot, k)
             base = k * height + 8 * place
-            shift_ref[pl.ds(base, 8), :] = jnp.where(lane == 0, edge, pltpu.roll(values, 1, 1))
+            shift_ref[pl.ds(base, 8), :] = jnp.where(lane == 0, outside, pltpu.roll(values, 1, 1))
             shift_ref[pl.ds(18 * height + base, 8), :] = values
-            shift_ref[pl.ds(36 * height + base, 8), :] = jnp.where(lane == 127, edge, pltpu.roll(values, 127, 1))
-
-
-def rows_kernel(disp, vec, low, high, sems):
-    copies = []
-    for out, x in ((low, 0), (high, 3)):
-        for source, at in ((disp, pl.ds(0, 48)), (vec, pl.ds(48, 192))):
-            copies.append(pltpu.make_async_copy(source.at[:, x, :], out.at[at, :], sems.at[len(copies)]))
+            shift_ref[pl.ds(36 * height + base, 8), :] = jnp.where(lane == 127, outside, pltpu.roll(values, 127, 1))
+
+
+def load_kernel(
+    disp_in, vec_in, load_in, nbr_in, species, block_of, precond_in,
+    disp, vec, low, high, load, nbr, group, precond, kind, block, sems,
+):
+    pairs = [(disp_in, disp), (vec_in, vec), (species, kind), (block_of, block), (load_in, load), (nbr_in, nbr)]
+    pairs.append((precond_in, precond))
+    copies = [pltpu.make_async_copy(source, out, sems.at[i]) for i, (source, out) in enumerate(pairs)]
     for copy in copies:
         copy.start()
-    for copy in copies:
+    copies[0].wait()
+    copies[1].wait()
+    for out, x in ((low, 0), (high, 3)):
+        out[pl.ds(0, 48), :] = disp[pl.ds(x, 48, stride=4), :]
+        out[pl.ds(48, 192), :] = vec[pl.ds(x, 192, stride=4), :]
+    for copy in copies[2:]:
         copy.wait()
+    group[...] = block[...] * NSPEC + kind[...]
 
 
 def natural_tile(source, above, below, base):
@@ -78,12 +95,12 @@
     return tile
 
 
-def blocked_tile(source, above, below):
+def term_tile(low, mid, high, above, below):
     def tile(place, k):
         b, x = k // 6, k % 6 - 1
-        if 0 <= x < 4:
-            return source[pl.ds((4 * b + x) * 64 + 8 * place, 8), :]
-        return (above if x < 0 else below)[pl.ds(b * 64 + 8 * place, 8), :]
+        if x in (1, 2):
+            return mid[pl.ds((2 * b + x - 1) * 64 + 8 * place, 8), :]
+        return {-1: above, 0: low, 3: high, 4: below}[x][pl.ds(b * 64 + 8 * place, 8), :]
 
     return tile
 
@@ -94,8 +111,8 @@
     pack_columns(lambda slot, k: disp_tile(slot, k) if slot < 2 else vec_tile(slot - 2, k), range(10), columns)
 
 
-def term_columns_kernel(term, above, below, columns):
-    pack_columns(blocked_tile(term, above, below), range(8), columns)
+def term_columns_kernel(low, mid, high, above, below, columns):
+    pack_columns(term_tile(low, mid, high, above, below), range(8), columns)
 
 
 def fold_rows(tiles, sub):
@@ -127,9 +144,9 @@
 CHUNK = 62
 
 
-def gram_kernel(copies, par, disp, forces, nbr, species, block_of, above, below, far, near, out, shift, feats, sums):
-    tile = natural_tile(disp, above, below, 0)
-    spread_columns(par[0] == 0, tile, range(2), near, far, shift, 16)
+def gram_kernel(copies, par, disp, forces, nbr, group, above, below, near, far, out, shift, feats, sums):
+    edge = edge_tiles(par[0] == 0, range(2), far, near)
+    spread_columns(edge, natural_tile(disp, above, below, 0), range(2), shift, 16)
     for x in range(4):
         for o, (dx, dy) in enumerate(OFFSETS):
             mask = nbr[pl.ds(4 * o + x, 1), :].astype(F32)
@@ -144,9 +161,8 @@
         for p in range(q, NP + 3):
             right = feats[pl.ds(p * 64, 64), :].reshape(8, 8, 128)
             sums[pl.ds(PAIR_AT[q, p] * 8, 8), :] = jnp.sum(left * right, axis=0)
-    group = block_of[...] * NSPEC + species[...]
     which = subs_of((16, 128))
-    members = jnp.concatenate([(which == group[x % 4 : x % 4 + 1, :]).astype(F32) for x in range(8)], axis=0)
+    members = jnp.concatenate([(which == group[pl.ds(x % 4, 1), :]).astype(F32) for x in range(8)], axis=0)
     members = members.astype(jnp.bfloat16)
     members = jnp.concatenate([members, members], axis=1)
     sub, eighth = subs_of((8, 128)), lanes_of((8, 128)) // 16
@@ -173,13 +189,13 @@
             out[pl.ds(copy * PAYLOAD + 8 * i, 8), :] = value
 
 
-def apply_operator(shift, weights, height, emit):
-    for x in range(4):
+def apply_operator(shift, weights, lattice_rows, emit):
+    for x in lattice_rows:
         total = [None] * 3
         for b in range(3):
-            center = shift[pl.ds((18 + 6 * b + x + 1) * height, height), :]
+            center = shift[pl.ds((18 + 6 * b + x + 1) * 64, 64), :]
             for o, (dx, dy) in enumerate(OFFSETS):
-                moved = shift[pl.ds(((dy + 1) * 18 + 6 * b + x + dx + 1) * height, height), :]
+                moved = shift[pl.ds(((dy + 1) * 18 + 6 * b + x + dx + 1) * 64, 64), :]
                 differ = center - moved
                 for a in range(3):
                     term = differ * weights[pl.ds(72 * x + 24 * a + 3 * o + b, 1), :]
@@ -189,8 +205,8 @@
 
 
 def fit_kernel(
-    copies, scale, par, sums, precond, vec, nbr, species, block_of, above, below, far, near,
-    theta, weights, term, low_out, high_out, shift,
+    copies, scale, par, sums, precond, vec, nbr, group, above, below, near, far,
+    theta, weights, low_out, high_out, shift,
 ):
     sub, eighth = subs_of((8, 128)), lanes_of((8, 128)) // 16
 
@@ -239,54 +255,87 @@
     stacked = jnp.concatenate(
         [jnp.where((of_part == a) & (of_group < NG), fitted, 0.0) for a in range(3)], axis=0
     )
-    group = block_of[...] * NSPEC + species[...]
     which = subs_of((128, 128)) & 15
     p_row, o_col = subs_of((NP, 8)), lanes_of((NP, 8))
     repeat = ((p_row >= 3 * o_col) & (p_row < 3 * o_col + 3)).astype(F32)
     for x in range(4):
-        member = (which == group[x : x + 1, :]).astype(F32)
+        member = (which == group[pl.ds(x, 1), :]).astype(F32)
         by_atom = jnp.dot(stacked, member, precision=HIGH, preferred_element_type=F32)
         mask = nbr[pl.ds(x, 8, stride=4), :].astype(F32)
         mask = jnp.dot(repeat, mask, precision=HIGH, preferred_element_type=F32)
         weights[pl.ds(72 * x, 72), :] = by_atom * jnp.concatenate([mask, mask, mask], axis=0)
 
     tile = natural_tile(vec, above, below, 48)
-    spread_columns(par[0] == 0, lambda slot, k: tile(slot - 2, k), range(2, 10), near, far, shift, 64)
+    edge = edge_tiles(par[0] == 0, range(2, 10), far, near)
+    spread_columns(edge, lambda slot, k: tile(slot - 2, k), range(2, 10), shift, 64)
 
     def emit(a, x, value):
-        term[pl.ds((4 * a + x) * 64, 64), :] = value
-        if x == 0:
-            low_out[pl.ds(64 * a, 64), :] = value
-        if x == 3:
-            high_out[pl.ds(64 * a, 64), :] = value
-
-    apply_operator(shift, weights, 64, emit)
-
-
-def last_kernel(par, term, above, below, far, near, weights, vec, out, shift):
-    spread_columns(par[0] == 0, blocked_tile(term, above, below), range(8), near, far, shift, 64)
-
+        (high_out if x else low_out)[pl.ds(64 * a, 64), :] = value
+
+    apply_operator(shift, weights, (0, 3), emit)
+
+
+def middle_kernel(shift, weights, theta, mid, constants):
     def emit(a, x, value):
-        at = pl.ds(4 * a + x, 64, stride=12)
-        out[at, :] = 2.0 * value - vec[at, :]
-
-    apply_operator(shift, weights, 64, emit)
+        mid[pl.ds((2 * a + x - 1) * 64, 64), :] = value
+
+    apply_operator(shift, weights, (1, 2), emit)
+    row, lane = subs_of((36, 128)), lanes_of((36, 128))
+    which = row >> 2
+    kind = (which >= 3).astype(jnp.int32) + (which >= 6).astype(jnp.int32)
+    pick = (lane == 16 * (which - 3 * kind) + 3 * (row & 3) + kind).astype(F32)
+    constants[...] = lax.dot_general(
+        pick, theta[...], (((1,), (1,)), ((), ())), precision=HIGH, preferred_element_type=F32
+    )
+
+
+def inner_kernel(low, mid, high, above, below, weights, vec, out, shift):
+    empty = jnp.zeros((8, 128), F32)
+    spread_columns(lambda slot, k: empty, term_tile(low, mid, high, above, below), range(8), shift, 64)
+
+    def emit(a, x, value):
+        out[pl.ds((4 * a + x) * 64, 64), :] = 2.0 * value - vec[pl.ds(4 * a + x, 64, stride=12), :]
+
+    apply_operator(shift, weights, range(4), emit)
+
+
+def outer_kernel(par, inner, near, far, weights, out, edges):
+    edge = edge_tiles(par[0] == 0, range(8), far, near)
+    for k in range(18):
+        for slot in range(8):
+            edges[pl.ds(64 * k + 8 * slot, 8), :] = edge(slot, k)
+    lane = lanes_of((1, 128))
+    for x in range(4):
+        total = [inner[pl.ds((4 * a + x) * 64, 64), :] for a in range(3)]
+        for b in range(3):
+            for dx in (-1, 0, 1):
+                outside = edges[pl.ds(64 * (6 * b + x + dx + 1), 64), :]
+                for a in range(3):
+                    base = 72 * x + 24 * a + b
+                    left = weights[pl.ds(base + 3 * OFFSETS.index((dx, -1)), 1), :]
+                    right = weights[pl.ds(base + 3 * OFFSETS.index((dx, 1)), 1), :]
+                    weight = jnp.where(lane == 0, 2.0 * left, jnp.where(lane == 127, 2.0 * right, 0.0))
+                    total[a] = total[a] - outside * weight
+        for a in range(3):
+            out[pl.ds(4 * a + x, 64, stride=12), :] = total[a]
 
 
 IN_SMEM = pl.BlockSpec(memory_space=pltpu.SMEM)
 IN_VMEM = pl.BlockSpec(memory_space=pltpu.VMEM)
-ANYWHERE = pl.BlockSpec(memory_space=pl.ANY)
-
-
-def call(kernel, name, ins, outs, scratch=()):
+IN_HBM = pl.BlockSpec(memory_space=pltpu.HBM)
+
+
+def call(kernel, name, ins, outs, scratch=(), flops=0):
+    outs = [jax.ShapeDtypeStruct((rows, 128), F32) if isinstance(rows, int) else rows for rows in outs]
     return pl.pallas_call(
         kernel,
         name=name,
         in_specs=ins,
         out_specs=[IN_VMEM] * len(outs),
-        out_shape=[jax.ShapeDtypeStruct((rows, 128), F32) for rows in outs],
+        out_shape=outs,
         scratch_shapes=[pltpu.VMEM((rows, 128), F32) if isinstance(rows, int) else rows for rows in scratch],
         compiler_params=pltpu.CompilerParams(vmem_limit_bytes=40 << 20),
+        cost_estimate=pl.CostEstimate(flops=flops, bytes_accessed=1 << 20, transcendentals=0),
     )
 
 
@@ -306,45 +355,64 @@
 def shards(displacements, forces, neighbours, species, block_of, precond, vectors):
     snap = lax.axis_size("snap")
     scale = 1.0 / (displacements.shape[0] * snap * AB)
-    disp = displacements.reshape(-1, 128)
-    load = forces.reshape(-1, 128)
-    vec = vectors.reshape(-1, 128)
-    nbr = neighbours.reshape(-1, 128)
     par = (lax.axis_index("gy") % 2).astype(jnp.int32).reshape(1)
 
-    low, high = call(rows_kernel, "rows", [ANYWHERE] * 2, (240, 240), (pltpu.SemaphoreType.DMA((4,)),))(
-        displacements.reshape(-1, 4, 128), vectors.reshape(-1, 4, 128)
-    )
+    whole = [
+        pltpu.with_memory_space_constraint(value, pltpu.HBM)
+        for value in (
+            displacements.reshape(-1, 128),
+            vectors.reshape(-1, 128),
+            forces.reshape(-1, 128),
+            neighbours.reshape(-1, 128),
+            species,
+            block_of,
+            precond.reshape(NG * NP, NP),
+        )
+    ]
+    tile = jax.ShapeDtypeStruct((4, 128), jnp.int32)
+    disp, vec, low, high, load, nbr, group, inverses = call(
+        load_kernel,
+        "load",
+        [IN_HBM] * 7,
+        (192, 768, 240, 240, 192, jax.ShapeDtypeStruct((32, 128), jnp.int32), tile, jax.ShapeDtypeStruct((NG * NP, NP), F32)),
+        (pltpu.VMEM((4, 128), jnp.int32), pltpu.VMEM((4, 128), jnp.int32), pltpu.SemaphoreType.DMA((7,))),
+    )(*whole)
     above, below = along(high, "gx", 1), along(low, "gx", -1)
     (columns,) = call(columns_kernel, "columns", [IN_VMEM] * 4, (32,))(disp, vec, above, below)
     near, far = from_both(columns)
     (part,) = call(
         functools.partial(gram_kernel, snap),
         "gram",
-        [IN_SMEM] + [IN_VMEM] * 9,
+        [IN_SMEM] + [IN_VMEM] * 8,
         (snap * PAYLOAD,),
         (54 * 16, 27 * 64, len(PAIRS) * 8),
-    )(par, disp, load, nbr, species, block_of, above, below, far, near)
+    )(par, disp, load, nbr, group, above, below, near, far)
     part = lax.all_to_all(part, "snap", 0, 0, tiled=True)
-    theta, weights, term, low, high = call(
+    theta, weights, low, high, shift = call(
         functools.partial(fit_kernel, snap, scale),
         "fit",
-        [IN_SMEM] + [IN_VMEM] * 10,
-        (NP, 288, 768, 192, 192),
-        (54 * 64,),
-    )(par, part, precond.reshape(NG * NP, NP), vec, nbr, species, block_of, above, below, far, near)
+        [IN_SMEM] + [IN_VMEM] * 9,
+        (NP, 288, 192, 192, 54 * 64),
+    )(par, part, inverses, vec, nbr, group, above, below, near, far)
     above, below = along(high, "gx", 1), along(low, "gx", -1)
-    (columns,) = call(term_columns_kernel, "term_columns", [IN_VMEM] * 3, (24,))(term, above, below)
+    mid, constants = call(
+        middle_kernel,
+        "middle",
+        [IN_VMEM] * 3,
+        (384, jax.ShapeDtypeStruct((3 * NG, NP), F32)),
+        flops=1 << 24,
+    )(shift, weights, theta)
+    (columns,) = call(term_columns_kernel, "term_columns", [IN_VMEM] * 5, (24,))(low, mid, high, above, below)
     near, far = from_both(columns)
-    (result,) = call(last_kernel, "last", [IN_SMEM] + [IN_VMEM] * 7, (768,), (54 * 64,))(
-        par, term, above, below, far, near, weights, vec
-    )
-
-    constants = theta.reshape(NP, 8, 16)[:, :3, :NG].transpose(2, 0, 1)
-    return (
-        constants.reshape(precond.shape[0], precond.shape[1], NP, 3),
-        result.reshape(vectors.shape),
-    )
+    (inner,) = call(inner_kernel, "inner", [IN_VMEM] * 7, (768,), (54 * 64,), flops=1 << 25)(
+        low, mid, high, above, below, weights, vec
+    )
+    (result,) = call(outer_kernel, "outer", [IN_SMEM] + [IN_VMEM] * 4, (768,), (18 * 64,))(
+        par, inner, near, far, weights
+    )
+
+    constants = constants.reshape(NSPEC, 3, precond.shape[0], NP).transpose(2, 0, 3, 1)
+    return (constants, result.reshape(vectors.shape))
 
 
 def solution(mesh):

time: 61.5 us -> 60.4 us (0.982)
  local copies, waits for them, and re-layouts: 3.39 us -> 0.62 us
  waiting for transfers between devices: 11.4 us -> 13.1 us
  Pallas kernels: 6.19 us -> 7.84 us
  starting transfers between devices: 30.4 us -> 28.9 us
    unnamed x19 -> x0, local copies, waits for them, and re-layouts: 3.2 us -> none
    ppermute x4, waiting for transfers between devices: 4.75 us -> 7.28 us  [along(): return lax.ppermute(value, axis, [(i, (i + step) % n) for i in range(n)])]
    ppermute x4, starting transfers between devices: 11.5 us -> 9.03 us  [along(): return lax.ppermute(value, axis, [(i, (i + step) % n) for i in range(n)])]
    pallas_call x3 -> x5, Pallas kernels: 2.15 us -> 4.05 us  [the longest x1 1.24 us: shards(): call(load_kernel, 'load', [IN_HBM] * 7, (192, 768, 240, 240, 192, jax.Sha...]
    ppermute x2, waiting for transfers between devices: 3.59 us -> 1.81 us  [from_both(): far = lax.ppermute(columns, 'gy', pairs + [(j, i) for i, j in pairs])]
    ppermute x2, waiting for transfers between devices: 3.02 us -> 4.04 us  [from_both(): near = lax.ppermute(columns, 'gy', [(i, i ^ 1) for i in range(n)])]
    ppermute x2, starting transfers between devices: 15 us -> 16.1 us  [from_both(): far = lax.ppermute(columns, 'gy', pairs + [(j, i) for i, j in pairs])]
  transfers between devices with their start and end apart: 8 -> 8, of which waited for: 5 -> 7; matrix products, arithmetic and copies ran while one was open for 1% -> 1% of each run, Pallas kernels for 0% -> 2%
where the time goes in v3:
time: 60.4 us; the launch traced here: 60.1 us
  starting transfers between devices  28.9 us (48%)
  waiting for transfers between devices  13.1 us (22%)
  blocking collectives  8.89 us (15%)
  Pallas kernels  7.84 us (13%)
  between operations  0.73 us (1%)
  local copies, waits for them, and re-layouts  0.62 us (1%)
    ppermute x2, starting transfers between devices, from_both(): far = lax.ppermute(columns, 'gy', pairs + [(j, i) for i, j in pairs])  16.1 us
    ppermute x4, starting transfers between devices, along(): return lax.ppermute(value, axis, [(i, (i + step) % n) for i in range(n)])  9.03 us
    all_to_all x1, blocking collectives, shards(): part = lax.all_to_all(part, 'snap', 0, 0, tiled=True)  8.89 us
    ppermute x4, waiting for transfers between devices, along(): return lax.ppermute(value, axis, [(i, (i + step) % n) for i in range(n)])  7.28 us
    ppermute x2, waiting for transfers between devices, from_both(): near = lax.ppermute(columns, 'gy', [(i, i ^ 1) for i in range(n)])  4.04 us
    ppermute x2, starting transfers between devices, from_both(): near = lax.ppermute(columns, 'gy', [(i, i ^ 1) for i in range(n)])  3.84 us
    pallas_call x1, Pallas kernels, shards(): call(functools.partial(fit_kernel, snap, scale), 'fit', [IN_SMEM] + [IN_V...  1.88 us
    ppermute x2, waiting for transfers between devices, from_both(): far = lax.ppermute(columns, 'gy', pairs + [(j, i) for i, j in pairs])  1.81 us
  transfers between devices with their start and end apart: 8, of which 7 were waited for; matrix products, arithmetic and copies ran while one was open for 1% of the time, Pallas kernels for 2%

profile of v3, /device:TPU:8, one launch (start us, length us, event | category | flops | bytes accessed | tf_op | source)
XLA Modules:
  0.0 60.1 jit_solution(15379269624966817440)
XLA Ops:
  0.6 1.2 %load.1 = (f32[192,128]{1,0:T(8,128)S(1)}, f32[768,128]{1,0:T(8,128)S(1)}, f32[240,128]{1,0:T(8,128)S(1)}, f32[240,128]{1,0:T(8,128)S(1)}, f32[192,128]{1,0:T(8,...) custom-call(f32[192,128]{1,0:T(8,128)} %bitcast.15, f32[768,128]{1,0:T(8,128)} %bitcast.12, ...), custom_call_target="tpu_custom_call" | custom-call | bytes 1048576 | tf_op jit(solution)/shard_map/load/pallas_call | solution.py:373
  1.9 0.0 collective-permute-start
  1.9 8.5 %collective-permute-start.1 = (f32[240,128]{1,0:T(8,128)S(1)}, f32[240,128]{1,0:T(8,128)S(1)}, u32[]{:S(2)}, u32[]{:S(2)}) collective-permute-start(f32[240,128]{1,0:T(8,128)S(1)} %get-tuple-element.22), channel_id=1, source_target_pairs={{0,120},{8,0},{16,8},{24,16},{32,24},{40,32},{48,40},{56,48},{64,5... | collective-permute-start | bytes 368648 | tf_op jit(solution)/shard_map/ppermute | solution.py:344
  10.4 2.5 %collective-permute-done.above = f32[240,128]{1,0:T(8,128)S(1)} collective-permute-done((f32[240,128]{1,0:T(8,128)S(1)}, f32[240,128]{1,0:T(8,128)S(1)}, u32[]{:S(2)}, u32[]{:S(2)}) %collective-permute-start) | collective-permute-done | bytes 122912 | tf_op jit(solution)/shard_map/ppermute | solution.py:344
  12.9 0.0 collective-permute-done.1.below
  12.9 0.3 columns.1
  13.2 9.0 %collective-permute-start.3 = (f32[32,128]{1,0:T(8,128)S(1)}, f32[32,128]{1,0:T(8,128)S(1)}, u32[]{:S(2)}, u32[]{:S(2)}) collective-permute-start(f32[32,128]{1,0:T(8,128)S(1)} %columns.1), channel_id=1, source_target_pairs={{1,2},{3,4},{5,6},{7,0},{2,1},{4,3},{6,5},{0,7},{9,10},{11,12},{13... | collective-permute-start | bytes 49160 | tf_op jit(solution)/shard_map/ppermute | solution.py:351
  22.2 1.9 %collective-permute-start.2 = (f32[32,128]{1,0:T(8,128)S(1)}, f32[32,128]{1,0:T(8,128)S(1)}, u32[]{:S(2)}, u32[]{:S(2)}) collective-permute-start(f32[32,128]{1,0:T(8,128)S(1)} %columns.1), channel_id=1, source_target_pairs={{0,1},{1,0},{2,3},{3,2},{4,5},{5,4},{6,7},{7,6},{8,9},{9,8},{10,11... | collective-permute-start | bytes 49160 | tf_op jit(solution)/shard_map/ppermute | solution.py:349
  24.2 0.7 %collective-permute-done.3.far = f32[32,128]{1,0:T(8,128)S(1)} collective-permute-done((f32[32,128]{1,0:T(8,128)S(1)}, f32[32,128]{1,0:T(8,128)S(1)}, u32[]{:S(2)}, u32[]{:S(2)}) %collective-permute-start.3) | collective-permute-done | bytes 16416 | tf_op jit(solution)/shard_map/ppermute | solution.py:351
  24.9 3.0 %collective-permute-done.2.near = f32[32,128]{1,0:T(8,128)S(1)} collective-permute-done((f32[32,128]{1,0:T(8,128)S(1)}, f32[32,128]{1,0:T(8,128)S(1)}, u32[]{:S(2)}, u32[]{:S(2)}) %collective-permute-start.2) | collective-permute-done | bytes 16416 | tf_op jit(solution)/shard_map/ppermute | solution.py:349
  27.9 1.6 %gram.1 = f32[256,128]{1,0:T(8,128)S(1)} custom-call(s32[1]{0:T(128)} %bitcast.par, f32[192,128]{1,0:T(8,128)S(1)} %get-tuple-element.17.disp, f32[192,128]{1,0:T(8,128)S(1)} %get-tuple-element.18.forces, s32[32,128]{1,0:T(8,128)S(1)} %get-tuple-element.19.nbr, s32[4,128]{1,0:T(4,128)S(1)} %get-tuple-element.20.group, ...), custom_call_target="tpu_custom_call" | custom-call | bytes 1048576 | tf_op jit(solution)/shard_map/gram/pallas_call | solution.py:383
  29.5 8.9 %all_to_all.11 = f32[4,64,128]{2,1,0:T(8,128)S(1)} all-to-all(f32[4,64,128]{2,1,0:T(8,128)S(1)} %bitcast.11), channel_id=1, replica_groups=mesh['snap'=4,'gx'=16,'gy'=8] {'snap'}, dimensions={0} | all-to-all | bytes 262144 | tf_op jit(solution)/shard_map/all_to_all | solution.py:390
  38.4 1.9 %fit.1 = (f32[24,128]{1,0:T(8,128)S(1)}, f32[288,128]{1,0:T(8,128)S(1)}, f32[192,128]{1,0:T(8,128)S(1)}, f32[192,128]{1,0:T(8,128)S(1)}, f32[3456,128]{1,0:T(8,128)S(1)}) custom-call(s32[1]{0:T(128)} %bitcast.par, f32[256,128]{1,0:T(8,128)S(1)} %bitcast.10, f32[288,24]{1,0:T(8,128)S(1)} %get-tuple-element.24.precond, f32[768,128]{1,0:T(8,128)S(1)} %get-tuple-element.23.vec, ...), custom_call_target="tpu_custom_call" | custom-call | bytes 1048576 | tf_op jit(solution)/shard_map/fit/pallas_call | solution.py:391
  40.3 0.5 collective-permute-start.5
  40.8 0.0 collective-permute-start.4
  40.8 0.5 middle.1
  41.3 1.7 %collective-permute-done.5.below = f32[192,128]{1,0:T(8,128)S(1)} collective-permute-done((f32[192,128]{1,0:T(8,128)S(1)}, f32[192,128]{1,0:T(8,128)S(1)}, u32[]{:S(2)}, u32[]{:S(2)}) %collective-permute-start.5) | collective-permute-done | bytes 98336 | tf_op jit(solution)/shard_map/ppermute | solution.py:344
  43.0 3.0 %collective-permute-done.4.above = f32[192,128]{1,0:T(8,128)S(1)} collective-permute-done((f32[192,128]{1,0:T(8,128)S(1)}, f32[192,128]{1,0:T(8,128)S(1)}, u32[]{:S(2)}, u32[]{:S(2)}) %collective-permute-start.4) | collective-permute-done | bytes 98336 | tf_op jit(solution)/shard_map/ppermute | solution.py:344
  46.1 0.2 term_columns.1
  46.3 7.0 %collective-permute-start.7 = (f32[24,128]{1,0:T(8,128)S(1)}, f32[24,128]{1,0:T(8,128)S(1)}, u32[]{:S(2)}, u32[]{:S(2)}) collective-permute-start(f32[24,128]{1,0:T(8,128)S(1)} %term_columns.1), channel_id=1, source_target_pairs={{1,2},{3,4},{5,6},{7,0},{2,1},{4,3},{6,5},{0,7},{9,10},{11,12},{13... | collective-permute-start | bytes 36872 | tf_op jit(solution)/shard_map/ppermute | solution.py:351
  53.3 1.9 %collective-permute-start.6 = (f32[24,128]{1,0:T(8,128)S(1)}, f32[24,128]{1,0:T(8,128)S(1)}, u32[]{:S(2)}, u32[]{:S(2)}) collective-permute-start(f32[24,128]{1,0:T(8,128)S(1)} %term_columns.1), channel_id=1, source_target_pairs={{0,1},{1,0},{2,3},{3,2},{4,5},{5,4},{6,7},{7,6},{8,9},{9,8},{10,11... | collective-permute-start | bytes 36872 | tf_op jit(solution)/shard_map/ppermute | solution.py:349
  55.3 0.6 %reshape.36 = f32[3,3,4,24]{3,2,1,0:T(4,128)} reshape(f32[36,24]{1,0:T(8,128)S(1)} %get-tuple-element.28) | data formatting | bytes 6912 | tf_op jit(solution)/shard_map/reshape | solution.py:414
  55.9 0.9 %inner.1 = f32[768,128]{1,0:T(8,128)S(1)} custom-call(f32[192,128]{1,0:T(8,128)S(1)} %get-tuple-element.29.low, f32[384,128]{1,0:T(8,128)S(1)} %get-tuple-element.30.mid, f32[192,128]{1,0:T(8,128)S(1)} %get-tuple-element.31.high, f32[192,128]{1,0:T(8,128)S(1)} %collective-permute-done.4.above, f32[192,128]{1,0:T(8,128)S(1)} %collective-permute-done.5.below, ...), custom_call_target="tpu_custom_call" | custom-call | flops 33554432 | bytes 1048576 | tf_op jit(solution)/shard_map/inner/pallas_call | solution.py:407
  56.8 1.1 %collective-permute-done.7.far = f32[24,128]{1,0:T(8,128)S(1)} collective-permute-done((f32[24,128]{1,0:T(8,128)S(1)}, f32[24,128]{1,0:T(8,128)S(1)}, u32[]{:S(2)}, u32[]{:S(2)}) %collective-permute-start.7) | collective-permute-done | bytes 12320 | tf_op jit(solution)/shard_map/ppermute | solution.py:351
  57.9 1.0 %collective-permute-done.6.near = f32[24,128]{1,0:T(8,128)S(1)} collective-permute-done((f32[24,128]{1,0:T(8,128)S(1)}, f32[24,128]{1,0:T(8,128)S(1)}, u32[]{:S(2)}, u32[]{:S(2)}) %collective-permute-start.6) | collective-permute-done | bytes 12320 | tf_op jit(solution)/shard_map/ppermute | solution.py:349
  58.9 1.2 %outer.1 = f32[768,128]{1,0:T(8,128)} custom-call(s32[1]{0:T(128)} %bitcast.par, f32[768,128]{1,0:T(8,128)S(1)} %inner.1, f32[24,128]{1,0:T(8,128)S(1)} %collective-permute-done.6.near, f32[24,128]{1,0:T(8,128)S(1)} %collective-permute-done.7.far, f32[288,128]{1,0:T(8,128)S(1)} %get-tuple-element.26.weights), custom_call_target="tpu_custom_call" | custom-call | bytes 1048576 | tf_op jit(solution)/shard_map/outer/pallas_call | solution.py:410
Async XLA Ops:
  1.9 11.1 %collective-permute-start = (f32[240,128]{1,0:T(8,128)S(1)}, f32[240,128]{1,0:T(8,128)S(1)}, u32[]{:S(2)}, u32[]{:S(2)}) collective-permute-start(f32[240,128]{1,0:T(8,128)S(1)} %get-tuple-element.21), channel_id=1, source_target_pairs={{0,8},{8,16},{16,24},{24,32},{32,40},{40,48},{48,56},{56,64},{64,7... | collective-permute-start | bytes 368648 | tf_op jit(solution)/shard_map/ppermute | solution.py:344
  1.9 11.0 %collective-permute-start.1 = (f32[240,128]{1,0:T(8,128)S(1)}, f32[240,128]{1,0:T(8,128)S(1)}, u32[]{:S(2)}, u32[]{:S(2)}) collective-permute-start(f32[240,128]{1,0:T(8,128)S(1)} %get-tuple-element.22), channel_id=1, source_target_pairs={{0,120},{8,0},{16,8},{24,16},{32,24},{40,32},{48,40},{56,48},{64,5... | collective-permute-start | bytes 368648 | tf_op jit(solution)/shard_map/ppermute | solution.py:344
  13.2 11.6 %collective-permute-start.3 = (f32[32,128]{1,0:T(8,128)S(1)}, f32[32,128]{1,0:T(8,128)S(1)}, u32[]{:S(2)}, u32[]{:S(2)}) collective-permute-start(f32[32,128]{1,0:T(8,128)S(1)} %columns.1), channel_id=1, source_target_pairs={{1,2},{3,4},{5,6},{7,0},{2,1},{4,3},{6,5},{0,7},{9,10},{11,12},{13... | collective-permute-start | bytes 49160 | tf_op jit(solution)/shard_map/ppermute | solution.py:351
  22.2 5.6 %collective-permute-start.2 = (f32[32,128]{1,0:T(8,128)S(1)}, f32[32,128]{1,0:T(8,128)S(1)}, u32[]{:S(2)}, u32[]{:S(2)}) collective-permute-start(f32[32,128]{1,0:T(8,128)S(1)} %columns.1), channel_id=1, source_target_pairs={{0,1},{1,0},{2,3},{3,2},{4,5},{5,4},{6,7},{7,6},{8,9},{9,8},{10,11... | collective-permute-start | bytes 49160 | tf_op jit(solution)/shard_map/ppermute | solution.py:349
  40.3 2.7 %collective-permute-start.5 = (f32[192,128]{1,0:T(8,128)S(1)}, f32[192,128]{1,0:T(8,128)S(1)}, u32[]{:S(2)}, u32[]{:S(2)}) collective-permute-start(f32[192,128]{1,0:T(8,128)S(1)} %get-tuple-element.29.low), channel_id=1, source_target_pairs={{0,120},{8,0},{16,8},{24,16},{32,24},{40,32},{48,40},{56,48},{64,5... | collective-permute-start | bytes 294920 | tf_op jit(solution)/shard_map/ppermute | solution.py:344
  40.8 5.3 %collective-permute-start.4 = (f32[192,128]{1,0:T(8,128)S(1)}, f32[192,128]{1,0:T(8,128)S(1)}, u32[]{:S(2)}, u32[]{:S(2)}) collective-permute-start(f32[192,128]{1,0:T(8,128)S(1)} %get-tuple-element.31.high), channel_id=1, source_target_pairs={{0,8},{8,16},{16,24},{24,32},{32,40},{40,48},{48,56},{56,64},{64,7... | collective-permute-start | bytes 294920 | tf_op jit(solution)/shard_map/ppermute | solution.py:344
  46.3 11.6 %collective-permute-start.7 = (f32[24,128]{1,0:T(8,128)S(1)}, f32[24,128]{1,0:T(8,128)S(1)}, u32[]{:S(2)}, u32[]{:S(2)}) collective-permute-start(f32[24,128]{1,0:T(8,128)S(1)} %term_columns.1), channel_id=1, source_target_pairs={{1,2},{3,4},{5,6},{7,0},{2,1},{4,3},{6,5},{0,7},{9,10},{11,12},{13... | collective-permute-start | bytes 36872 | tf_op jit(solution)/shard_map/ppermute | solution.py:351
  53.3 5.6 %collective-permute-start.6 = (f32[24,128]{1,0:T(8,128)S(1)}, f32[24,128]{1,0:T(8,128)S(1)}, u32[]{:S(2)}, u32[]{:S(2)}) collective-permute-start(f32[24,128]{1,0:T(8,128)S(1)} %term_columns.1), channel_id=1, source_target_pairs={{0,1},{1,0},{2,3},{3,2},{4,5},{5,4},{6,7},{7,6},{8,9},{9,8},{10,11... | collective-permute-start | bytes 36872 | tf_op jit(solution)/shard_map/ppermute | solution.py:349

commit v4 on v3

--- a/solution.py
+++ b/solution.py
@@ -66,23 +66,36 @@
             shift_ref[pl.ds(36 * height + base, 8), :] = jnp.where(lane == 127, outside, pltpu.roll(values, 127, 1))
 
 
+def rows_kernel(disp, vec, low, high, sems):
+    copies = []
+    for out, x in ((low, 0), (high, 3)):
+        for source, at in ((disp, pl.ds(0, 48)), (vec, pl.ds(48, 192))):
+            copies.append(pltpu.make_async_copy(source.at[:, x, :], out.at[at, :], sems.at[len(copies)]))
+    for copy in copies:
+        copy.start()
+    for copy in copies:
+        copy.wait()
+
+
 def load_kernel(
     disp_in, vec_in, load_in, nbr_in, species, block_of, precond_in,
-    disp, vec, low, high, load, nbr, group, precond, kind, block, sems,
+    disp, vec, load, nbr, group, precond, masks, members, kind, block, sems,
 ):
     pairs = [(disp_in, disp), (vec_in, vec), (species, kind), (block_of, block), (load_in, load), (nbr_in, nbr)]
     pairs.append((precond_in, precond))
     copies = [pltpu.make_async_copy(source, out, sems.at[i]) for i, (source, out) in enumerate(pairs)]
     for copy in copies:
         copy.start()
-    copies[0].wait()
-    copies[1].wait()
-    for out, x in ((low, 0), (high, 3)):
-        out[pl.ds(0, 48), :] = disp[pl.ds(x, 48, stride=4), :]
-        out[pl.ds(48, 192), :] = vec[pl.ds(x, 192, stride=4), :]
-    for copy in copies[2:]:
+    for copy in copies:
         copy.wait()
     group[...] = block[...] * NSPEC + kind[...]
+    which = subs_of((128, 128)) & 15
+    p_row, o_col = subs_of((NP, 8)), lanes_of((NP, 8))
+    repeat = ((p_row >= 3 * o_col) & (p_row < 3 * o_col + 3)).astype(jnp.bfloat16)
+    for x in range(4):
+        mask = nbr[pl.ds(x, 8, stride=4), :].astype(F32).astype(jnp.bfloat16)
+        masks[pl.ds(NP * x, NP), :] = jnp.dot(repeat, mask, preferred_element_type=F32)
+        members[:, pl.ds(128 * x, 128)] = (which == group[pl.ds(x, 1), :]).astype(F32).astype(jnp.bfloat16)
 
 
 def natural_tile(source, above, below, base):
@@ -205,7 +218,7 @@
 
 
 def fit_kernel(
-    copies, scale, par, sums, precond, vec, nbr, group, above, below, near, far,
+    copies, scale, par, sums, precond, vec, masks, members, above, below, near, far,
     theta, weights, low_out, high_out, shift,
 ):
     sub, eighth = subs_of((8, 128)), lanes_of((8, 128)) // 16
@@ -255,15 +268,15 @@
     stacked = jnp.concatenate(
         [jnp.where((of_part == a) & (of_group < NG), fitted, 0.0) for a in range(3)], axis=0
     )
-    which = subs_of((128, 128)) & 15
-    p_row, o_col = subs_of((NP, 8)), lanes_of((NP, 8))
-    repeat = ((p_row >= 3 * o_col) & (p_row < 3 * o_col + 3)).astype(F32)
+    by_atom = None
+    for _ in range(3):
+        piece = stacked.astype(jnp.bfloat16)
+        stacked = stacked - piece.astype(F32)
+        term = jnp.dot(piece, members[...], preferred_element_type=F32)
+        by_atom = term if by_atom is None else by_atom + term
     for x in range(4):
-        member = (which == group[pl.ds(x, 1), :]).astype(F32)
-        by_atom = jnp.dot(stacked, member, precision=HIGH, preferred_element_type=F32)
-        mask = nbr[pl.ds(x, 8, stride=4), :].astype(F32)
-        mask = jnp.dot(repeat, mask, precision=HIGH, preferred_element_type=F32)
-        weights[pl.ds(72 * x, 72), :] = by_atom * jnp.concatenate([mask, mask, mask], axis=0)
+        mask = masks[pl.ds(NP * x, NP), :]
+        weights[pl.ds(72 * x, 72), :] = by_atom[:, 128 * x : 128 * x + 128] * jnp.concatenate([mask] * 3, axis=0)
 
     tile = natural_tile(vec, above, below, 48)
     edge = edge_tiles(par[0] == 0, range(2, 10), far, near)
@@ -284,9 +297,11 @@
     which = row >> 2
     kind = (which >= 3).astype(jnp.int32) + (which >= 6).astype(jnp.int32)
     pick = (lane == 16 * (which - 3 * kind) + 3 * (row & 3) + kind).astype(F32)
-    constants[...] = lax.dot_general(
+    picked = lax.dot_general(
         pick, theta[...], (((1,), (1,)), ((), ())), precision=HIGH, preferred_element_type=F32
     )
+    for i in range(9):
+        constants[i] = picked[4 * i : 4 * i + 4]
 
 
 def inner_kernel(low, mid, high, above, below, weights, vec, out, shift):
@@ -299,25 +314,32 @@
     apply_operator(shift, weights, range(4), emit)
 
 
-def outer_kernel(par, inner, near, far, weights, out, edges):
+def outer_kernel(par, inner, near, far, weights, out, edges, result, sems):
     edge = edge_tiles(par[0] == 0, range(8), far, near)
-    for k in range(18):
-        for slot in range(8):
-            edges[pl.ds(64 * k + 8 * slot, 8), :] = edge(slot, k)
     lane = lanes_of((1, 128))
-    for x in range(4):
-        total = [inner[pl.ds((4 * a + x) * 64, 64), :] for a in range(3)]
-        for b in range(3):
-            for dx in (-1, 0, 1):
-                outside = edges[pl.ds(64 * (6 * b + x + dx + 1), 64), :]
-                for a in range(3):
-                    base = 72 * x + 24 * a + b
-                    left = weights[pl.ds(base + 3 * OFFSETS.index((dx, -1)), 1), :]
-                    right = weights[pl.ds(base + 3 * OFFSETS.index((dx, 1)), 1), :]
-                    weight = jnp.where(lane == 0, 2.0 * left, jnp.where(lane == 127, 2.0 * right, 0.0))
-                    total[a] = total[a] - outside * weight
-        for a in range(3):
-            out[pl.ds(4 * a + x, 64, stride=12), :] = total[a]
+    copies = []
+    for half in range(2):
+        for k in range(18):
+            for slot in range(4 * half, 4 * half + 4):
+                edges[pl.ds(64 * k + 8 * slot, 8), :] = edge(slot, k)
+        for x in range(4):
+            total = [inner[pl.ds((4 * a + x) * 64 + 32 * half, 32), :] for a in range(3)]
+            for b in range(3):
+                for dx in (-1, 0, 1):
+                    outside = edges[pl.ds(64 * (6 * b + x + dx + 1) + 32 * half, 32), :]
+                    for a in range(3):
+                        base = 72 * x + 24 * a + b
+                        left = weights[pl.ds(base + 3 * OFFSETS.index((dx, -1)), 1), :]
+                        right = weights[pl.ds(base + 3 * OFFSETS.index((dx, 1)), 1), :]
+                        weight = jnp.where(lane == 0, 2.0 * left, jnp.where(lane == 127, 2.0 * right, 0.0))
+                        total[a] = total[a] - outside * weight
+            for a in range(3):
+                result[pl.ds(384 * half + 4 * a + x, 32, stride=12), :] = total[a]
+        rows = pl.ds(384 * half, 384)
+        copies.append(pltpu.make_async_copy(result.at[rows, :], out.at[rows, :], sems.at[half]))
+        copies[half].start()
+    for copy in copies:
+        copy.wait()
 
 
 IN_SMEM = pl.BlockSpec(memory_space=pltpu.SMEM)
@@ -325,13 +347,13 @@
 IN_HBM = pl.BlockSpec(memory_space=pltpu.HBM)
 
 
-def call(kernel, name, ins, outs, scratch=(), flops=0):
+def call(kernel, name, ins, outs, scratch=(), flops=0, out_spec=IN_VMEM):
     outs = [jax.ShapeDtypeStruct((rows, 128), F32) if isinstance(rows, int) else rows for rows in outs]
     return pl.pallas_call(
         kernel,
         name=name,
         in_specs=ins,
-        out_specs=[IN_VMEM] * len(outs),
+        out_specs=[out_spec] * len(outs),
         out_shape=outs,
         scratch_shapes=[pltpu.VMEM((rows, 128), F32) if isinstance(rows, int) else rows for rows in scratch],
         compiler_params=pltpu.CompilerParams(vmem_limit_bytes=40 << 20),
@@ -357,9 +379,32 @@
     scale = 1.0 / (displacements.shape[0] * snap * AB)
     par = (lax.axis_index("gy") % 2).astype(jnp.int32).reshape(1)
 
-    whole = [
-        pltpu.with_memory_space_constraint(value, pltpu.HBM)
-        for value in (
+    def in_hbm(*values):
+        return [pltpu.with_memory_space_constraint(value, pltpu.HBM) for value in values]
+
+    low, high = call(rows_kernel, "rows", [IN_HBM] * 2, (240, 240), (pltpu.SemaphoreType.DMA((4,)),))(
+        *in_hbm(displacements.reshape(-1, 4, 128), vectors.reshape(-1, 4, 128))
+    )
+    above, below = along(high, "gx", 1), along(low, "gx", -1)
+    tile = jax.ShapeDtypeStruct((4, 128), jnp.int32)
+    disp, vec, load, nbr, group, inverses, masks, members = call(
+        load_kernel,
+        "load",
+        [IN_HBM] * 7,
+        (
+            192,
+            768,
+            192,
+            jax.ShapeDtypeStruct((32, 128), jnp.int32),
+            tile,
+            jax.ShapeDtypeStruct((NG * NP, NP), F32),
+            4 * NP,
+            jax.ShapeDtypeStruct((128, 512), jnp.bfloat16),
+        ),
+        (pltpu.VMEM((4, 128), jnp.int32), pltpu.VMEM((4, 128), jnp.int32), pltpu.SemaphoreType.DMA((7,))),
+        flops=1 << 24,
+    )(
+        *in_hbm(
             displacements.reshape(-1, 128),
             vectors.reshape(-1, 128),
             forces.reshape(-1, 128),
@@ -368,16 +413,7 @@
             block_of,
             precond.reshape(NG * NP, NP),
         )
-    ]
-    tile = jax.ShapeDtypeStruct((4, 128), jnp.int32)
-    disp, vec, low, high, load, nbr, group, inverses = call(
-        load_kernel,
-        "load",
-        [IN_HBM] * 7,
-        (192, 768, 240, 240, 192, jax.ShapeDtypeStruct((32, 128), jnp.int32), tile, jax.ShapeDtypeStruct((NG * NP, NP), F32)),
-        (pltpu.VMEM((4, 128), jnp.int32), pltpu.VMEM((4, 128), jnp.int32), pltpu.SemaphoreType.DMA((7,))),
-    )(*whole)
-    above, below = along(high, "gx", 1), along(low, "gx", -1)
+    )
     (columns,) = call(columns_kernel, "columns", [IN_VMEM] * 4, (32,))(disp, vec, above, below)
     near, far = from_both(columns)
     (part,) = call(
@@ -393,13 +429,13 @@
         "fit",
         [IN_SMEM] + [IN_VMEM] * 9,
         (NP, 288, 192, 192, 54 * 64),
-    )(par, part, inverses, vec, nbr, group, above, below, near, far)
+    )(par, part, inverses, vec, masks, members, above, below, near, far)
     above, below = along(high, "gx", 1), along(low, "gx", -1)
     mid, constants = call(
         middle_kernel,
         "middle",
         [IN_VMEM] * 3,
-        (384, jax.ShapeDtypeStruct((3 * NG, NP), F32)),
+        (384, jax.ShapeDtypeStruct((9, 4, NP), F32)),
         flops=1 << 24,
     )(shift, weights, theta)
     (columns,) = call(term_columns_kernel, "term_columns", [IN_VMEM] * 5, (24,))(low, mid, high, above, below)
@@ -407,7 +443,14 @@
     (inner,) = call(inner_kernel, "inner", [IN_VMEM] * 7, (768,), (54 * 64,), flops=1 << 25)(
         low, mid, high, above, below, weights, vec
     )
-    (result,) = call(outer_kernel, "outer", [IN_SMEM] + [IN_VMEM] * 4, (768,), (18 * 64,))(
+    (result,) = call(
+        outer_kernel,
+        "outer",
+        [IN_SMEM] + [IN_VMEM] * 4,
+        (768,),
+        (18 * 64, 768, pltpu.SemaphoreType.DMA((2,))),
+        out_spec=IN_HBM,
+    )(
         par, inner, near, far, weights
     )
 

time: 60.4 us -> 59.8 us (0.990)
  Pallas kernels: 7.84 us -> 9.27 us
  waiting for transfers between devices: 13.1 us -> 11.7 us
  local copies, waits for them, and re-layouts: 0.62 us -> 0 us
    ppermute x4, waiting for transfers between devices: 7.28 us -> 5.24 us  [along(): return lax.ppermute(value, axis, [(i, (i + step) % n) for i in range(n)])]
    pallas_call x2 -> x3, Pallas kernels: 2.45 us -> 3.59 us  [the longest x1 1.39 us: shards(): call(load_kernel, 'load', [IN_HBM] * 7, (192, 768, 192, jax.ShapeDtypeStr...]
    pallas_call x1, Pallas kernels: 0.5 us -> 1.14 us  [shards(): call(middle_kernel, 'middle', [IN_VMEM] * 3, (384, jax.ShapeDtypeStruct((...]
    reshape x1 -> x0, local copies, waits for them, and re-layouts: 0.62 us -> none  [shards(): constants.reshape(NSPEC, 3, precond.shape[0], NP).transpose(2, 0, 3, 1)]
    ppermute x2, waiting for transfers between devices: 1.81 us -> 2.41 us  [from_both(): far = lax.ppermute(columns, 'gy', pairs + [(j, i) for i, j in pairs])]
  transfers between devices with their start and end apart: 8 -> 8, of which waited for: 7 -> 7; matrix products, arithmetic and copies ran while one was open for 1% -> 0% of each run, Pallas kernels for 2% -> 6%
where the time goes in v4:
time: 59.8 us; the launch traced here: 59.5 us
  starting transfers between devices  28.9 us (48%)
  waiting for transfers between devices  11.7 us (20%)
  Pallas kernels  9.27 us (16%)
  blocking collectives  8.89 us (15%)
  between operations  0.73 us (1%)
    ppermute x2, starting transfers between devices, from_both(): far = lax.ppermute(columns, 'gy', pairs + [(j, i) for i, j in pairs])  16.1 us
    ppermute x4, starting transfers between devices, along(): return lax.ppermute(value, axis, [(i, (i + step) % n) for i in range(n)])  9.03 us
    all_to_all x1, blocking collectives, shards(): part = lax.all_to_all(part, 'snap', 0, 0, tiled=True)  8.89 us
    ppermute x4, waiting for transfers between devices, along(): return lax.ppermute(value, axis, [(i, (i + step) % n) for i in range(n)])  5.24 us
    ppermute x2, waiting for transfers between devices, from_both(): near = lax.ppermute(columns, 'gy', [(i, i ^ 1) for i in range(n)])  4.04 us
    ppermute x2, starting transfers between devices, from_both(): near = lax.ppermute(columns, 'gy', [(i, i ^ 1) for i in range(n)])  3.84 us
    ppermute x2, waiting for transfers between devices, from_both(): far = lax.ppermute(columns, 'gy', pairs + [(j, i) for i, j in pairs])  2.41 us
    pallas_call x1, Pallas kernels, shards(): call(functools.partial(gram_kernel, snap), 'gram', [IN_SMEM] + [IN_VMEM]...  1.65 us
  transfers between devices with their start and end apart: 8, of which 7 were waited for; matrix products, arithmetic and copies ran while one was open for 0% of the time, Pallas kernels for 6%

profile of v4, /device:TPU:8, one launch (start us, length us, event | category | flops | bytes accessed | tf_op | source)
XLA Modules:
  0.0 59.5 jit_solution(131605795598750908)
XLA Ops:
  0.6 1.0 %rows.1 = (f32[240,128]{1,0:T(8,128)S(1)}, f32[240,128]{1,0:T(8,128)S(1)}) custom-call(f32[48,4,128]{2,1,0:T(4,128)} %bitcast.19, f32[192,4,128]{2,1,0:T(4,128)} %bitcast.16), custom_call_target="tpu_custom_call" | custom-call | bytes 1048576 | tf_op jit(solution)/shard_map/rows/pallas_call | solution.py:385
  1.6 0.0 collective-permute-start
  1.7 8.5 %collective-permute-start.1 = (f32[240,128]{1,0:T(8,128)S(1)}, f32[240,128]{1,0:T(8,128)S(1)}, u32[]{:S(2)}, u32[]{:S(2)}) collective-permute-start(f32[240,128]{1,0:T(8,128)S(1)} %get-tuple-element.24), channel_id=1, source_target_pairs={{0,120},{8,0},{16,8},{24,16},{32,24},{40,32},{48,40},{56,48},{64,5... | collective-permute-start | bytes 368648 | tf_op jit(solution)/shard_map/ppermute | solution.py:366
  10.2 1.4 %load.1 = (f32[192,128]{1,0:T(8,128)S(1)}, f32[768,128]{1,0:T(8,128)S(1)}, f32[192,128]{1,0:T(8,128)S(1)}, s32[32,128]{1,0:T(8,128)S(1)}, s32[4,128]{1,0:T(4,128...) custom-call(f32[192,128]{1,0:T(8,128)} %bitcast.20, f32[768,128]{1,0:T(8,128)} %bitcast.17, ...), custom_call_target="tpu_custom_call" | custom-call | flops 16777216 | bytes 1048576 | tf_op jit(solution)/shard_map/load/pallas_call | solution.py:390
  11.6 1.1 %collective-permute-done.above = f32[240,128]{1,0:T(8,128)S(1)} collective-permute-done((f32[240,128]{1,0:T(8,128)S(1)}, f32[240,128]{1,0:T(8,128)S(1)}, u32[]{:S(2)}, u32[]{:S(2)}) %collective-permute-start) | collective-permute-done | bytes 122912 | tf_op jit(solution)/shard_map/ppermute | solution.py:366
  12.7 0.0 collective-permute-done.1.below
  12.7 0.3 columns.1
  13.0 9.0 %collective-permute-start.3 = (f32[32,128]{1,0:T(8,128)S(1)}, f32[32,128]{1,0:T(8,128)S(1)}, u32[]{:S(2)}, u32[]{:S(2)}) collective-permute-start(f32[32,128]{1,0:T(8,128)S(1)} %columns.1), channel_id=1, source_target_pairs={{1,2},{3,4},{5,6},{7,0},{2,1},{4,3},{6,5},{0,7},{9,10},{11,12},{13... | collective-permute-start | bytes 49160 | tf_op jit(solution)/shard_map/ppermute | solution.py:373
  22.0 1.9 %collective-permute-start.2 = (f32[32,128]{1,0:T(8,128)S(1)}, f32[32,128]{1,0:T(8,128)S(1)}, u32[]{:S(2)}, u32[]{:S(2)}) collective-permute-start(f32[32,128]{1,0:T(8,128)S(1)} %columns.1), channel_id=1, source_target_pairs={{0,1},{1,0},{2,3},{3,2},{4,5},{5,4},{6,7},{7,6},{8,9},{9,8},{10,11... | collective-permute-start | bytes 49160 | tf_op jit(solution)/shard_map/ppermute | solution.py:371
  23.9 0.7 %collective-permute-done.3.far = f32[32,128]{1,0:T(8,128)S(1)} collective-permute-done((f32[32,128]{1,0:T(8,128)S(1)}, f32[32,128]{1,0:T(8,128)S(1)}, u32[]{:S(2)}, u32[]{:S(2)}) %collective-permute-start.3) | collective-permute-done | bytes 16416 | tf_op jit(solution)/shard_map/ppermute | solution.py:373
  24.6 3.0 %collective-permute-done.2.near = f32[32,128]{1,0:T(8,128)S(1)} collective-permute-done((f32[32,128]{1,0:T(8,128)S(1)}, f32[32,128]{1,0:T(8,128)S(1)}, u32[]{:S(2)}, u32[]{:S(2)}) %collective-permute-start.2) | collective-permute-done | bytes 16416 | tf_op jit(solution)/shard_map/ppermute | solution.py:371
  27.6 1.6 %gram.1 = f32[256,128]{1,0:T(8,128)S(1)} custom-call(s32[1]{0:T(128)} %bitcast.par, f32[192,128]{1,0:T(8,128)S(1)} %get-tuple-element.19.disp, f32[192,128]{1,0:T(8,128)S(1)} %get-tuple-element.20.forces, s32[32,128]{1,0:T(8,128)S(1)} %get-tuple-element.21.nbr, s32[4,128]{1,0:T(4,128)S(1)} %get-tuple-element.22.group, ...), custom_call_target="tpu_custom_call" | custom-call | bytes 1048576 | tf_op jit(solution)/shard_map/gram/pallas_call | solution.py:419
  29.3 8.9 %all_to_all.11 = f32[4,64,128]{2,1,0:T(8,128)S(1)} all-to-all(f32[4,64,128]{2,1,0:T(8,128)S(1)} %bitcast.14), channel_id=1, replica_groups=mesh['snap'=4,'gx'=16,'gy'=8] {'snap'}, dimensions={0} | all-to-all | bytes 262144 | tf_op jit(solution)/shard_map/all_to_all | solution.py:426
  38.2 1.5 %fit.1 = (f32[24,128]{1,0:T(8,128)S(1)}, f32[288,128]{1,0:T(8,128)S(1)}, f32[192,128]{1,0:T(8,128)S(1)}, f32[192,128]{1,0:T(8,128)S(1)}, f32[3456,128]{1,0:T(8,128)S(1)}) custom-call(s32[1]{0:T(128)} %bitcast.par, f32[256,128]{1,0:T(8,128)S(1)} %bitcast.15, f32[288,24]{1,0:T(8,128)S(1)} %get-tuple-element.26.precond, f32[768,128]{1,0:T(8,128)S(1)} %get-tuple-element.25.vec, ...), custom_call_target="tpu_custom_call" | custom-call | bytes 1048576 | tf_op jit(solution)/shard_map/fit/pallas_call | solution.py:427
  39.7 0.5 collective-permute-start.5
  40.2 0.0 collective-permute-start.4
  40.2 1.1 %middle.1 = (f32[384,128]{1,0:T(8,128)S(1)}, f32[9,4,24]{2,1,0:T(4,128)}) custom-call(f32[3456,128]{1,0:T(8,128)S(1)} %get-tuple-element.29.shift, f32[288,128]{1,0:T(8,128)S(1)} %get-tuple-element.30.weights, f32[24,128]{1,0:T(8,128)S(1)} %get-tuple-element.31.theta), custom_call_target="tpu_custom_call" | custom-call | flops 16777216 | bytes 1048576 | tf_op jit(solution)/shard_map/middle/pallas_call | solution.py:434
  41.4 1.1 %collective-permute-done.5.below = f32[192,128]{1,0:T(8,128)S(1)} collective-permute-done((f32[192,128]{1,0:T(8,128)S(1)}, f32[192,128]{1,0:T(8,128)S(1)}, u32[]{:S(2)}, u32[]{:S(2)}) %collective-permute-start.5) | collective-permute-done | bytes 98336 | tf_op jit(solution)/shard_map/ppermute | solution.py:366
  42.4 3.0 %collective-permute-done.4.above = f32[192,128]{1,0:T(8,128)S(1)} collective-permute-done((f32[192,128]{1,0:T(8,128)S(1)}, f32[192,128]{1,0:T(8,128)S(1)}, u32[]{:S(2)}, u32[]{:S(2)}) %collective-permute-start.4) | collective-permute-done | bytes 98336 | tf_op jit(solution)/shard_map/ppermute | solution.py:366
  45.5 0.2 term_columns.1
  45.7 7.0 %collective-permute-start.7 = (f32[24,128]{1,0:T(8,128)S(1)}, f32[24,128]{1,0:T(8,128)S(1)}, u32[]{:S(2)}, u32[]{:S(2)}) collective-permute-start(f32[24,128]{1,0:T(8,128)S(1)} %term_columns.1), channel_id=1, source_target_pairs={{1,2},{3,4},{5,6},{7,0},{2,1},{4,3},{6,5},{0,7},{9,10},{11,12},{13... | collective-permute-start | bytes 36872 | tf_op jit(solution)/shard_map/ppermute | solution.py:373
  52.7 1.9 %collective-permute-start.6 = (f32[24,128]{1,0:T(8,128)S(1)}, f32[24,128]{1,0:T(8,128)S(1)}, u32[]{:S(2)}, u32[]{:S(2)}) collective-permute-start(f32[24,128]{1,0:T(8,128)S(1)} %term_columns.1), channel_id=1, source_target_pairs={{0,1},{1,0},{2,3},{3,2},{4,5},{5,4},{6,7},{7,6},{8,9},{9,8},{10,11... | collective-permute-start | bytes 36872 | tf_op jit(solution)/shard_map/ppermute | solution.py:371
  54.7 0.9 %inner.1 = f32[768,128]{1,0:T(8,128)S(1)} custom-call(f32[192,128]{1,0:T(8,128)S(1)} %get-tuple-element.33.low, f32[384,128]{1,0:T(8,128)S(1)} %get-tuple-element.34.mid, f32[192,128]{1,0:T(8,128)S(1)} %get-tuple-element.35.high, f32[192,128]{1,0:T(8,128)S(1)} %collective-permute-done.4.above, f32[192,128]{1,0:T(8,128)S(1)} %collective-permute-done.5.below, ...), custom_call_target="tpu_custom_call" | custom-call | flops 33554432 | bytes 1048576 | tf_op jit(solution)/shard_map/inner/pallas_call | solution.py:443
  55.6 1.7 %collective-permute-done.7.far = f32[24,128]{1,0:T(8,128)S(1)} collective-permute-done((f32[24,128]{1,0:T(8,128)S(1)}, f32[24,128]{1,0:T(8,128)S(1)}, u32[]{:S(2)}, u32[]{:S(2)}) %collective-permute-start.7) | collective-permute-done | bytes 12320 | tf_op jit(solution)/shard_map/ppermute | solution.py:373
  57.3 1.0 %collective-permute-done.6.near = f32[24,128]{1,0:T(8,128)S(1)} collective-permute-done((f32[24,128]{1,0:T(8,128)S(1)}, f32[24,128]{1,0:T(8,128)S(1)}, u32[]{:S(2)}, u32[]{:S(2)}) %collective-permute-start.6) | collective-permute-done | bytes 12320 | tf_op jit(solution)/shard_map/ppermute | solution.py:371
  58.3 1.2 %outer.1 = f32[768,128]{1,0:T(8,128)} custom-call(s32[1]{0:T(128)} %bitcast.par, f32[768,128]{1,0:T(8,128)S(1)} %inner.1, f32[24,128]{1,0:T(8,128)S(1)} %collective-permute-done.6.near, f32[24,128]{1,0:T(8,128)S(1)} %collective-permute-done.7.far, f32[288,128]{1,0:T(8,128)S(1)} %get-tuple-element.30.weights), custom_call_target="tpu_custom_call" | custom-call | bytes 1048576 | tf_op jit(solution)/shard_map/outer/pallas_call | solution.py:446
Async XLA Ops:
  1.6 11.1 %collective-permute-start = (f32[240,128]{1,0:T(8,128)S(1)}, f32[240,128]{1,0:T(8,128)S(1)}, u32[]{:S(2)}, u32[]{:S(2)}) collective-permute-start(f32[240,128]{1,0:T(8,128)S(1)} %get-tuple-element.23), channel_id=1, source_target_pairs={{0,8},{8,16},{16,24},{24,32},{32,40},{40,48},{48,56},{56,64},{64,7... | collective-permute-start | bytes 368648 | tf_op jit(solution)/shard_map/ppermute | solution.py:366
  1.7 11.0 %collective-permute-start.1 = (f32[240,128]{1,0:T(8,128)S(1)}, f32[240,128]{1,0:T(8,128)S(1)}, u32[]{:S(2)}, u32[]{:S(2)}) collective-permute-start(f32[240,128]{1,0:T(8,128)S(1)} %get-tuple-element.24), channel_id=1, source_target_pairs={{0,120},{8,0},{16,8},{24,16},{32,24},{40,32},{48,40},{56,48},{64,5... | collective-permute-start | bytes 368648 | tf_op jit(solution)/shard_map/ppermute | solution.py:366
  13.0 11.6 %collective-permute-start.3 = (f32[32,128]{1,0:T(8,128)S(1)}, f32[32,128]{1,0:T(8,128)S(1)}, u32[]{:S(2)}, u32[]{:S(2)}) collective-permute-start(f32[32,128]{1,0:T(8,128)S(1)} %columns.1), channel_id=1, source_target_pairs={{1,2},{3,4},{5,6},{7,0},{2,1},{4,3},{6,5},{0,7},{9,10},{11,12},{13... | collective-permute-start | bytes 49160 | tf_op jit(solution)/shard_map/ppermute | solution.py:373
  22.0 5.6 %collective-permute-start.2 = (f32[32,128]{1,0:T(8,128)S(1)}, f32[32,128]{1,0:T(8,128)S(1)}, u32[]{:S(2)}, u32[]{:S(2)}) collective-permute-start(f32[32,128]{1,0:T(8,128)S(1)} %columns.1), channel_id=1, source_target_pairs={{0,1},{1,0},{2,3},{3,2},{4,5},{5,4},{6,7},{7,6},{8,9},{9,8},{10,11... | collective-permute-start | bytes 49160 | tf_op jit(solution)/shard_map/ppermute | solution.py:371
  39.7 2.7 %collective-permute-start.5 = (f32[192,128]{1,0:T(8,128)S(1)}, f32[192,128]{1,0:T(8,128)S(1)}, u32[]{:S(2)}, u32[]{:S(2)}) collective-permute-start(f32[192,128]{1,0:T(8,128)S(1)} %get-tuple-element.33.low), channel_id=1, source_target_pairs={{0,120},{8,0},{16,8},{24,16},{32,24},{40,32},{48,40},{56,48},{64,5... | collective-permute-start | bytes 294920 | tf_op jit(solution)/shard_map/ppermute | solution.py:366
  40.2 5.3 %collective-permute-start.4 = (f32[192,128]{1,0:T(8,128)S(1)}, f32[192,128]{1,0:T(8,128)S(1)}, u32[]{:S(2)}, u32[]{:S(2)}) collective-permute-start(f32[192,128]{1,0:T(8,128)S(1)} %get-tuple-element.35.high), channel_id=1, source_target_pairs={{0,8},{8,16},{16,24},{24,32},{32,40},{40,48},{48,56},{56,64},{64,7... | collective-permute-start | bytes 294920 | tf_op jit(solution)/shard_map/ppermute | solution.py:366
  45.7 11.6 %collective-permute-start.7 = (f32[24,128]{1,0:T(8,128)S(1)}, f32[24,128]{1,0:T(8,128)S(1)}, u32[]{:S(2)}, u32[]{:S(2)}) collective-permute-start(f32[24,128]{1,0:T(8,128)S(1)} %term_columns.1), channel_id=1, source_target_pairs={{1,2},{3,4},{5,6},{7,0},{2,1},{4,3},{6,5},{0,7},{9,10},{11,12},{13... | collective-permute-start | bytes 36872 | tf_op jit(solution)/shard_map/ppermute | solution.py:373
  52.7 5.6 %collective-permute-start.6 = (f32[24,128]{1,0:T(8,128)S(1)}, f32[24,128]{1,0:T(8,128)S(1)}, u32[]{:S(2)}, u32[]{:S(2)}) collective-permute-start(f32[24,128]{1,0:T(8,128)S(1)} %term_columns.1), channel_id=1, source_target_pairs={{0,1},{1,0},{2,3},{3,2},{4,5},{5,4},{6,7},{7,6},{8,9},{9,8},{10,11... | collective-permute-start | bytes 36872 | tf_op jit(solution)/shard_map/ppermute | solution.py:371

commit v5 on v4

--- a/solution.py
+++ b/solution.py
@@ -28,28 +28,50 @@
     return slot // 3, (slot % 3) * 36 + 2 * k
 
 
-def pack_columns(tile_at, slots, columns):
+def own_slot(slot, k):
+    return slot // 5, (slot % 5) * 24 + 2 * (4 * (k // 6) + k % 6 - 1)
+
+
+OWN = [k for k in range(18) if 0 < k % 6 < 5]
+
+
+def pack_columns(tile_at, slots, columns, where, ks):
     pair = lanes_of((8, 128)) // 2
     packed = [jnp.zeros((8, 128), F32) for _ in range(columns.shape[0] // 8)]
     for slot in slots:
-        for k in range(18):
-            t, at = lane_slot(slot, k)
+        for k in ks:
+            t, at = where(slot, k)
             packed[t] = jnp.where(pair == at // 2, pltpu.roll(tile_at(slot, k), (at + 1) % 128, 1), packed[t])
     for t, value in enumerate(packed):
         columns[pl.ds(8 * t, 8), :] = value
 
 
+def merge_edges(even, near, far):
+    lane = lanes_of((8, 128))
+    left, right = jnp.where(even, far, near), jnp.where(even, near, far)
+    return jnp.where((lane & 1) == 0, pltpu.roll(right, 127, 1), pltpu.roll(left, 1, 1))
+
+
 def edge_tiles(even, slots, far_ref, near_ref):
-    lane = lanes_of((8, 128))
     edges = {}
     for t in sorted({lane_slot(slot, 0)[0] for slot in slots}):
-        near, far = near_ref[pl.ds(8 * t, 8), :], far_ref[pl.ds(8 * t, 8), :]
-        left, right = jnp.where(even, far, near), jnp.where(even, near, far)
-        edges[t] = jnp.where((lane & 1) == 0, pltpu.roll(right, 127, 1), pltpu.roll(left, 1, 1))
+        rows = pl.ds(8 * t, 8)
+        edges[t] = merge_edges(even, near_ref[rows, :], far_ref[rows, :])
 
     def edge(slot, k):
         t, at = lane_slot(slot, k)
         return pltpu.roll(edges[t], 127 - at, 1)
+
+    return edge
+
+
+def merged_edge(own, above, below):
+    def edge(slot, k):
+        x = k % 6 - 1
+        source, base, at_k = (above, 240, k + 4) if x < 0 else (below, 240, k - 4) if x > 3 else (own, 0, k)
+        t, at = own_slot(slot, at_k)
+        step = (127 - at) % 128
+        return pltpu.roll(source[pl.ds(base + 8 * t, 8), :], step, 1)
 
     return edge
 
@@ -66,23 +88,37 @@
             shift_ref[pl.ds(36 * height + base, 8), :] = jnp.where(lane == 127, outside, pltpu.roll(values, 127, 1))
 
 
-def rows_kernel(disp, vec, low, high, sems):
-    copies = []
-    for out, x in ((low, 0), (high, 3)):
-        for source, at in ((disp, pl.ds(0, 48)), (vec, pl.ds(48, 192))):
-            copies.append(pltpu.make_async_copy(source.at[:, x, :], out.at[at, :], sems.at[len(copies)]))
+def first_kernel(disp_in, vec_in, disp, vec, columns, low, high, sems):
+    copies = [pltpu.make_async_copy(disp_in, disp, sems.at[0]), pltpu.make_async_copy(vec_in, vec, sems.at[1])]
     for copy in copies:
         copy.start()
     for copy in copies:
         copy.wait()
+    disp_tile, vec_tile = natural_tile(disp, None, None, 0), natural_tile(vec, None, None, 0)
+    pack_columns(
+        lambda slot, k: disp_tile(slot, k) if slot < 2 else vec_tile(slot - 2, k), range(10), columns, own_slot, OWN
+    )
+    for out, x in ((low, 0), (high, 3)):
+        out[pl.ds(0, 48), :] = disp[pl.ds(x, 48, stride=4), :]
+        out[pl.ds(48, 192), :] = vec[pl.ds(x, 192, stride=4), :]
+
+
+def edges_kernel(par, near, far, low, high, own, low_out, high_out):
+    for t in range(2):
+        rows = pl.ds(8 * t, 8)
+        merged = merge_edges(par[0] == 0, near[rows, :], far[rows, :])
+        own[rows, :] = merged
+        low_out[pl.ds(240 + 8 * t, 8), :] = merged
+        high_out[pl.ds(240 + 8 * t, 8), :] = merged
+    low_out[pl.ds(0, 240), :] = low[...]
+    high_out[pl.ds(0, 240), :] = high[...]
 
 
 def load_kernel(
-    disp_in, vec_in, load_in, nbr_in, species, block_of, precond_in,
-    disp, vec, load, nbr, group, precond, masks, members, kind, block, sems,
+    load_in, nbr_in, species, block_of, precond_in,
+    load, nbr, group, precond, masks, members, kind, block, sems,
 ):
-    pairs = [(disp_in, disp), (vec_in, vec), (species, kind), (block_of, block), (load_in, load), (nbr_in, nbr)]
-    pairs.append((precond_in, precond))
+    pairs = [(species, kind), (block_of, block), (load_in, load), (nbr_in, nbr), (precond_in, precond)]
     copies = [pltpu.make_async_copy(source, out, sems.at[i]) for i, (source, out) in enumerate(pairs)]
     for copy in copies:
         copy.start()
@@ -118,14 +154,8 @@
     return tile
 
 
-def columns_kernel(disp, vec, above, below, columns):
-    disp_tile = natural_tile(disp, above, below, 0)
-    vec_tile = natural_tile(vec, above, below, 48)
-    pack_columns(lambda slot, k: disp_tile(slot, k) if slot < 2 else vec_tile(slot - 2, k), range(10), columns)
-
-
 def term_columns_kernel(low, mid, high, above, below, columns):
-    pack_columns(term_tile(low, mid, high, above, below), range(8), columns)
+    pack_columns(term_tile(low, mid, high, above, below), range(8), columns, lane_slot, range(18))
 
 
 def fold_rows(tiles, sub):
@@ -157,8 +187,8 @@
 CHUNK = 62
 
 
-def gram_kernel(copies, par, disp, forces, nbr, group, above, below, near, far, out, shift, feats, sums):
-    edge = edge_tiles(par[0] == 0, range(2), far, near)
+def gram_kernel(copies, own, disp, forces, nbr, group, above, below, out, shift, feats, sums):
+    edge = merged_edge(own, above, below)
     spread_columns(edge, natural_tile(disp, above, below, 0), range(2), shift, 16)
     for x in range(4):
         for o, (dx, dy) in enumerate(OFFSETS):
@@ -179,7 +209,7 @@
     members = members.astype(jnp.bfloat16)
     members = jnp.concatenate([members, members], axis=1)
     sub, eighth = subs_of((8, 128)), lanes_of((8, 128)) // 16
-    own = (sub == eighth).astype(F32)
+    diagonal = (sub == eighth).astype(F32)
     for c in range(len(PAIRS) // CHUNK):
         at = pl.ds(c * CHUNK * 8, CHUNK * 8)
         value = sums[at, :]
@@ -188,7 +218,7 @@
         by_group = lax.dot_general(
             jnp.concatenate([high, low], axis=1), members, (((1,), (1,)), ((), ())), preferred_element_type=F32
         )
-        sums[at, :] = (by_group.reshape(CHUNK, 8, 128) * own[None]).reshape(CHUNK * 8, 128)
+        sums[at, :] = (by_group.reshape(CHUNK, 8, 128) * diagonal[None]).reshape(CHUNK * 8, 128)
 
     def column(fixed, block):
         pairs = [(min(fixed, 8 * block + r), max(fixed, 8 * block + r)) for r in range(8)]
@@ -218,7 +248,7 @@
 
 
 def fit_kernel(
-    copies, scale, par, sums, precond, vec, masks, members, above, below, near, far,
+    copies, scale, own, sums, precond, vec, masks, members, above, below,
     theta, weights, low_out, high_out, shift,
 ):
     sub, eighth = subs_of((8, 128)), lanes_of((8, 128)) // 16
@@ -279,7 +309,7 @@
         weights[pl.ds(72 * x, 72), :] = by_atom[:, 128 * x : 128 * x + 128] * jnp.concatenate([mask] * 3, axis=0)
 
     tile = natural_tile(vec, above, below, 48)
-    edge = edge_tiles(par[0] == 0, range(2, 10), far, near)
+    edge = merged_edge(own, above, below)
     spread_columns(edge, lambda slot, k: tile(slot - 2, k), range(2, 10), shift, 64)
 
     def emit(a, x, value):
@@ -382,31 +412,27 @@
     def in_hbm(*values):
         return [pltpu.with_memory_space_constraint(value, pltpu.HBM) for value in values]
 
-    low, high = call(rows_kernel, "rows", [IN_HBM] * 2, (240, 240), (pltpu.SemaphoreType.DMA((4,)),))(
-        *in_hbm(displacements.reshape(-1, 4, 128), vectors.reshape(-1, 4, 128))
-    )
-    above, below = along(high, "gx", 1), along(low, "gx", -1)
-    tile = jax.ShapeDtypeStruct((4, 128), jnp.int32)
-    disp, vec, load, nbr, group, inverses, masks, members = call(
+    disp, vec, columns, low, high = call(
+        first_kernel, "first", [IN_HBM] * 2, (192, 768, 16, 240, 240), (pltpu.SemaphoreType.DMA((2,)),)
+    )(*in_hbm(displacements.reshape(-1, 128), vectors.reshape(-1, 128)))
+    near, far = from_both(columns)
+    small = pltpu.VMEM((4, 128), jnp.int32)
+    load, nbr, group, inverses, masks, members = call(
         load_kernel,
         "load",
-        [IN_HBM] * 7,
+        [IN_HBM] * 5,
         (
             192,
-            768,
-            192,
             jax.ShapeDtypeStruct((32, 128), jnp.int32),
-            tile,
+            jax.ShapeDtypeStruct((4, 128), jnp.int32),
             jax.ShapeDtypeStruct((NG * NP, NP), F32),
             4 * NP,
             jax.ShapeDtypeStruct((128, 512), jnp.bfloat16),
         ),
-        (pltpu.VMEM((4, 128), jnp.int32), pltpu.VMEM((4, 128), jnp.int32), pltpu.SemaphoreType.DMA((7,))),
+        (small, small, pltpu.SemaphoreType.DMA((5,))),
         flops=1 << 24,
     )(
         *in_hbm(
-            displacements.reshape(-1, 128),
-            vectors.reshape(-1, 128),
             forces.reshape(-1, 128),
             neighbours.reshape(-1, 128),
             species,
@@ -414,22 +440,22 @@
             precond.reshape(NG * NP, NP),
         )
     )
-    (columns,) = call(columns_kernel, "columns", [IN_VMEM] * 4, (32,))(disp, vec, above, below)
-    near, far = from_both(columns)
+    own, low, high = call(edges_kernel, "edges", [IN_SMEM] + [IN_VMEM] * 4, (16, 256, 256))(par, near, far, low, high)
+    above, below = along(high, "gx", 1), along(low, "gx", -1)
     (part,) = call(
         functools.partial(gram_kernel, snap),
         "gram",
-        [IN_SMEM] + [IN_VMEM] * 8,
+        [IN_VMEM] * 7,
         (snap * PAYLOAD,),
         (54 * 16, 27 * 64, len(PAIRS) * 8),
-    )(par, disp, load, nbr, group, above, below, near, far)
+    )(own, disp, load, nbr, group, above, below)
     part = lax.all_to_all(part, "snap", 0, 0, tiled=True)
     theta, weights, low, high, shift = call(
         functools.partial(fit_kernel, snap, scale),
         "fit",
-        [IN_SMEM] + [IN_VMEM] * 9,
+        [IN_VMEM] * 8,
         (NP, 288, 192, 192, 54 * 64),
-    )(par, part, inverses, vec, masks, members, above, below, near, far)
+    )(own, part, inverses, vec, masks, members, above, below)
     above, below = along(high, "gx", 1), along(low, "gx", -1)
     mid, constants = call(
         middle_kernel,

time: 59.8 us -> 59 us (0.987)
  starting transfers between devices: 28.9 us -> 28 us
    ppermute x2, starting transfers between devices: 16.1 us -> 15.2 us  [from_both(): far = lax.ppermute(columns, 'gy', pairs + [(j, i) for i, j in pairs])]
    ppermute x2, waiting for transfers between devices: 4.04 us -> 3.2 us  [from_both(): near = lax.ppermute(columns, 'gy', [(i, i ^ 1) for i in range(n)])]
    ppermute x2, waiting for transfers between devices: 2.41 us -> 3.16 us  [from_both(): far = lax.ppermute(columns, 'gy', pairs + [(j, i) for i, j in pairs])]
where the time goes in v5:
time: 59 us; the launch traced here: 58.7 us
  starting transfers between devices  28 us (47%)
  waiting for transfers between devices  11.9 us (20%)
  Pallas kernels  9.16 us (16%)
  blocking collectives  8.89 us (15%)
  between operations  0.72 us (1%)
    ppermute x2, starting transfers between devices, from_both(): far = lax.ppermute(columns, 'gy', pairs + [(j, i) for i, j in pairs])  15.2 us
    ppermute x4, starting transfers between devices, along(): return lax.ppermute(value, axis, [(i, (i + step) % n) for i in range(n)])  8.97 us
    all_to_all x1, blocking collectives, shards(): part = lax.all_to_all(part, 'snap', 0, 0, tiled=True)  8.89 us
    ppermute x4, waiting for transfers between devices, along(): return lax.ppermute(value, axis, [(i, (i + step) % n) for i in range(n)])  5.55 us
    ppermute x2, starting transfers between devices, from_both(): near = lax.ppermute(columns, 'gy', [(i, i ^ 1) for i in range(n)])  3.84 us
    ppermute x2, waiting for transfers between devices, from_both(): near = lax.ppermute(columns, 'gy', [(i, i ^ 1) for i in range(n)])  3.2 us
    ppermute x2, waiting for transfers between devices, from_both(): far = lax.ppermute(columns, 'gy', pairs + [(j, i) for i, j in pairs])  3.16 us
    pallas_call x1, Pallas kernels, shards(): call(functools.partial(gram_kernel, snap), 'gram', [IN_VMEM] * 7, (snap *...  1.61 us
  transfers between devices with their start and end apart: 8, of which 7 were waited for; matrix products, arithmetic and copies ran while one was open for 0% of the time, Pallas kernels for 6%

profile of v5, /device:TPU:8, one launch (start us, length us, event | category | flops | bytes accessed | tf_op | source)
XLA Modules:
  0.0 58.7 jit_solution(17596286698294383596)
XLA Ops:
  0.6 1.3 %first.1 = (f32[192,128]{1,0:T(8,128)S(1)}, f32[768,128]{1,0:T(8,128)S(1)}, f32[16,128]{1,0:T(8,128)S(1)}, f32[240,128]{1,0:T(8,128)S(1)}, f32[240,128]{1,0:T(8,128)S(1)}) custom-call(f32[192,128]{1,0:T(8,128)} %bitcast.18, f32[768,128]{1,0:T(8,128)} %bitcast.15), custom_call_target="tpu_custom_call" | custom-call | bytes 1048576 | tf_op jit(solution)/shard_map/first/pallas_call | solution.py:415
  1.9 9.0 %collective-permute-start.1 = (f32[16,128]{1,0:T(8,128)S(1)}, f32[16,128]{1,0:T(8,128)S(1)}, u32[]{:S(2)}, u32[]{:S(2)}) collective-permute-start(f32[16,128]{1,0:T(8,128)S(1)} %get-tuple-element.23), channel_id=1, source_target_pairs={{1,2},{3,4},{5,6},{7,0},{2,1},{4,3},{6,5},{0,7},{9,10},{11,12},{13... | collective-permute-start | bytes 24584 | tf_op jit(solution)/shard_map/ppermute | solution.py:403
  11.0 1.9 %collective-permute-start = (f32[16,128]{1,0:T(8,128)S(1)}, f32[16,128]{1,0:T(8,128)S(1)}, u32[]{:S(2)}, u32[]{:S(2)}) collective-permute-start(f32[16,128]{1,0:T(8,128)S(1)} %get-tuple-element.23), channel_id=1, source_target_pairs={{0,1},{1,0},{2,3},{3,2},{4,5},{5,4},{6,7},{7,6},{8,9},{9,8},{10,11... | collective-permute-start | bytes 24584 | tf_op jit(solution)/shard_map/ppermute | solution.py:401
  12.9 0.6 collective-permute-done.1.far
  13.5 3.0 %collective-permute-done.near = f32[16,128]{1,0:T(8,128)S(1)} collective-permute-done((f32[16,128]{1,0:T(8,128)S(1)}, f32[16,128]{1,0:T(8,128)S(1)}, u32[]{:S(2)}, u32[]{:S(2)}) %collective-permute-start) | collective-permute-done | bytes 8224 | tf_op jit(solution)/shard_map/ppermute | solution.py:401
  16.5 0.1 edges.1
  16.6 0.0 collective-permute-start.2
  16.6 7.1 %collective-permute-start.3 = (f32[256,128]{1,0:T(8,128)S(1)}, f32[256,128]{1,0:T(8,128)S(1)}, u32[]{:S(2)}, u32[]{:S(2)}) collective-permute-start(f32[256,128]{1,0:T(8,128)S(1)} %get-tuple-element.32), channel_id=1, source_target_pairs={{0,120},{8,0},{16,8},{24,16},{32,24},{40,32},{48,40},{56,48},{64,5... | collective-permute-start | bytes 393224 | tf_op jit(solution)/shard_map/ppermute | solution.py:396
  23.6 1.2 %load.1 = (f32[192,128]{1,0:T(8,128)S(1)}, s32[32,128]{1,0:T(8,128)S(1)}, s32[4,128]{1,0:T(4,128)S(1)}, f32[288,24]{1,0:T(8,128)S(1)}, f32[96,128]{1,0:T(8,128)S(1)}, /*index=5*/bf16[128,512]{1,0:T(8,128)(2,1)S(1)}) custom-call(f32[192,128]{1,0:T(8,128)} %bitcast.17, s32[32,128]{1,0:T(8,128)} %bitcast.19, s32[4,128]{1,0:T(4,128)} %species.1, ...), custom_call_target="tpu_custom_call" | custom-call | flops 16777216 | bytes 1048576 | tf_op jit(solution)/shard_map/load/pallas_call | solution.py:420
  24.8 1.4 %collective-permute-done.2.above = f32[256,128]{1,0:T(8,128)S(1)} collective-permute-done((f32[256,128]{1,0:T(8,128)S(1)}, f32[256,128]{1,0:T(8,128)S(1)}, u32[]{:S(2)}, u32[]{:S(2)}) %collective-permute-start.2) | collective-permute-done | bytes 131104 | tf_op jit(solution)/shard_map/ppermute | solution.py:396
  26.3 0.0 collective-permute-done.3.below
  26.3 1.6 %gram.1 = f32[256,128]{1,0:T(8,128)S(1)} custom-call(f32[16,128]{1,0:T(8,128)S(1)} %get-tuple-element.26.own, f32[192,128]{1,0:T(8,128)S(1)} %get-tuple-element.27.disp, f32[192,128]{1,0:T(8,128)S(1)} %get-tuple-element.28.forces, s32[32,128]{1,0:T(8,128)S(1)} %get-tuple-element.29.nbr, s32[4,128]{1,0:T(4,128)S(1)} %get-tuple-element.30.group, ...), custom_call_target="tpu_custom_call" | custom-call | bytes 1048576 | tf_op jit(solution)/shard_map/gram/pallas_call | solution.py:445
  27.9 8.9 %all_to_all.11 = f32[4,64,128]{2,1,0:T(8,128)S(1)} all-to-all(f32[4,64,128]{2,1,0:T(8,128)S(1)} %bitcast.13), channel_id=1, replica_groups=mesh['snap'=4,'gx'=16,'gy'=8] {'snap'}, dimensions={0} | all-to-all | bytes 262144 | tf_op jit(solution)/shard_map/all_to_all | solution.py:452
  36.8 1.6 %fit.1 = (f32[24,128]{1,0:T(8,128)S(1)}, f32[288,128]{1,0:T(8,128)S(1)}, f32[192,128]{1,0:T(8,128)S(1)}, f32[192,128]{1,0:T(8,128)S(1)}, f32[3456,128]{1,0:T(8,128)S(1)}) custom-call(f32[16,128]{1,0:T(8,128)S(1)} %get-tuple-element.26.own, f32[256,128]{1,0:T(8,128)S(1)} %bitcast.12, f32[288,24]{1,0:T(8,128)S(1)} %get-tuple-element.33.precond, ...), custom_call_target="tpu_custom_call" | custom-call | bytes 1048576 | tf_op jit(solution)/shard_map/fit/pallas_call | solution.py:453
  38.4 1.9 %collective-permute-start.5 = (f32[192,128]{1,0:T(8,128)S(1)}, f32[192,128]{1,0:T(8,128)S(1)}, u32[]{:S(2)}, u32[]{:S(2)}) collective-permute-start(f32[192,128]{1,0:T(8,128)S(1)} %get-tuple-element.41.low), channel_id=1, source_target_pairs={{0,120},{8,0},{16,8},{24,16},{32,24},{40,32},{48,40},{56,48},{64,5... | collective-permute-start | bytes 294920 | tf_op jit(solution)/shard_map/ppermute | solution.py:396
  40.3 0.0 collective-permute-start.4
  40.3 1.1 %middle.1 = (f32[384,128]{1,0:T(8,128)S(1)}, f32[9,4,24]{2,1,0:T(4,128)}) custom-call(f32[3456,128]{1,0:T(8,128)S(1)} %get-tuple-element.37.shift, f32[288,128]{1,0:T(8,128)S(1)} %get-tuple-element.38.weights, f32[24,128]{1,0:T(8,128)S(1)} %get-tuple-element.39.theta), custom_call_target="tpu_custom_call" | custom-call | flops 16777216 | bytes 1048576 | tf_op jit(solution)/shard_map/middle/pallas_call | solution.py:460
  41.4 1.1 %collective-permute-done.5.below = f32[192,128]{1,0:T(8,128)S(1)} collective-permute-done((f32[192,128]{1,0:T(8,128)S(1)}, f32[192,128]{1,0:T(8,128)S(1)}, u32[]{:S(2)}, u32[]{:S(2)}) %collective-permute-start.5) | collective-permute-done | bytes 98336 | tf_op jit(solution)/shard_map/ppermute | solution.py:396
  42.5 3.0 %collective-permute-done.4.above = f32[192,128]{1,0:T(8,128)S(1)} collective-permute-done((f32[192,128]{1,0:T(8,128)S(1)}, f32[192,128]{1,0:T(8,128)S(1)}, u32[]{:S(2)}, u32[]{:S(2)}) %collective-permute-start.4) | collective-permute-done | bytes 98336 | tf_op jit(solution)/shard_map/ppermute | solution.py:396
  45.5 0.2 term_columns.1
  45.7 6.2 %collective-permute-start.7 = (f32[24,128]{1,0:T(8,128)S(1)}, f32[24,128]{1,0:T(8,128)S(1)}, u32[]{:S(2)}, u32[]{:S(2)}) collective-permute-start(f32[24,128]{1,0:T(8,128)S(1)} %term_columns.1), channel_id=1, source_target_pairs={{1,2},{3,4},{5,6},{7,0},{2,1},{4,3},{6,5},{0,7},{9,10},{11,12},{13... | collective-permute-start | bytes 36872 | tf_op jit(solution)/shard_map/ppermute | solution.py:403
  51.9 1.9 %collective-permute-start.6 = (f32[24,128]{1,0:T(8,128)S(1)}, f32[24,128]{1,0:T(8,128)S(1)}, u32[]{:S(2)}, u32[]{:S(2)}) collective-permute-start(f32[24,128]{1,0:T(8,128)S(1)} %term_columns.1), channel_id=1, source_target_pairs={{0,1},{1,0},{2,3},{3,2},{4,5},{5,4},{6,7},{7,6},{8,9},{9,8},{10,11... | collective-permute-start | bytes 36872 | tf_op jit(solution)/shard_map/ppermute | solution.py:401
  53.9 0.9 %inner.1 = f32[768,128]{1,0:T(8,128)S(1)} custom-call(f32[192,128]{1,0:T(8,128)S(1)} %get-tuple-element.41.low, f32[384,128]{1,0:T(8,128)S(1)} %get-tuple-element.42.mid, f32[192,128]{1,0:T(8,128)S(1)} %get-tuple-element.43.high, f32[192,128]{1,0:T(8,128)S(1)} %collective-permute-done.4.above, f32[192,128]{1,0:T(8,128)S(1)} %collective-permute-done.5.below, ...), custom_call_target="tpu_custom_call" | custom-call | flops 33554432 | bytes 1048576 | tf_op jit(solution)/shard_map/inner/pallas_call | solution.py:469
  54.8 2.6 %collective-permute-done.7.far = f32[24,128]{1,0:T(8,128)S(1)} collective-permute-done((f32[24,128]{1,0:T(8,128)S(1)}, f32[24,128]{1,0:T(8,128)S(1)}, u32[]{:S(2)}, u32[]{:S(2)}) %collective-permute-start.7) | collective-permute-done | bytes 12320 | tf_op jit(solution)/shard_map/ppermute | solution.py:403
  57.3 0.2 collective-permute-done.6.near
  57.5 1.2 %outer.1 = f32[768,128]{1,0:T(8,128)} custom-call(s32[1]{0:T(128)} %bitcast.par, f32[768,128]{1,0:T(8,128)S(1)} %inner.1, f32[24,128]{1,0:T(8,128)S(1)} %collective-permute-done.6.near, f32[24,128]{1,0:T(8,128)S(1)} %collective-permute-done.7.far, f32[288,128]{1,0:T(8,128)S(1)} %get-tuple-element.38.weights), custom_call_target="tpu_custom_call" | custom-call | bytes 1048576 | tf_op jit(solution)/shard_map/outer/pallas_call | solution.py:472
Async XLA Ops:
  1.9 11.6 %collective-permute-start.1 = (f32[16,128]{1,0:T(8,128)S(1)}, f32[16,128]{1,0:T(8,128)S(1)}, u32[]{:S(2)}, u32[]{:S(2)}) collective-permute-start(f32[16,128]{1,0:T(8,128)S(1)} %get-tuple-element.23), channel_id=1, source_target_pairs={{1,2},{3,4},{5,6},{7,0},{2,1},{4,3},{6,5},{0,7},{9,10},{11,12},{13... | collective-permute-start | bytes 24584 | tf_op jit(solution)/shard_map/ppermute | solution.py:403
  11.0 5.5 %collective-permute-start = (f32[16,128]{1,0:T(8,128)S(1)}, f32[16,128]{1,0:T(8,128)S(1)}, u32[]{:S(2)}, u32[]{:S(2)}) collective-permute-start(f32[16,128]{1,0:T(8,128)S(1)} %get-tuple-element.23), channel_id=1, source_target_pairs={{0,1},{1,0},{2,3},{3,2},{4,5},{5,4},{6,7},{7,6},{8,9},{9,8},{10,11... | collective-permute-start | bytes 24584 | tf_op jit(solution)/shard_map/ppermute | solution.py:401
  16.6 9.7 %collective-permute-start.2 = (f32[256,128]{1,0:T(8,128)S(1)}, f32[256,128]{1,0:T(8,128)S(1)}, u32[]{:S(2)}, u32[]{:S(2)}) collective-permute-start(f32[256,128]{1,0:T(8,128)S(1)} %get-tuple-element.31), channel_id=1, source_target_pairs={{0,8},{8,16},{16,24},{24,32},{32,40},{40,48},{48,56},{56,64},{64,7... | collective-permute-start | bytes 393224 | tf_op jit(solution)/shard_map/ppermute | solution.py:396
  16.6 9.7 %collective-permute-start.3 = (f32[256,128]{1,0:T(8,128)S(1)}, f32[256,128]{1,0:T(8,128)S(1)}, u32[]{:S(2)}, u32[]{:S(2)}) collective-permute-start(f32[256,128]{1,0:T(8,128)S(1)} %get-tuple-element.32), channel_id=1, source_target_pairs={{0,120},{8,0},{16,8},{24,16},{32,24},{40,32},{48,40},{56,48},{64,5... | collective-permute-start | bytes 393224 | tf_op jit(solution)/shard_map/ppermute | solution.py:396
  38.4 4.1 %collective-permute-start.5 = (f32[192,128]{1,0:T(8,128)S(1)}, f32[192,128]{1,0:T(8,128)S(1)}, u32[]{:S(2)}, u32[]{:S(2)}) collective-permute-start(f32[192,128]{1,0:T(8,128)S(1)} %get-tuple-element.41.low), channel_id=1, source_target_pairs={{0,120},{8,0},{16,8},{24,16},{32,24},{40,32},{48,40},{56,48},{64,5... | collective-permute-start | bytes 294920 | tf_op jit(solution)/shard_map/ppermute | solution.py:396
  40.3 5.3 %collective-permute-start.4 = (f32[192,128]{1,0:T(8,128)S(1)}, f32[192,128]{1,0:T(8,128)S(1)}, u32[]{:S(2)}, u32[]{:S(2)}) collective-permute-start(f32[192,128]{1,0:T(8,128)S(1)} %get-tuple-element.43.high), channel_id=1, source_target_pairs={{0,8},{8,16},{16,24},{24,32},{32,40},{40,48},{48,56},{56,64},{64,7... | collective-permute-start | bytes 294920 | tf_op jit(solution)/shard_map/ppermute | solution.py:396
  45.7 11.6 %collective-permute-start.7 = (f32[24,128]{1,0:T(8,128)S(1)}, f32[24,128]{1,0:T(8,128)S(1)}, u32[]{:S(2)}, u32[]{:S(2)}) collective-permute-start(f32[24,128]{1,0:T(8,128)S(1)} %term_columns.1), channel_id=1, source_target_pairs={{1,2},{3,4},{5,6},{7,0},{2,1},{4,3},{6,5},{0,7},{9,10},{11,12},{13... | collective-permute-start | bytes 36872 | tf_op jit(solution)/shard_map/ppermute | solution.py:403
  51.9 5.6 %collective-permute-start.6 = (f32[24,128]{1,0:T(8,128)S(1)}, f32[24,128]{1,0:T(8,128)S(1)}, u32[]{:S(2)}, u32[]{:S(2)}) collective-permute-start(f32[24,128]{1,0:T(8,128)S(1)} %term_columns.1), channel_id=1, source_target_pairs={{0,1},{1,0},{2,3},{3,2},{4,5},{5,4},{6,7},{7,6},{8,9},{9,8},{10,11... | collective-permute-start | bytes 36872 | tf_op jit(solution)/shard_map/ppermute | solution.py:401

commit v6 on v5

--- a/solution.py
+++ b/solution.py
@@ -89,15 +89,20 @@
 
 
 def first_kernel(disp_in, vec_in, disp, vec, columns, low, high, sems):
-    copies = [pltpu.make_async_copy(disp_in, disp, sems.at[0]), pltpu.make_async_copy(vec_in, vec, sems.at[1])]
+    copies = [pltpu.make_async_copy(disp_in, disp, sems.at[0])]
+    for part in range(4):
+        rows = pl.ds(192 * part, 192)
+        copies.append(pltpu.make_async_copy(vec_in.at[rows, :], vec.at[rows, :], sems.at[1 + part]))
     for copy in copies:
         copy.start()
-    for copy in copies:
-        copy.wait()
     disp_tile, vec_tile = natural_tile(disp, None, None, 0), natural_tile(vec, None, None, 0)
-    pack_columns(
-        lambda slot, k: disp_tile(slot, k) if slot < 2 else vec_tile(slot - 2, k), range(10), columns, own_slot, OWN
-    )
+
+    def tile(slot, k):
+        if k == OWN[0] and slot % 2 == 0:
+            copies[slot // 2].wait()
+        return disp_tile(slot, k) if slot < 2 else vec_tile(slot - 2, k)
+
+    pack_columns(tile, range(10), columns, own_slot, OWN)
     for out, x in ((low, 0), (high, 3)):
         out[pl.ds(0, 48), :] = disp[pl.ds(x, 48, stride=4), :]
         out[pl.ds(48, 192), :] = vec[pl.ds(x, 192, stride=4), :]
@@ -334,7 +339,18 @@
         constants[i] = picked[4 * i : 4 * i + 4]
 
 
-def inner_kernel(low, mid, high, above, below, weights, vec, out, shift):
+def inner_kernel(low, mid, high, above, below, weights, vec, out, outside, shift):
+    lane = lanes_of((1, 128))
+    for x in range(4):
+        for a in range(3):
+            for b in range(3):
+                for dx in (-1, 0, 1):
+                    base = 72 * x + 24 * a + b
+                    left = weights[pl.ds(base + 3 * OFFSETS.index((dx, -1)), 1), :]
+                    right = weights[pl.ds(base + 3 * OFFSETS.index((dx, 1)), 1), :]
+                    outside[pl.ds(27 * x + 9 * a + 3 * b + dx + 1, 1), :] = jnp.where(
+                        lane == 0, 2.0 * left, jnp.where(lane == 127, 2.0 * right, 0.0)
+                    )
     empty = jnp.zeros((8, 128), F32)
     spread_columns(lambda slot, k: empty, term_tile(low, mid, high, above, below), range(8), shift, 64)
 
@@ -346,7 +362,6 @@
 
 def outer_kernel(par, inner, near, far, weights, out, edges, result, sems):
     edge = edge_tiles(par[0] == 0, range(8), far, near)
-    lane = lanes_of((1, 128))
     copies = []
     for half in range(2):
         for k in range(18):
@@ -358,10 +373,7 @@
                 for dx in (-1, 0, 1):
                     outside = edges[pl.ds(64 * (6 * b + x + dx + 1) + 32 * half, 32), :]
                     for a in range(3):
-                        base = 72 * x + 24 * a + b
-                        left = weights[pl.ds(base + 3 * OFFSETS.index((dx, -1)), 1), :]
-                        right = weights[pl.ds(base + 3 * OFFSETS.index((dx, 1)), 1), :]
-                        weight = jnp.where(lane == 0, 2.0 * left, jnp.where(lane == 127, 2.0 * right, 0.0))
+                        weight = weights[pl.ds(27 * x + 9 * a + 3 * b + dx + 1, 1), :]
                         total[a] = total[a] - outside * weight
             for a in range(3):
                 result[pl.ds(384 * half + 4 * a + x, 32, stride=12), :] = total[a]
@@ -413,7 +425,7 @@
         return [pltpu.with_memory_space_constraint(value, pltpu.HBM) for value in values]
 
     disp, vec, columns, low, high = call(
-        first_kernel, "first", [IN_HBM] * 2, (192, 768, 16, 240, 240), (pltpu.SemaphoreType.DMA((2,)),)
+        first_kernel, "first", [IN_HBM] * 2, (192, 768, 16, 240, 240), (pltpu.SemaphoreType.DMA((5,)),)
     )(*in_hbm(displacements.reshape(-1, 128), vectors.reshape(-1, 128)))
     near, far = from_both(columns)
     small = pltpu.VMEM((4, 128), jnp.int32)
@@ -466,7 +478,7 @@
     )(shift, weights, theta)
     (columns,) = call(term_columns_kernel, "term_columns", [IN_VMEM] * 5, (24,))(low, mid, high, above, below)
     near, far = from_both(columns)
-    (inner,) = call(inner_kernel, "inner", [IN_VMEM] * 7, (768,), (54 * 64,), flops=1 << 25)(
+    inner, outside = call(inner_kernel, "inner", [IN_VMEM] * 7, (768, 108), (54 * 64,), flops=1 << 25)(
         low, mid, high, above, below, weights, vec
     )
     (result,) = call(
@@ -477,7 +489,7 @@
         (18 * 64, 768, pltpu.SemaphoreType.DMA((2,))),
         out_spec=IN_HBM,
     )(
-        par, inner, near, far, weights
+        par, inner, near, far, outside
     )
 
     constants = constants.reshape(NSPEC, 3, precond.shape[0], NP).transpose(2, 0, 3, 1)

time: 59 us -> 59.1 us (level)
  no operation moved by 1% of the time
where the time goes in v6:
time: 59.1 us; the launch traced here: 58.8 us
  starting transfers between devices  28 us (47%)
  waiting for transfers between devices  11.8 us (20%)
  Pallas kernels  9.38 us (16%)
  blocking collectives  8.89 us (15%)
  between operations  0.72 us (1%)
    ppermute x2, starting transfers between devices, from_both(): far = lax.ppermute(columns, 'gy', pairs + [(j, i) for i, j in pairs])  15.2 us
    ppermute x4, starting transfers between devices, along(): return lax.ppermute(value, axis, [(i, (i + step) % n) for i in range(n)])  8.97 us
    all_to_all x1, blocking collectives, shards(): part = lax.all_to_all(part, 'snap', 0, 0, tiled=True)  8.89 us
    ppermute x4, waiting for transfers between devices, along(): return lax.ppermute(value, axis, [(i, (i + step) % n) for i in range(n)])  5.55 us
    ppermute x2, starting transfers between devices, from_both(): near = lax.ppermute(columns, 'gy', [(i, i ^ 1) for i in range(n)])  3.84 us
    ppermute x2, waiting for transfers between devices, from_both(): near = lax.ppermute(columns, 'gy', [(i, i ^ 1) for i in range(n)])  3.2 us
    ppermute x2, waiting for transfers between devices, from_both(): far = lax.ppermute(columns, 'gy', pairs + [(j, i) for i, j in pairs])  3.03 us
    pallas_call x1, Pallas kernels, shards(): call(functools.partial(gram_kernel, snap), 'gram', [IN_VMEM] * 7, (snap *...  1.61 us
  transfers between devices with their start and end apart: 8, of which 7 were waited for; matrix products, arithmetic and copies ran while one was open for 0% of the time, Pallas kernels for 6%

profile of v6, /device:TPU:8, one launch (start us, length us, event | category | flops | bytes accessed | tf_op | source)
XLA Modules:
  0.0 58.8 jit_solution(13189667714387568355)
XLA Ops:
  0.6 1.4 %first.1 = (f32[192,128]{1,0:T(8,128)S(1)}, f32[768,128]{1,0:T(8,128)S(1)}, f32[16,128]{1,0:T(8,128)S(1)}, f32[240,128]{1,0:T(8,128)S(1)}, f32[240,128]{1,0:T(8,128)S(1)}) custom-call(f32[192,128]{1,0:T(8,128)} %bitcast.18, f32[768,128]{1,0:T(8,128)} %bitcast.15), custom_call_target="tpu_custom_call" | custom-call | bytes 1048576 | tf_op jit(solution)/shard_map/first/pallas_call | solution.py:427
  2.1 9.0 %collective-permute-start.1 = (f32[16,128]{1,0:T(8,128)S(1)}, f32[16,128]{1,0:T(8,128)S(1)}, u32[]{:S(2)}, u32[]{:S(2)}) collective-permute-start(f32[16,128]{1,0:T(8,128)S(1)} %get-tuple-element.25), channel_id=1, source_target_pairs={{1,2},{3,4},{5,6},{7,0},{2,1},{4,3},{6,5},{0,7},{9,10},{11,12},{13... | collective-permute-start | bytes 24584 | tf_op jit(solution)/shard_map/ppermute | solution.py:415
  11.1 1.9 %collective-permute-start = (f32[16,128]{1,0:T(8,128)S(1)}, f32[16,128]{1,0:T(8,128)S(1)}, u32[]{:S(2)}, u32[]{:S(2)}) collective-permute-start(f32[16,128]{1,0:T(8,128)S(1)} %get-tuple-element.25), channel_id=1, source_target_pairs={{0,1},{1,0},{2,3},{3,2},{4,5},{5,4},{6,7},{7,6},{8,9},{9,8},{10,11... | collective-permute-start | bytes 24584 | tf_op jit(solution)/shard_map/ppermute | solution.py:413
  13.0 0.6 collective-permute-done.1.far
  13.6 3.0 %collective-permute-done.near = f32[16,128]{1,0:T(8,128)S(1)} collective-permute-done((f32[16,128]{1,0:T(8,128)S(1)}, f32[16,128]{1,0:T(8,128)S(1)}, u32[]{:S(2)}, u32[]{:S(2)}) %collective-permute-start) | collective-permute-done | bytes 8224 | tf_op jit(solution)/shard_map/ppermute | solution.py:413
  16.6 0.1 edges.1
  16.7 0.0 collective-permute-start.2
  16.7 7.1 %collective-permute-start.3 = (f32[256,128]{1,0:T(8,128)S(1)}, f32[256,128]{1,0:T(8,128)S(1)}, u32[]{:S(2)}, u32[]{:S(2)}) collective-permute-start(f32[256,128]{1,0:T(8,128)S(1)} %get-tuple-element.34), channel_id=1, source_target_pairs={{0,120},{8,0},{16,8},{24,16},{32,24},{40,32},{48,40},{56,48},{64,5... | collective-permute-start | bytes 393224 | tf_op jit(solution)/shard_map/ppermute | solution.py:408
  23.8 1.2 %load.1 = (f32[192,128]{1,0:T(8,128)S(1)}, s32[32,128]{1,0:T(8,128)S(1)}, s32[4,128]{1,0:T(4,128)S(1)}, f32[288,24]{1,0:T(8,128)S(1)}, f32[96,128]{1,0:T(8,128)S(1)}, /*index=5*/bf16[128,512]{1,0:T(8,128)(2,1)S(1)}) custom-call(f32[192,128]{1,0:T(8,128)} %bitcast.17, s32[32,128]{1,0:T(8,128)} %bitcast.19, s32[4,128]{1,0:T(4,128)} %species.1, ...), custom_call_target="tpu_custom_call" | custom-call | flops 16777216 | bytes 1048576 | tf_op jit(solution)/shard_map/load/pallas_call | solution.py:432
  25.0 1.4 %collective-permute-done.2.above = f32[256,128]{1,0:T(8,128)S(1)} collective-permute-done((f32[256,128]{1,0:T(8,128)S(1)}, f32[256,128]{1,0:T(8,128)S(1)}, u32[]{:S(2)}, u32[]{:S(2)}) %collective-permute-start.2) | collective-permute-done | bytes 131104 | tf_op jit(solution)/shard_map/ppermute | solution.py:408
  26.4 0.0 collective-permute-done.3.below
  26.4 1.6 %gram.1 = f32[256,128]{1,0:T(8,128)S(1)} custom-call(f32[16,128]{1,0:T(8,128)S(1)} %get-tuple-element.28.own, f32[192,128]{1,0:T(8,128)S(1)} %get-tuple-element.29.disp, f32[192,128]{1,0:T(8,128)S(1)} %get-tuple-element.30.forces, s32[32,128]{1,0:T(8,128)S(1)} %get-tuple-element.31.nbr, s32[4,128]{1,0:T(4,128)S(1)} %get-tuple-element.32.group, ...), custom_call_target="tpu_custom_call" | custom-call | bytes 1048576 | tf_op jit(solution)/shard_map/gram/pallas_call | solution.py:457
  28.0 8.9 %all_to_all.11 = f32[4,64,128]{2,1,0:T(8,128)S(1)} all-to-all(f32[4,64,128]{2,1,0:T(8,128)S(1)} %bitcast.13), channel_id=1, replica_groups=mesh['snap'=4,'gx'=16,'gy'=8] {'snap'}, dimensions={0} | all-to-all | bytes 262144 | tf_op jit(solution)/shard_map/all_to_all | solution.py:464
  36.9 1.6 %fit.1 = (f32[24,128]{1,0:T(8,128)S(1)}, f32[288,128]{1,0:T(8,128)S(1)}, f32[192,128]{1,0:T(8,128)S(1)}, f32[192,128]{1,0:T(8,128)S(1)}, f32[3456,128]{1,0:T(8,128)S(1)}) custom-call(f32[16,128]{1,0:T(8,128)S(1)} %get-tuple-element.28.own, f32[256,128]{1,0:T(8,128)S(1)} %bitcast.12, f32[288,24]{1,0:T(8,128)S(1)} %get-tuple-element.35.precond, ...), custom_call_target="tpu_custom_call" | custom-call | bytes 1048576 | tf_op jit(solution)/shard_map/fit/pallas_call | solution.py:465
  38.5 1.9 %collective-permute-start.5 = (f32[192,128]{1,0:T(8,128)S(1)}, f32[192,128]{1,0:T(8,128)S(1)}, u32[]{:S(2)}, u32[]{:S(2)}) collective-permute-start(f32[192,128]{1,0:T(8,128)S(1)} %get-tuple-element.43.low), channel_id=1, source_target_pairs={{0,120},{8,0},{16,8},{24,16},{32,24},{40,32},{48,40},{56,48},{64,5... | collective-permute-start | bytes 294920 | tf_op jit(solution)/shard_map/ppermute | solution.py:408
  40.4 0.0 collective-permute-start.4
  40.5 1.1 %middle.1 = (f32[384,128]{1,0:T(8,128)S(1)}, f32[9,4,24]{2,1,0:T(4,128)}) custom-call(f32[3456,128]{1,0:T(8,128)S(1)} %get-tuple-element.39.shift, f32[288,128]{1,0:T(8,128)S(1)} %get-tuple-element.40.weights, f32[24,128]{1,0:T(8,128)S(1)} %get-tuple-element.41.theta), custom_call_target="tpu_custom_call" | custom-call | flops 16777216 | bytes 1048576 | tf_op jit(solution)/shard_map/middle/pallas_call | solution.py:472
  41.6 1.1 %collective-permute-done.5.below = f32[192,128]{1,0:T(8,128)S(1)} collective-permute-done((f32[192,128]{1,0:T(8,128)S(1)}, f32[192,128]{1,0:T(8,128)S(1)}, u32[]{:S(2)}, u32[]{:S(2)}) %collective-permute-start.5) | collective-permute-done | bytes 98336 | tf_op jit(solution)/shard_map/ppermute | solution.py:408
  42.7 3.0 %collective-permute-done.4.above = f32[192,128]{1,0:T(8,128)S(1)} collective-permute-done((f32[192,128]{1,0:T(8,128)S(1)}, f32[192,128]{1,0:T(8,128)S(1)}, u32[]{:S(2)}, u32[]{:S(2)}) %collective-permute-start.4) | collective-permute-done | bytes 98336 | tf_op jit(solution)/shard_map/ppermute | solution.py:408
  45.7 0.2 term_columns.1
  45.9 6.2 %collective-permute-start.7 = (f32[24,128]{1,0:T(8,128)S(1)}, f32[24,128]{1,0:T(8,128)S(1)}, u32[]{:S(2)}, u32[]{:S(2)}) collective-permute-start(f32[24,128]{1,0:T(8,128)S(1)} %term_columns.1), channel_id=1, source_target_pairs={{1,2},{3,4},{5,6},{7,0},{2,1},{4,3},{6,5},{0,7},{9,10},{11,12},{13... | collective-permute-start | bytes 36872 | tf_op jit(solution)/shard_map/ppermute | solution.py:415
  52.1 1.9 %collective-permute-start.6 = (f32[24,128]{1,0:T(8,128)S(1)}, f32[24,128]{1,0:T(8,128)S(1)}, u32[]{:S(2)}, u32[]{:S(2)}) collective-permute-start(f32[24,128]{1,0:T(8,128)S(1)} %term_columns.1), channel_id=1, source_target_pairs={{0,1},{1,0},{2,3},{3,2},{4,5},{5,4},{6,7},{7,6},{8,9},{9,8},{10,11... | collective-permute-start | bytes 36872 | tf_op jit(solution)/shard_map/ppermute | solution.py:413
  54.1 1.0 %inner.1 = (f32[768,128]{1,0:T(8,128)S(1)}, f32[108,128]{1,0:T(8,128)S(1)}) custom-call(f32[192,128]{1,0:T(8,128)S(1)} %get-tuple-element.43.low, f32[384,128]{1,0:T(8,128)S(1)} %get-tuple-element.44.mid, f32[192,128]{1,0:T(8,128)S(1)} %get-tuple-element.45.high, f32[192,128]{1,0:T(8,128)S(1)} %collective-permute-done.4.above, ...), custom_call_target="tpu_custom_call" | custom-call | flops 33554432 | bytes 1048576 | tf_op jit(solution)/shard_map/inner/pallas_call | solution.py:481
  55.1 2.4 %collective-permute-done.7.far = f32[24,128]{1,0:T(8,128)S(1)} collective-permute-done((f32[24,128]{1,0:T(8,128)S(1)}, f32[24,128]{1,0:T(8,128)S(1)}, u32[]{:S(2)}, u32[]{:S(2)}) %collective-permute-start.7) | collective-permute-done | bytes 12320 | tf_op jit(solution)/shard_map/ppermute | solution.py:415
  57.5 0.2 collective-permute-done.6.near
  57.7 1.1 %outer.1 = f32[768,128]{1,0:T(8,128)} custom-call(s32[1]{0:T(128)} %bitcast.par, f32[768,128]{1,0:T(8,128)S(1)} %get-tuple-element.46.inner, f32[24,128]{1,0:T(8,128)S(1)} %collective-permute-done.6.near, f32[24,128]{1,0:T(8,128)S(1)} %collective-permute-done.7.far, f32[108,128]{1,0:T(8,128)S(1)} %get-tuple-element.47.weights), custom_call_target="tpu_custom_call" | custom-call | bytes 1048576 | tf_op jit(solution)/shard_map/outer/pallas_call | solution.py:484
Async XLA Ops:
  2.1 11.6 %collective-permute-start.1 = (f32[16,128]{1,0:T(8,128)S(1)}, f32[16,128]{1,0:T(8,128)S(1)}, u32[]{:S(2)}, u32[]{:S(2)}) collective-permute-start(f32[16,128]{1,0:T(8,128)S(1)} %get-tuple-element.25), channel_id=1, source_target_pairs={{1,2},{3,4},{5,6},{7,0},{2,1},{4,3},{6,5},{0,7},{9,10},{11,12},{13... | collective-permute-start | bytes 24584 | tf_op jit(solution)/shard_map/ppermute | solution.py:415
  11.1 5.5 %collective-permute-start = (f32[16,128]{1,0:T(8,128)S(1)}, f32[16,128]{1,0:T(8,128)S(1)}, u32[]{:S(2)}, u32[]{:S(2)}) collective-permute-start(f32[16,128]{1,0:T(8,128)S(1)} %get-tuple-element.25), channel_id=1, source_target_pairs={{0,1},{1,0},{2,3},{3,2},{4,5},{5,4},{6,7},{7,6},{8,9},{9,8},{10,11... | collective-permute-start | bytes 24584 | tf_op jit(solution)/shard_map/ppermute | solution.py:413
  16.7 9.7 %collective-permute-start.2 = (f32[256,128]{1,0:T(8,128)S(1)}, f32[256,128]{1,0:T(8,128)S(1)}, u32[]{:S(2)}, u32[]{:S(2)}) collective-permute-start(f32[256,128]{1,0:T(8,128)S(1)} %get-tuple-element.33), channel_id=1, source_target_pairs={{0,8},{8,16},{16,24},{24,32},{32,40},{40,48},{48,56},{56,64},{64,7... | collective-permute-start | bytes 393224 | tf_op jit(solution)/shard_map/ppermute | solution.py:408
  16.7 9.7 %collective-permute-start.3 = (f32[256,128]{1,0:T(8,128)S(1)}, f32[256,128]{1,0:T(8,128)S(1)}, u32[]{:S(2)}, u32[]{:S(2)}) collective-permute-start(f32[256,128]{1,0:T(8,128)S(1)} %get-tuple-element.34), channel_id=1, source_target_pairs={{0,120},{8,0},{16,8},{24,16},{32,24},{40,32},{48,40},{56,48},{64,5... | collective-permute-start | bytes 393224 | tf_op jit(solution)/shard_map/ppermute | solution.py:408
  38.5 4.1 %collective-permute-start.5 = (f32[192,128]{1,0:T(8,128)S(1)}, f32[192,128]{1,0:T(8,128)S(1)}, u32[]{:S(2)}, u32[]{:S(2)}) collective-permute-start(f32[192,128]{1,0:T(8,128)S(1)} %get-tuple-element.43.low), channel_id=1, source_target_pairs={{0,120},{8,0},{16,8},{24,16},{32,24},{40,32},{48,40},{56,48},{64,5... | collective-permute-start | bytes 294920 | tf_op jit(solution)/shard_map/ppermute | solution.py:408
  40.4 5.3 %collective-permute-start.4 = (f32[192,128]{1,0:T(8,128)S(1)}, f32[192,128]{1,0:T(8,128)S(1)}, u32[]{:S(2)}, u32[]{:S(2)}) collective-permute-start(f32[192,128]{1,0:T(8,128)S(1)} %get-tuple-element.45.high), channel_id=1, source_target_pairs={{0,8},{8,16},{16,24},{24,32},{32,40},{40,48},{48,56},{56,64},{64,7... | collective-permute-start | bytes 294920 | tf_op jit(solution)/shard_map/ppermute | solution.py:408
  45.9 11.6 %collective-permute-start.7 = (f32[24,128]{1,0:T(8,128)S(1)}, f32[24,128]{1,0:T(8,128)S(1)}, u32[]{:S(2)}, u32[]{:S(2)}) collective-permute-start(f32[24,128]{1,0:T(8,128)S(1)} %term_columns.1), channel_id=1, source_target_pairs={{1,2},{3,4},{5,6},{7,0},{2,1},{4,3},{6,5},{0,7},{9,10},{11,12},{13... | collective-permute-start | bytes 36872 | tf_op jit(solution)/shard_map/ppermute | solution.py:415
  52.1 5.6 %collective-permute-start.6 = (f32[24,128]{1,0:T(8,128)S(1)}, f32[24,128]{1,0:T(8,128)S(1)}, u32[]{:S(2)}, u32[]{:S(2)}) collective-permute-start(f32[24,128]{1,0:T(8,128)S(1)} %term_columns.1), channel_id=1, source_target_pairs={{0,1},{1,0},{2,3},{3,2},{4,5},{5,4},{6,7},{7,6},{8,9},{9,8},{10,11... | collective-permute-start | bytes 36872 | tf_op jit(solution)/shard_map/ppermute | solution.py:413

commit v7 on v6

--- a/solution.py
+++ b/solution.py
@@ -187,8 +187,8 @@
 
 PAIRS = [(q, p) for q in range(NP) for p in range(q, NP + 3)]
 PAIR_AT = {pair: i for i, pair in enumerate(PAIRS)}
-BLOCKS = [(i, j) for i in range(3) for j in range(i, 3)]
-PAYLOAD = 64
+BLOCKS = [(i, j) for i in range(3) for j in range(i + 1, 3)]
+PAYLOAD = 48
 CHUNK = 62
 
 
@@ -229,9 +229,15 @@
         pairs = [(min(fixed, 8 * block + r), max(fixed, 8 * block + r)) for r in range(8)]
         return fold_rows([sums[pl.ds(PAIR_AT[pair] * 8, 8), :] for pair in pairs], sub)
 
-    packed = [fold_lanes([column(8 * i + r, j) for r in range(8)], eighth) for i, j in BLOCKS]
-    sides = [column(NP + a, block) for a in range(3) for block in range(3)] + [jnp.zeros((8, 128), F32)] * 7
-    packed += [fold_lanes(sides[:8], eighth), fold_lanes(sides[8:], eighth)]
+    def lower(block, q):
+        pairs = [(q, r) if r >= q else (8 - q, 8 - q + r) for r in range(8)]
+        at = [PAIR_AT[8 * block + i, 8 * block + j] for i, j in pairs]
+        return fold_rows([sums[pl.ds(8 * i, 8), :] for i in at], sub)
+
+    tiles = [column(8 * i + r, j) for i, j in BLOCKS for r in range(8)]
+    tiles += [lower(block, q) for block in range(3) for q in range(5)]
+    tiles += [column(NP + a, block) for a in range(3) for block in range(3)]
+    packed = [fold_lanes(tiles[8 * m : 8 * m + 8], eighth) for m in range(6)]
     for i, value in enumerate(packed):
         for copy in range(copies):
             out[pl.ds(copy * PAYLOAD + 8 * i, 8), :] = value
@@ -270,7 +276,12 @@
             value = value + pltpu.roll(value, step, 1)
         return value
 
-    sides = [spread(total(6 + i // 8), i % 8) for i in range(9)]
+    totals = [total(m) for m in range(6)]
+
+    def tile_of(i):
+        return spread(totals[i // 8], i % 8)
+
+    sides = [tile_of(39 + i) for i in range(9)]
     rhs = []
     for block in range(3):
         value = jnp.where(eighth == 0, sides[block], 0.0)
@@ -290,12 +301,16 @@
     part = [first[8 * i : 8 * i + 8] for i in range(3)]
     remain = list(rhs)
     for m, (i, j) in enumerate(BLOCKS):
-        value = total(m)
-        tiles = [spread(value, r) for r in range(8)]
+        tiles = [tile_of(8 * m + r) for r in range(8)]
         for r in range(8):
             remain[j] = remain[j] - tiles[r] * part[i][r : r + 1, :]
-        if i != j:
-            remain[i] = remain[i] - fold_rows([tiles[r] * part[j] for r in range(8)], sub)
+        remain[i] = remain[i] - fold_rows([tiles[r] * part[j] for r in range(8)], sub)
+    for i in range(3):
+        mixed = [tile_of(24 + 5 * i + q) for q in range(5)]
+        lower = mixed + [pltpu.roll(mixed[8 - q], q, 0) for q in (5, 6, 7)]
+        for q in range(8):
+            remain[i] = remain[i] - jnp.where(sub >= q, lower[q], 0.0) * part[i][q : q + 1, :]
+        remain[i] = remain[i] - fold_rows([jnp.where(sub > q, lower[q], 0.0) * part[i] for q in range(8)], sub)
     fitted = first + solve(jnp.concatenate(remain, axis=0))
     theta[...] = fitted
 

time: 59.1 us -> 58.8 us (level)
  no operation moved by 1% of the time
where the time goes in v7:
time: 58.8 us; the launch traced here: 58.5 us
  starting transfers between devices  28 us (48%)
  waiting for transfers between devices  11.8 us (20%)
  Pallas kernels  9.38 us (16%)
  blocking collectives  8.61 us (15%)
  between operations  0.72 us (1%)
    ppermute x2, starting transfers between devices, from_both(): far = lax.ppermute(columns, 'gy', pairs + [(j, i) for i, j in pairs])  15.2 us
    ppermute x4, starting transfers between devices, along(): return lax.ppermute(value, axis, [(i, (i + step) % n) for i in range(n)])  8.98 us
    all_to_all x1, blocking collectives, shards(): part = lax.all_to_all(part, 'snap', 0, 0, tiled=True)  8.61 us
    ppermute x4, waiting for transfers between devices, along(): return lax.ppermute(value, axis, [(i, (i + step) % n) for i in range(n)])  5.55 us
    ppermute x2, starting transfers between devices, from_both(): near = lax.ppermute(columns, 'gy', [(i, i ^ 1) for i in range(n)])  3.84 us
    ppermute x2, waiting for transfers between devices, from_both(): near = lax.ppermute(columns, 'gy', [(i, i ^ 1) for i in range(n)])  3.2 us
    ppermute x2, waiting for transfers between devices, from_both(): far = lax.ppermute(columns, 'gy', pairs + [(j, i) for i, j in pairs])  3.03 us
    pallas_call x1, Pallas kernels, shards(): call(functools.partial(fit_kernel, snap, scale), 'fit', [IN_VMEM] * 8, (N...  1.62 us
  transfers between devices with their start and end apart: 8, of which 7 were waited for; matrix products, arithmetic and copies ran while one was open for 0% of the time, Pallas kernels for 6%

profile of v7, /device:TPU:8, one launch (start us, length us, event | category | flops | bytes accessed | tf_op | source)
XLA Modules:
  0.0 58.5 jit_solution(11498761965683764796)
XLA Ops:
  0.6 1.4 %first.1 = (f32[192,128]{1,0:T(8,128)S(1)}, f32[768,128]{1,0:T(8,128)S(1)}, f32[16,128]{1,0:T(8,128)S(1)}, f32[240,128]{1,0:T(8,128)S(1)}, f32[240,128]{1,0:T(8,128)S(1)}) custom-call(f32[192,128]{1,0:T(8,128)} %bitcast.18, f32[768,128]{1,0:T(8,128)} %bitcast.15), custom_call_target="tpu_custom_call" | custom-call | bytes 1048576 | tf_op jit(solution)/shard_map/first/pallas_call | solution.py:442
  2.1 9.0 %collective-permute-start.1 = (f32[16,128]{1,0:T(8,128)S(1)}, f32[16,128]{1,0:T(8,128)S(1)}, u32[]{:S(2)}, u32[]{:S(2)}) collective-permute-start(f32[16,128]{1,0:T(8,128)S(1)} %get-tuple-element.25), channel_id=1, source_target_pairs={{1,2},{3,4},{5,6},{7,0},{2,1},{4,3},{6,5},{0,7},{9,10},{11,12},{13... | collective-permute-start | bytes 24584 | tf_op jit(solution)/shard_map/ppermute | solution.py:430
  11.1 1.9 %collective-permute-start = (f32[16,128]{1,0:T(8,128)S(1)}, f32[16,128]{1,0:T(8,128)S(1)}, u32[]{:S(2)}, u32[]{:S(2)}) collective-permute-start(f32[16,128]{1,0:T(8,128)S(1)} %get-tuple-element.25), channel_id=1, source_target_pairs={{0,1},{1,0},{2,3},{3,2},{4,5},{5,4},{6,7},{7,6},{8,9},{9,8},{10,11... | collective-permute-start | bytes 24584 | tf_op jit(solution)/shard_map/ppermute | solution.py:428
  13.0 0.6 %collective-permute-done.1.far = f32[16,128]{1,0:T(8,128)S(1)} collective-permute-done((f32[16,128]{1,0:T(8,128)S(1)}, f32[16,128]{1,0:T(8,128)S(1)}, u32[]{:S(2)}, u32[]{:S(2)}) %collective-permute-start.1) | collective-permute-done | bytes 8224 | tf_op jit(solution)/shard_map/ppermute | solution.py:430
  13.6 3.0 %collective-permute-done.near = f32[16,128]{1,0:T(8,128)S(1)} collective-permute-done((f32[16,128]{1,0:T(8,128)S(1)}, f32[16,128]{1,0:T(8,128)S(1)}, u32[]{:S(2)}, u32[]{:S(2)}) %collective-permute-start) | collective-permute-done | bytes 8224 | tf_op jit(solution)/shard_map/ppermute | solution.py:428
  16.6 0.1 edges.1
  16.7 0.0 collective-permute-start.2
  16.7 7.1 %collective-permute-start.3 = (f32[256,128]{1,0:T(8,128)S(1)}, f32[256,128]{1,0:T(8,128)S(1)}, u32[]{:S(2)}, u32[]{:S(2)}) collective-permute-start(f32[256,128]{1,0:T(8,128)S(1)} %get-tuple-element.34), channel_id=1, source_target_pairs={{0,120},{8,0},{16,8},{24,16},{32,24},{40,32},{48,40},{56,48},{64,5... | collective-permute-start | bytes 393224 | tf_op jit(solution)/shard_map/ppermute | solution.py:423
  23.8 1.2 %load.1 = (f32[192,128]{1,0:T(8,128)S(1)}, s32[32,128]{1,0:T(8,128)S(1)}, s32[4,128]{1,0:T(4,128)S(1)}, f32[288,24]{1,0:T(8,128)S(1)}, f32[96,128]{1,0:T(8,128)S(1)}, /*index=5*/bf16[128,512]{1,0:T(8,128)(2,1)S(1)}) custom-call(f32[192,128]{1,0:T(8,128)} %bitcast.17, s32[32,128]{1,0:T(8,128)} %bitcast.19, s32[4,128]{1,0:T(4,128)} %species.1, ...), custom_call_target="tpu_custom_call" | custom-call | flops 16777216 | bytes 1048576 | tf_op jit(solution)/shard_map/load/pallas_call | solution.py:447
  25.0 1.4 %collective-permute-done.2.above = f32[256,128]{1,0:T(8,128)S(1)} collective-permute-done((f32[256,128]{1,0:T(8,128)S(1)}, f32[256,128]{1,0:T(8,128)S(1)}, u32[]{:S(2)}, u32[]{:S(2)}) %collective-permute-start.2) | collective-permute-done | bytes 131104 | tf_op jit(solution)/shard_map/ppermute | solution.py:423
  26.4 0.0 collective-permute-done.3.below
  26.4 1.6 %gram.1 = f32[192,128]{1,0:T(8,128)S(1)} custom-call(f32[16,128]{1,0:T(8,128)S(1)} %get-tuple-element.28.own, f32[192,128]{1,0:T(8,128)S(1)} %get-tuple-element.29.disp, f32[192,128]{1,0:T(8,128)S(1)} %get-tuple-element.30.forces, s32[32,128]{1,0:T(8,128)S(1)} %get-tuple-element.31.nbr, s32[4,128]{1,0:T(4,128)S(1)} %get-tuple-element.32.group, ...), custom_call_target="tpu_custom_call" | custom-call | bytes 1048576 | tf_op jit(solution)/shard_map/gram/pallas_call | solution.py:472
  28.0 8.6 %all_to_all.11 = f32[4,48,128]{2,1,0:T(8,128)S(1)} all-to-all(f32[4,48,128]{2,1,0:T(8,128)S(1)} %bitcast.13), channel_id=1, replica_groups=mesh['snap'=4,'gx'=16,'gy'=8] {'snap'}, dimensions={0} | all-to-all | bytes 196608 | tf_op jit(solution)/shard_map/all_to_all | solution.py:479
  36.6 1.6 %fit.1 = (f32[24,128]{1,0:T(8,128)S(1)}, f32[288,128]{1,0:T(8,128)S(1)}, f32[192,128]{1,0:T(8,128)S(1)}, f32[192,128]{1,0:T(8,128)S(1)}, f32[3456,128]{1,0:T(8,128)S(1)}) custom-call(f32[16,128]{1,0:T(8,128)S(1)} %get-tuple-element.28.own, f32[192,128]{1,0:T(8,128)S(1)} %bitcast.12, f32[288,24]{1,0:T(8,128)S(1)} %get-tuple-element.35.precond, ...), custom_call_target="tpu_custom_call" | custom-call | bytes 1048576 | tf_op jit(solution)/shard_map/fit/pallas_call | solution.py:480
  38.2 1.9 %collective-permute-start.5 = (f32[192,128]{1,0:T(8,128)S(1)}, f32[192,128]{1,0:T(8,128)S(1)}, u32[]{:S(2)}, u32[]{:S(2)}) collective-permute-start(f32[192,128]{1,0:T(8,128)S(1)} %get-tuple-element.43.low), channel_id=1, source_target_pairs={{0,120},{8,0},{16,8},{24,16},{32,24},{40,32},{48,40},{56,48},{64,5... | collective-permute-start | bytes 294920 | tf_op jit(solution)/shard_map/ppermute | solution.py:423
  40.2 0.0 collective-permute-start.4
  40.2 1.1 %middle.1 = (f32[384,128]{1,0:T(8,128)S(1)}, f32[9,4,24]{2,1,0:T(4,128)}) custom-call(f32[3456,128]{1,0:T(8,128)S(1)} %get-tuple-element.39.shift, f32[288,128]{1,0:T(8,128)S(1)} %get-tuple-element.40.weights, f32[24,128]{1,0:T(8,128)S(1)} %get-tuple-element.41.theta), custom_call_target="tpu_custom_call" | custom-call | flops 16777216 | bytes 1048576 | tf_op jit(solution)/shard_map/middle/pallas_call | solution.py:487
  41.3 1.1 %collective-permute-done.5.below = f32[192,128]{1,0:T(8,128)S(1)} collective-permute-done((f32[192,128]{1,0:T(8,128)S(1)}, f32[192,128]{1,0:T(8,128)S(1)}, u32[]{:S(2)}, u32[]{:S(2)}) %collective-permute-start.5) | collective-permute-done | bytes 98336 | tf_op jit(solution)/shard_map/ppermute | solution.py:423
  42.4 3.0 %collective-permute-done.4.above = f32[192,128]{1,0:T(8,128)S(1)} collective-permute-done((f32[192,128]{1,0:T(8,128)S(1)}, f32[192,128]{1,0:T(8,128)S(1)}, u32[]{:S(2)}, u32[]{:S(2)}) %collective-permute-start.4) | collective-permute-done | bytes 98336 | tf_op jit(solution)/shard_map/ppermute | solution.py:423
  45.4 0.2 term_columns.1
  45.6 6.2 %collective-permute-start.7 = (f32[24,128]{1,0:T(8,128)S(1)}, f32[24,128]{1,0:T(8,128)S(1)}, u32[]{:S(2)}, u32[]{:S(2)}) collective-permute-start(f32[24,128]{1,0:T(8,128)S(1)} %term_columns.1), channel_id=1, source_target_pairs={{1,2},{3,4},{5,6},{7,0},{2,1},{4,3},{6,5},{0,7},{9,10},{11,12},{13... | collective-permute-start | bytes 36872 | tf_op jit(solution)/shard_map/ppermute | solution.py:430
  51.8 1.9 %collective-permute-start.6 = (f32[24,128]{1,0:T(8,128)S(1)}, f32[24,128]{1,0:T(8,128)S(1)}, u32[]{:S(2)}, u32[]{:S(2)}) collective-permute-start(f32[24,128]{1,0:T(8,128)S(1)} %term_columns.1), channel_id=1, source_target_pairs={{0,1},{1,0},{2,3},{3,2},{4,5},{5,4},{6,7},{7,6},{8,9},{9,8},{10,11... | collective-permute-start | bytes 36872 | tf_op jit(solution)/shard_map/ppermute | solution.py:428
  53.8 1.0 %inner.1 = (f32[768,128]{1,0:T(8,128)S(1)}, f32[108,128]{1,0:T(8,128)S(1)}) custom-call(f32[192,128]{1,0:T(8,128)S(1)} %get-tuple-element.43.low, f32[384,128]{1,0:T(8,128)S(1)} %get-tuple-element.44.mid, f32[192,128]{1,0:T(8,128)S(1)} %get-tuple-element.45.high, f32[192,128]{1,0:T(8,128)S(1)} %collective-permute-done.4.above, ...), custom_call_target="tpu_custom_call" | custom-call | flops 33554432 | bytes 1048576 | tf_op jit(solution)/shard_map/inner/pallas_call | solution.py:496
  54.8 2.4 %collective-permute-done.7.far = f32[24,128]{1,0:T(8,128)S(1)} collective-permute-done((f32[24,128]{1,0:T(8,128)S(1)}, f32[24,128]{1,0:T(8,128)S(1)}, u32[]{:S(2)}, u32[]{:S(2)}) %collective-permute-start.7) | collective-permute-done | bytes 12320 | tf_op jit(solution)/shard_map/ppermute | solution.py:430
  57.3 0.2 collective-permute-done.6.near
  57.4 1.1 %outer.1 = f32[768,128]{1,0:T(8,128)} custom-call(s32[1]{0:T(128)} %bitcast.par, f32[768,128]{1,0:T(8,128)S(1)} %get-tuple-element.46.inner, f32[24,128]{1,0:T(8,128)S(1)} %collective-permute-done.6.near, f32[24,128]{1,0:T(8,128)S(1)} %collective-permute-done.7.far, f32[108,128]{1,0:T(8,128)S(1)} %get-tuple-element.47.weights), custom_call_target="tpu_custom_call" | custom-call | bytes 1048576 | tf_op jit(solution)/shard_map/outer/pallas_call | solution.py:499
Async XLA Ops:
  2.1 11.6 %collective-permute-start.1 = (f32[16,128]{1,0:T(8,128)S(1)}, f32[16,128]{1,0:T(8,128)S(1)}, u32[]{:S(2)}, u32[]{:S(2)}) collective-permute-start(f32[16,128]{1,0:T(8,128)S(1)} %get-tuple-element.25), channel_id=1, source_target_pairs={{1,2},{3,4},{5,6},{7,0},{2,1},{4,3},{6,5},{0,7},{9,10},{11,12},{13... | collective-permute-start | bytes 24584 | tf_op jit(solution)/shard_map/ppermute | solution.py:430
  11.1 5.5 %collective-permute-start = (f32[16,128]{1,0:T(8,128)S(1)}, f32[16,128]{1,0:T(8,128)S(1)}, u32[]{:S(2)}, u32[]{:S(2)}) collective-permute-start(f32[16,128]{1,0:T(8,128)S(1)} %get-tuple-element.25), channel_id=1, source_target_pairs={{0,1},{1,0},{2,3},{3,2},{4,5},{5,4},{6,7},{7,6},{8,9},{9,8},{10,11... | collective-permute-start | bytes 24584 | tf_op jit(solution)/shard_map/ppermute | solution.py:428
  16.7 9.7 %collective-permute-start.2 = (f32[256,128]{1,0:T(8,128)S(1)}, f32[256,128]{1,0:T(8,128)S(1)}, u32[]{:S(2)}, u32[]{:S(2)}) collective-permute-start(f32[256,128]{1,0:T(8,128)S(1)} %get-tuple-element.33), channel_id=1, source_target_pairs={{0,8},{8,16},{16,24},{24,32},{32,40},{40,48},{48,56},{56,64},{64,7... | collective-permute-start | bytes 393224 | tf_op jit(solution)/shard_map/ppermute | solution.py:423
  16.7 9.7 %collective-permute-start.3 = (f32[256,128]{1,0:T(8,128)S(1)}, f32[256,128]{1,0:T(8,128)S(1)}, u32[]{:S(2)}, u32[]{:S(2)}) collective-permute-start(f32[256,128]{1,0:T(8,128)S(1)} %get-tuple-element.34), channel_id=1, source_target_pairs={{0,120},{8,0},{16,8},{24,16},{32,24},{40,32},{48,40},{56,48},{64,5... | collective-permute-start | bytes 393224 | tf_op jit(solution)/shard_map/ppermute | solution.py:423
  38.2 4.1 %collective-permute-start.5 = (f32[192,128]{1,0:T(8,128)S(1)}, f32[192,128]{1,0:T(8,128)S(1)}, u32[]{:S(2)}, u32[]{:S(2)}) collective-permute-start(f32[192,128]{1,0:T(8,128)S(1)} %get-tuple-element.43.low), channel_id=1, source_target_pairs={{0,120},{8,0},{16,8},{24,16},{32,24},{40,32},{48,40},{56,48},{64,5... | collective-permute-start | bytes 294920 | tf_op jit(solution)/shard_map/ppermute | solution.py:423
  40.2 5.3 %collective-permute-start.4 = (f32[192,128]{1,0:T(8,128)S(1)}, f32[192,128]{1,0:T(8,128)S(1)}, u32[]{:S(2)}, u32[]{:S(2)}) collective-permute-start(f32[192,128]{1,0:T(8,128)S(1)} %get-tuple-element.45.high), channel_id=1, source_target_pairs={{0,8},{8,16},{16,24},{24,32},{32,40},{40,48},{48,56},{56,64},{64,7... | collective-permute-start | bytes 294920 | tf_op jit(solution)/shard_map/ppermute | solution.py:423
  45.6 11.6 %collective-permute-start.7 = (f32[24,128]{1,0:T(8,128)S(1)}, f32[24,128]{1,0:T(8,128)S(1)}, u32[]{:S(2)}, u32[]{:S(2)}) collective-permute-start(f32[24,128]{1,0:T(8,128)S(1)} %term_columns.1), channel_id=1, source_target_pairs={{1,2},{3,4},{5,6},{7,0},{2,1},{4,3},{6,5},{0,7},{9,10},{11,12},{13... | collective-permute-start | bytes 36872 | tf_op jit(solution)/shard_map/ppermute | solution.py:430
  51.8 5.6 %collective-permute-start.6 = (f32[24,128]{1,0:T(8,128)S(1)}, f32[24,128]{1,0:T(8,128)S(1)}, u32[]{:S(2)}, u32[]{:S(2)}) collective-permute-start(f32[24,128]{1,0:T(8,128)S(1)} %term_columns.1), channel_id=1, source_target_pairs={{0,1},{1,0},{2,3},{3,2},{4,5},{5,4},{6,7},{7,6},{8,9},{9,8},{10,11... | collective-permute-start | bytes 36872 | tf_op jit(solution)/shard_map/ppermute | solution.py:428

commit v8 on v7

--- a/solution.py
+++ b/solution.py
@@ -89,17 +89,14 @@
 
 
 def first_kernel(disp_in, vec_in, disp, vec, columns, low, high, sems):
-    copies = [pltpu.make_async_copy(disp_in, disp, sems.at[0])]
-    for part in range(4):
-        rows = pl.ds(192 * part, 192)
-        copies.append(pltpu.make_async_copy(vec_in.at[rows, :], vec.at[rows, :], sems.at[1 + part]))
+    copies = [pltpu.make_async_copy(disp_in, disp, sems.at[0]), pltpu.make_async_copy(vec_in, vec, sems.at[1])]
     for copy in copies:
         copy.start()
+    for copy in copies:
+        copy.wait()
     disp_tile, vec_tile = natural_tile(disp, None, None, 0), natural_tile(vec, None, None, 0)
 
     def tile(slot, k):
-        if k == OWN[0] and slot % 2 == 0:
-            copies[slot // 2].wait()
         return disp_tile(slot, k) if slot < 2 else vec_tile(slot - 2, k)
 
     pack_columns(tile, range(10), columns, own_slot, OWN)
@@ -440,7 +437,7 @@
         return [pltpu.with_memory_space_constraint(value, pltpu.HBM) for value in values]
 
     disp, vec, columns, low, high = call(
-        first_kernel, "first", [IN_HBM] * 2, (192, 768, 16, 240, 240), (pltpu.SemaphoreType.DMA((5,)),)
+        first_kernel, "first", [IN_HBM] * 2, (192, 768, 16, 240, 240), (pltpu.SemaphoreType.DMA((2,)),)
     )(*in_hbm(displacements.reshape(-1, 128), vectors.reshape(-1, 128)))
     near, far = from_both(columns)
     small = pltpu.VMEM((4, 128), jnp.int32)

time: 58.8 us -> 58.7 us (level)
  no operation moved by 1% of the time
where the time goes in v8:
time: 58.7 us; the launch traced here: 58.4 us
  starting transfers between devices  28 us (48%)
  waiting for transfers between devices  11.8 us (20%)
  Pallas kernels  9.23 us (16%)
  blocking collectives  8.61 us (15%)
  between operations  0.72 us (1%)
    ppermute x2, starting transfers between devices, from_both(): far = lax.ppermute(columns, 'gy', pairs + [(j, i) for i, j in pairs])  15.2 us
    ppermute x4, starting transfers between devices, along(): return lax.ppermute(value, axis, [(i, (i + step) % n) for i in range(n)])  8.98 us
    all_to_all x1, blocking collectives, shards(): part = lax.all_to_all(part, 'snap', 0, 0, tiled=True)  8.61 us
    ppermute x4, waiting for transfers between devices, along(): return lax.ppermute(value, axis, [(i, (i + step) % n) for i in range(n)])  5.55 us
    ppermute x2, starting transfers between devices, from_both(): near = lax.ppermute(columns, 'gy', [(i, i ^ 1) for i in range(n)])  3.84 us
    ppermute x2, waiting for transfers between devices, from_both(): near = lax.ppermute(columns, 'gy', [(i, i ^ 1) for i in range(n)])  3.19 us
    ppermute x2, waiting for transfers between devices, from_both(): far = lax.ppermute(columns, 'gy', pairs + [(j, i) for i, j in pairs])  3.03 us
    pallas_call x1, Pallas kernels, shards(): call(functools.partial(fit_kernel, snap, scale), 'fit', [IN_VMEM] * 8, (N...  1.62 us
  transfers between devices with their start and end apart: 8, of which 7 were waited for; matrix products, arithmetic and copies ran while one was open for 0% of the time, Pallas kernels for 6%

profile of v8, /device:TPU:8, one launch (start us, length us, event | category | flops | bytes accessed | tf_op | source)
XLA Modules:
  0.0 58.4 jit_solution(11254797643325831667)
XLA Ops:
  0.6 1.3 %first.1 = (f32[192,128]{1,0:T(8,128)S(1)}, f32[768,128]{1,0:T(8,128)S(1)}, f32[16,128]{1,0:T(8,128)S(1)}, f32[240,128]{1,0:T(8,128)S(1)}, f32[240,128]{1,0:T(8,128)S(1)}) custom-call(f32[192,128]{1,0:T(8,128)} %bitcast.18, f32[768,128]{1,0:T(8,128)} %bitcast.15), custom_call_target="tpu_custom_call" | custom-call | bytes 1048576 | tf_op jit(solution)/shard_map/first/pallas_call | solution.py:439
  1.9 9.0 %collective-permute-start.1 = (f32[16,128]{1,0:T(8,128)S(1)}, f32[16,128]{1,0:T(8,128)S(1)}, u32[]{:S(2)}, u32[]{:S(2)}) collective-permute-start(f32[16,128]{1,0:T(8,128)S(1)} %get-tuple-element.25), channel_id=1, source_target_pairs={{1,2},{3,4},{5,6},{7,0},{2,1},{4,3},{6,5},{0,7},{9,10},{11,12},{13... | collective-permute-start | bytes 24584 | tf_op jit(solution)/shard_map/ppermute | solution.py:427
  11.0 1.9 %collective-permute-start = (f32[16,128]{1,0:T(8,128)S(1)}, f32[16,128]{1,0:T(8,128)S(1)}, u32[]{:S(2)}, u32[]{:S(2)}) collective-permute-start(f32[16,128]{1,0:T(8,128)S(1)} %get-tuple-element.25), channel_id=1, source_target_pairs={{0,1},{1,0},{2,3},{3,2},{4,5},{5,4},{6,7},{7,6},{8,9},{9,8},{10,11... | collective-permute-start | bytes 24584 | tf_op jit(solution)/shard_map/ppermute | solution.py:425
  12.9 0.6 %collective-permute-done.1.far = f32[16,128]{1,0:T(8,128)S(1)} collective-permute-done((f32[16,128]{1,0:T(8,128)S(1)}, f32[16,128]{1,0:T(8,128)S(1)}, u32[]{:S(2)}, u32[]{:S(2)}) %collective-permute-start.1) | collective-permute-done | bytes 8224 | tf_op jit(solution)/shard_map/ppermute | solution.py:427
  13.5 3.0 %collective-permute-done.near = f32[16,128]{1,0:T(8,128)S(1)} collective-permute-done((f32[16,128]{1,0:T(8,128)S(1)}, f32[16,128]{1,0:T(8,128)S(1)}, u32[]{:S(2)}, u32[]{:S(2)}) %collective-permute-start) | collective-permute-done | bytes 8224 | tf_op jit(solution)/shard_map/ppermute | solution.py:425
  16.5 0.1 edges.1
  16.6 0.0 collective-permute-start.2
  16.6 7.1 %collective-permute-start.3 = (f32[256,128]{1,0:T(8,128)S(1)}, f32[256,128]{1,0:T(8,128)S(1)}, u32[]{:S(2)}, u32[]{:S(2)}) collective-permute-start(f32[256,128]{1,0:T(8,128)S(1)} %get-tuple-element.34), channel_id=1, source_target_pairs={{0,120},{8,0},{16,8},{24,16},{32,24},{40,32},{48,40},{56,48},{64,5... | collective-permute-start | bytes 393224 | tf_op jit(solution)/shard_map/ppermute | solution.py:420
  23.6 1.2 %load.1 = (f32[192,128]{1,0:T(8,128)S(1)}, s32[32,128]{1,0:T(8,128)S(1)}, s32[4,128]{1,0:T(4,128)S(1)}, f32[288,24]{1,0:T(8,128)S(1)}, f32[96,128]{1,0:T(8,128)S(1)}, /*index=5*/bf16[128,512]{1,0:T(8,128)(2,1)S(1)}) custom-call(f32[192,128]{1,0:T(8,128)} %bitcast.17, s32[32,128]{1,0:T(8,128)} %bitcast.19, s32[4,128]{1,0:T(4,128)} %species.1, ...), custom_call_target="tpu_custom_call" | custom-call | flops 16777216 | bytes 1048576 | tf_op jit(solution)/shard_map/load/pallas_call | solution.py:444
  24.8 1.4 %collective-permute-done.2.above = f32[256,128]{1,0:T(8,128)S(1)} collective-permute-done((f32[256,128]{1,0:T(8,128)S(1)}, f32[256,128]{1,0:T(8,128)S(1)}, u32[]{:S(2)}, u32[]{:S(2)}) %collective-permute-start.2) | collective-permute-done | bytes 131104 | tf_op jit(solution)/shard_map/ppermute | solution.py:420
  26.3 0.0 collective-permute-done.3.below
  26.3 1.6 %gram.1 = f32[192,128]{1,0:T(8,128)S(1)} custom-call(f32[16,128]{1,0:T(8,128)S(1)} %get-tuple-element.28.own, f32[192,128]{1,0:T(8,128)S(1)} %get-tuple-element.29.disp, f32[192,128]{1,0:T(8,128)S(1)} %get-tuple-element.30.forces, s32[32,128]{1,0:T(8,128)S(1)} %get-tuple-element.31.nbr, s32[4,128]{1,0:T(4,128)S(1)} %get-tuple-element.32.group, ...), custom_call_target="tpu_custom_call" | custom-call | bytes 1048576 | tf_op jit(solution)/shard_map/gram/pallas_call | solution.py:469
  27.9 8.6 %all_to_all.11 = f32[4,48,128]{2,1,0:T(8,128)S(1)} all-to-all(f32[4,48,128]{2,1,0:T(8,128)S(1)} %bitcast.13), channel_id=1, replica_groups=mesh['snap'=4,'gx'=16,'gy'=8] {'snap'}, dimensions={0} | all-to-all | bytes 196608 | tf_op jit(solution)/shard_map/all_to_all | solution.py:476
  36.5 1.6 %fit.1 = (f32[24,128]{1,0:T(8,128)S(1)}, f32[288,128]{1,0:T(8,128)S(1)}, f32[192,128]{1,0:T(8,128)S(1)}, f32[192,128]{1,0:T(8,128)S(1)}, f32[3456,128]{1,0:T(8,128)S(1)}) custom-call(f32[16,128]{1,0:T(8,128)S(1)} %get-tuple-element.28.own, f32[192,128]{1,0:T(8,128)S(1)} %bitcast.12, f32[288,24]{1,0:T(8,128)S(1)} %get-tuple-element.35.precond, ...), custom_call_target="tpu_custom_call" | custom-call | bytes 1048576 | tf_op jit(solution)/shard_map/fit/pallas_call | solution.py:477
  38.1 1.9 %collective-permute-start.5 = (f32[192,128]{1,0:T(8,128)S(1)}, f32[192,128]{1,0:T(8,128)S(1)}, u32[]{:S(2)}, u32[]{:S(2)}) collective-permute-start(f32[192,128]{1,0:T(8,128)S(1)} %get-tuple-element.43.low), channel_id=1, source_target_pairs={{0,120},{8,0},{16,8},{24,16},{32,24},{40,32},{48,40},{56,48},{64,5... | collective-permute-start | bytes 294920 | tf_op jit(solution)/shard_map/ppermute | solution.py:420
  40.0 0.0 collective-permute-start.4
  40.0 1.1 %middle.1 = (f32[384,128]{1,0:T(8,128)S(1)}, f32[9,4,24]{2,1,0:T(4,128)}) custom-call(f32[3456,128]{1,0:T(8,128)S(1)} %get-tuple-element.39.shift, f32[288,128]{1,0:T(8,128)S(1)} %get-tuple-element.40.weights, f32[24,128]{1,0:T(8,128)S(1)} %get-tuple-element.41.theta), custom_call_target="tpu_custom_call" | custom-call | flops 16777216 | bytes 1048576 | tf_op jit(solution)/shard_map/middle/pallas_call | solution.py:484
  41.2 1.1 %collective-permute-done.5.below = f32[192,128]{1,0:T(8,128)S(1)} collective-permute-done((f32[192,128]{1,0:T(8,128)S(1)}, f32[192,128]{1,0:T(8,128)S(1)}, u32[]{:S(2)}, u32[]{:S(2)}) %collective-permute-start.5) | collective-permute-done | bytes 98336 | tf_op jit(solution)/shard_map/ppermute | solution.py:420
  42.2 3.0 %collective-permute-done.4.above = f32[192,128]{1,0:T(8,128)S(1)} collective-permute-done((f32[192,128]{1,0:T(8,128)S(1)}, f32[192,128]{1,0:T(8,128)S(1)}, u32[]{:S(2)}, u32[]{:S(2)}) %collective-permute-start.4) | collective-permute-done | bytes 98336 | tf_op jit(solution)/shard_map/ppermute | solution.py:420
  45.3 0.2 term_columns.1
  45.5 6.2 %collective-permute-start.7 = (f32[24,128]{1,0:T(8,128)S(1)}, f32[24,128]{1,0:T(8,128)S(1)}, u32[]{:S(2)}, u32[]{:S(2)}) collective-permute-start(f32[24,128]{1,0:T(8,128)S(1)} %term_columns.1), channel_id=1, source_target_pairs={{1,2},{3,4},{5,6},{7,0},{2,1},{4,3},{6,5},{0,7},{9,10},{11,12},{13... | collective-permute-start | bytes 36872 | tf_op jit(solution)/shard_map/ppermute | solution.py:427
  51.7 1.9 %collective-permute-start.6 = (f32[24,128]{1,0:T(8,128)S(1)}, f32[24,128]{1,0:T(8,128)S(1)}, u32[]{:S(2)}, u32[]{:S(2)}) collective-permute-start(f32[24,128]{1,0:T(8,128)S(1)} %term_columns.1), channel_id=1, source_target_pairs={{0,1},{1,0},{2,3},{3,2},{4,5},{5,4},{6,7},{7,6},{8,9},{9,8},{10,11... | collective-permute-start | bytes 36872 | tf_op jit(solution)/shard_map/ppermute | solution.py:425
  53.6 1.0 %inner.1 = (f32[768,128]{1,0:T(8,128)S(1)}, f32[108,128]{1,0:T(8,128)S(1)}) custom-call(f32[192,128]{1,0:T(8,128)S(1)} %get-tuple-element.43.low, f32[384,128]{1,0:T(8,128)S(1)} %get-tuple-element.44.mid, f32[192,128]{1,0:T(8,128)S(1)} %get-tuple-element.45.high, f32[192,128]{1,0:T(8,128)S(1)} %collective-permute-done.4.above, ...), custom_call_target="tpu_custom_call" | custom-call | flops 33554432 | bytes 1048576 | tf_op jit(solution)/shard_map/inner/pallas_call | solution.py:493
  54.7 2.4 %collective-permute-done.7.far = f32[24,128]{1,0:T(8,128)S(1)} collective-permute-done((f32[24,128]{1,0:T(8,128)S(1)}, f32[24,128]{1,0:T(8,128)S(1)}, u32[]{:S(2)}, u32[]{:S(2)}) %collective-permute-start.7) | collective-permute-done | bytes 12320 | tf_op jit(solution)/shard_map/ppermute | solution.py:427
  57.1 0.2 collective-permute-done.6.near
  57.3 1.1 %outer.1 = f32[768,128]{1,0:T(8,128)} custom-call(s32[1]{0:T(128)} %bitcast.par, f32[768,128]{1,0:T(8,128)S(1)} %get-tuple-element.46.inner, f32[24,128]{1,0:T(8,128)S(1)} %collective-permute-done.6.near, f32[24,128]{1,0:T(8,128)S(1)} %collective-permute-done.7.far, f32[108,128]{1,0:T(8,128)S(1)} %get-tuple-element.47.weights), custom_call_target="tpu_custom_call" | custom-call | bytes 1048576 | tf_op jit(solution)/shard_map/outer/pallas_call | solution.py:496
Async XLA Ops:
  1.9 11.6 %collective-permute-start.1 = (f32[16,128]{1,0:T(8,128)S(1)}, f32[16,128]{1,0:T(8,128)S(1)}, u32[]{:S(2)}, u32[]{:S(2)}) collective-permute-start(f32[16,128]{1,0:T(8,128)S(1)} %get-tuple-element.25), channel_id=1, source_target_pairs={{1,2},{3,4},{5,6},{7,0},{2,1},{4,3},{6,5},{0,7},{9,10},{11,12},{13... | collective-permute-start | bytes 24584 | tf_op jit(solution)/shard_map/ppermute | solution.py:427
  11.0 5.5 %collective-permute-start = (f32[16,128]{1,0:T(8,128)S(1)}, f32[16,128]{1,0:T(8,128)S(1)}, u32[]{:S(2)}, u32[]{:S(2)}) collective-permute-start(f32[16,128]{1,0:T(8,128)S(1)} %get-tuple-element.25), channel_id=1, source_target_pairs={{0,1},{1,0},{2,3},{3,2},{4,5},{5,4},{6,7},{7,6},{8,9},{9,8},{10,11... | collective-permute-start | bytes 24584 | tf_op jit(solution)/shard_map/ppermute | solution.py:425
  16.6 9.7 %collective-permute-start.2 = (f32[256,128]{1,0:T(8,128)S(1)}, f32[256,128]{1,0:T(8,128)S(1)}, u32[]{:S(2)}, u32[]{:S(2)}) collective-permute-start(f32[256,128]{1,0:T(8,128)S(1)} %get-tuple-element.33), channel_id=1, source_target_pairs={{0,8},{8,16},{16,24},{24,32},{32,40},{40,48},{48,56},{56,64},{64,7... | collective-permute-start | bytes 393224 | tf_op jit(solution)/shard_map/ppermute | solution.py:420
  16.6 9.7 %collective-permute-start.3 = (f32[256,128]{1,0:T(8,128)S(1)}, f32[256,128]{1,0:T(8,128)S(1)}, u32[]{:S(2)}, u32[]{:S(2)}) collective-permute-start(f32[256,128]{1,0:T(8,128)S(1)} %get-tuple-element.34), channel_id=1, source_target_pairs={{0,120},{8,0},{16,8},{24,16},{32,24},{40,32},{48,40},{56,48},{64,5... | collective-permute-start | bytes 393224 | tf_op jit(solution)/shard_map/ppermute | solution.py:420
  38.1 4.1 %collective-permute-start.5 = (f32[192,128]{1,0:T(8,128)S(1)}, f32[192,128]{1,0:T(8,128)S(1)}, u32[]{:S(2)}, u32[]{:S(2)}) collective-permute-start(f32[192,128]{1,0:T(8,128)S(1)} %get-tuple-element.43.low), channel_id=1, source_target_pairs={{0,120},{8,0},{16,8},{24,16},{32,24},{40,32},{48,40},{56,48},{64,5... | collective-permute-start | bytes 294920 | tf_op jit(solution)/shard_map/ppermute | solution.py:420
  40.0 5.3 %collective-permute-start.4 = (f32[192,128]{1,0:T(8,128)S(1)}, f32[192,128]{1,0:T(8,128)S(1)}, u32[]{:S(2)}, u32[]{:S(2)}) collective-permute-start(f32[192,128]{1,0:T(8,128)S(1)} %get-tuple-element.45.high), channel_id=1, source_target_pairs={{0,8},{8,16},{16,24},{24,32},{32,40},{40,48},{48,56},{56,64},{64,7... | collective-permute-start | bytes 294920 | tf_op jit(solution)/shard_map/ppermute | solution.py:420
  45.5 11.6 %collective-permute-start.7 = (f32[24,128]{1,0:T(8,128)S(1)}, f32[24,128]{1,0:T(8,128)S(1)}, u32[]{:S(2)}, u32[]{:S(2)}) collective-permute-start(f32[24,128]{1,0:T(8,128)S(1)} %term_columns.1), channel_id=1, source_target_pairs={{1,2},{3,4},{5,6},{7,0},{2,1},{4,3},{6,5},{0,7},{9,10},{11,12},{13... | collective-permute-start | bytes 36872 | tf_op jit(solution)/shard_map/ppermute | solution.py:427
  51.7 5.6 %collective-permute-start.6 = (f32[24,128]{1,0:T(8,128)S(1)}, f32[24,128]{1,0:T(8,128)S(1)}, u32[]{:S(2)}, u32[]{:S(2)}) collective-permute-start(f32[24,128]{1,0:T(8,128)S(1)} %term_columns.1), channel_id=1, source_target_pairs={{0,1},{1,0},{2,3},{3,2},{4,5},{5,4},{6,7},{7,6},{8,9},{9,8},{10,11... | collective-permute-start | bytes 36872 | tf_op jit(solution)/shard_map/ppermute | solution.py:425
